TPU v7x, 768 devices: a whole 4x8x12 slice. The times are simulated.
768 devices in a mesh: space: 96 (over x, z, core), group: 8 (over y).
Axes of the slice: x: 4, y: 8, z: 12, core: 2. Of those that a mesh axis runs over, the one named last changes fastest.
Arguments:
- point_feats: bfloat16 [1572864, 32], P(('space', 'group')), may hold values from -6 to 6
- point_voxel: int32 [1572864], P(('space', 'group')), may hold values from -1 to 4095, as said below
- cotangent: bfloat16 [1572864, 32], P(('space', 'group')), may hold values from -6 to 6
- kernel: bfloat16 [3, 3, 3, 32, 32], replicated, may hold values from -0.21875 to 0.21875
Outputs:
- point_grad: bfloat16 [1572864, 32], P(('space', 'group'))
Inputs may be any that keep to these rules, and one draw needn't show every extreme that they name: `point_voxel`: in each block of 256 slots that one device sends to one member of its group the live slots come first and hold voxel numbers below 4096, the rest -1; every device fills one of its blocks completely.
All inputs are finite; a program needn't handle non-finite values.
Results may differ from a plain program's by a relative error of at most 0.0049.
Values may be sent and summed in bfloat16 or wider, within the bound.
No kernel may reach another device: no remote copies, remote signals or barrier semaphores. Data moves between devices by JAX's collectives and lax.ppermute only.
A program may use at most 64 MiB of HBM per device.

v0:
```python
import jax
import jax.numpy as jnp
from jax import lax
from jax.sharding import PartitionSpec as P

XD = 16
YD = 16
ZB = 16


def extended(shard, sides, width):
    for axis, dim in sides:
        size, length = (lax.axis_size(axis), shard.shape[dim])
        up = [(i, (i + 1) % size) for i in range(size - 1)]
        down = [(j, i) for i, j in up]
        last = lax.slice_in_dim(shard, length - width, length, axis=dim)
        first = lax.slice_in_dim(shard, 0, width, axis=dim)
        before = lax.ppermute(last, axis, up)
        after = lax.ppermute(first, axis, down)
        shard = jnp.concatenate([before, shard, after], axis=dim)
    return shard


def convolve(padded, weights):
    return lax.conv_general_dilated(
        padded[None],
        weights,
        (1, 1, 1),
        "VALID",
        dimension_numbers=("NDHWC", "DHWIO", "NDHWC"),
        preferred_element_type=jnp.float32,
    )[0]


def pad_depth(field):
    return jnp.pad(field, ((0, 0), (0, 0), (1, 1), (0, 0)))


def forward_conv(padded, kernel):
    return convolve(padded, kernel)


def per_device(point_feats, point_voxel, cotangent, kernel):
    voxels = XD * YD * ZB
    channels = point_feats.shape[1]
    feats_in, cot_in, voxel_in = (
        lax.all_to_all(point_feats, "group", split_axis=0, concat_axis=0, tiled=True),
        lax.all_to_all(cotangent, "group", split_axis=0, concat_axis=0, tiled=True),
        lax.all_to_all(point_voxel, "group", split_axis=0, concat_axis=0, tiled=True),
    )
    index = jnp.where(voxel_in >= 0, voxel_in, voxels).astype(jnp.int32)
    sums = jax.ops.segment_sum(feats_in.astype(jnp.float32), index, voxels + 1)
    counts = jax.ops.segment_sum(jnp.ones(index.shape, jnp.float32), index, voxels + 1)
    divisor = jnp.maximum(counts, 1.0)
    mean = (sums / divisor[:, None])[:voxels].reshape(XD, YD, ZB, channels).astype(jnp.bfloat16)
    flipped = jnp.swapaxes(kernel[::-1, ::-1, ::-1], 3, 4)
    padded = pad_depth(extended(mean, (("space", 0), ("group", 1)), 1))
    out = forward_conv(padded, kernel)
    gy = jax.ops.segment_sum(cot_in.astype(jnp.float32), index, voxels + 1)[:voxels].reshape(
        XD, YD, ZB, channels
    )
    sig = jax.nn.sigmoid(out)
    gout = (gy * sig * (1.0 + out * (1.0 - sig))).astype(jnp.bfloat16)
    grad_padded = pad_depth(extended(gout, (("space", 0), ("group", 1)), 1))
    ggrid = convolve(grad_padded, flipped)
    table = jnp.concatenate(
        [ggrid.reshape(voxels, channels), jnp.zeros((1, channels), jnp.float32)], axis=0
    )
    grads = (table[index] / divisor[index][:, None]).astype(jnp.bfloat16)
    return lax.all_to_all(grads, "group", split_axis=0, concat_axis=0, tiled=True)


def solution(mesh):
    placed = (P(("space", "group"), None), P(("space", "group")), P(("space", "group"), None), P())
    return jax.shard_map(
        per_device,
        mesh=mesh,
        in_specs=placed,
        out_specs=P(("space", "group"), None),
        check_vma=False,
    )
```

profile of v0, /device:TPU:6, one launch (start us, length us, event | category | flops | bytes accessed | tf_op | source)
XLA Modules:
  0.0 172.7 jit_solution(10103457459254365)
XLA Ops:
  0.0 7.2 %all-to-all-start = ((s32[8,256,1]{1,2,0:T(1,128)}), s32[8,256,1]{1,2,0:T(1,128)S(1)}, u32[]{:S(2)}, u32[]{:S(2)}) async-start(s32[8,256,1]{1,2,0:T(1,128)} %bitcast.69), calls=%async_computation | async-start | bytes 16384 | tf_op jit(solution)/shard_map/all_to_all | solution.py:49
  7.2 1.6 copy.63
  8.8 1.6 copy.64
  10.4 4.6 %all-to-all-done = s32[8,256,1]{1,2,0:T(1,128)S(1)} async-done(((s32[8,256,1]{1,2,0:T(1,128)}), s32[8,256,1]{1,2,0:T(1,128)S(1)}, u32[]{:S(2)}, u32[]{:S(2)}) %all-to-all-start) | async-done | bytes 8224 | tf_op jit(solution)/shard_map/all_to_all | solution.py:49
  15.0 3.4 %all-to-all-start.2 = ((bf16[8,256,32]{1,2,0:T(8,128)(2,1)}), bf16[8,256,32]{1,2,0:T(8,128)(2,1)S(1)}, u32[]{:S(2)}, u32[]{:S(2)}) async-start(bf16[8,256,32]{1,2,0:T(8,128)(2,1)} %bitcast.47), calls=%async_computation.2 | async-start | bytes 262144 | tf_op jit(solution)/shard_map/all_to_all | solution.py:47
  18.4 13.2 %scatter_custom_fusion.2 = f32[4097]{0:T(1024)S(1)} fusion(s32[2048]{0:T(1024)S(1)} %bitcast.66, f32[2048]{0:T(1024)S(1)} %broadcast.65, f32[]{:T(128)} %constant.6.clone.1), kind=kCustom, calls=%fused_computation.67 | custom fusion | flops 2048 | bytes 16392 | tf_op jit(solution)/shard_map/scatter-add | solution.py:53
  31.6 6.6 %all-to-all-start.1 = ((bf16[8,256,32]{1,2,0:T(8,128)(2,1)}), bf16[8,256,32]{1,2,0:T(8,128)(2,1)S(1)}, u32[]{:S(2)}, u32[]{:S(2)}) async-start(bf16[8,256,32]{1,2,0:T(8,128)(2,1)} %bitcast.48), calls=%async_computation.1 | async-start | bytes 262144 | tf_op jit(solution)/shard_map/all_to_all | solution.py:48
  38.2 0.2 copy.48
  38.4 13.6 %scatter_custom_fusion.1 = f32[4097,32]{1,0:T(8,128)S(1)} fusion(s32[2048]{0:T(1024)S(1)} %bitcast.67, f32[2048,32]{1,0:T(8,128)S(1)} %bitcast.58, f32[]{:T(128)} %constant.6.clone.1), kind=kCustom, calls=%fused_computation.51 | custom fusion | flops 65536 | bytes 524420 | tf_op jit(solution)/shard_map/scatter-add | solution.py:52
  52.1 1.8 %divide_convert_fusion = bf16[4097,32]{1,0:T(8,128)(2,1)S(1)} fusion(f32[4097,32]{1,0:T(8,128)S(1)} %scatter_custom_fusion.1, f32[4097]{0:T(1024)S(1)} %broadcast_maximum_fusion), kind=kLoop, calls=%fused_computation.26 | loop fusion | flops 262208 | bytes 803012 | tf_op jit(solution)/shard_map/convert.2
  53.9 1.9 %collective-permute-start = (bf16[1,16,16,32]{3,2,1,0:T(8,128)(2,1)S(1)}, bf16[1,16,16,32]{3,2,1,0:T(8,128)(2,1)S(1)}, u32[]{:S(2)}, u32[]{:S(2)}) collective-permute-start(bf16[1,16,16,32]{3,2,1,0:T(8,128)(2,1)S(1)} %bitcast.63), channel_id=1, source_target_pairs={{0,8},{8,16},{16,24},{24,32},{32,40},{40,48},{48,56},{56,64},{64,7... | collective-permute-start | bytes 49160 | tf_op jit(solution)/shard_map/ppermute | solution.py:18
  55.8 12.8 %collective-permute-start.1 = (bf16[1,16,16,32]{3,2,1,0:T(8,128)(2,1)S(1)}, bf16[1,16,16,32]{3,2,1,0:T(8,128)(2,1)S(1)}, u32[]{:S(2)}, u32[]{:S(2)}) collective-permute-start(bf16[1,16,16,32]{3,2,1,0:T(8,128)(2,1)S(1)} %bitcast.62), channel_id=1, source_target_pairs={{8,0},{16,8},{24,16},{32,24},{40,32},{48,40},{56,48},{64,56},{72,6... | collective-permute-start | bytes 49160 | tf_op jit(solution)/shard_map/ppermute | solution.py:19
  68.7 1.8 %collective-permute-done.1 = bf16[1,16,16,32]{3,2,1,0:T(8,128)(2,1)S(1)} collective-permute-done((bf16[1,16,16,32]{3,2,1,0:T(8,128)(2,1)S(1)}, bf16[1,16,16,32]{3,2,1,0:T(8,128)(2,1)S(1)}, u32[]{:S(2)}, u32[]{:S(2)}) %collective-permute-start.1) | collective-permute-done | bytes 16416 | tf_op jit(solution)/shard_map/ppermute | solution.py:19
  70.5 0.7 pad_maximum_fusion.5
  71.2 4.2 %collective-permute-start.2 = (bf16[18,1,16,32]{3,2,1,0:T(8,128)(2,1)}, bf16[18,1,16,32]{3,2,1,0:T(8,128)(2,1)}, u32[]{:S(2)}, u32[]{:S(2)}) collective-permute-start(bf16[18,1,16,32]{3,2,1,0:T(8,128)(2,1)} %get-tuple-element.7), channel_id=1, source_target_pairs={{0,1},{1,2},{2,3},{3,4},{4,5},{5,6},{6,7},{8,9},{9,10},{10,11},{11... | collective-permute-start | bytes 55304 | tf_op jit(solution)/shard_map/ppermute | solution.py:18
  75.4 1.3 collective-permute-start.3
  76.7 1.2 copy.47
  77.9 14.2 %scatter_custom_fusion = f32[4097,32]{1,0:T(8,128)S(1)} fusion(s32[2048]{0:T(1024)S(1)} %bitcast.68, f32[2048,32]{1,0:T(8,128)} %bitcast.57, f32[]{:T(128)} %constant.6.clone.1), kind=kCustom, calls=%fused_computation.53 | custom fusion | flops 65536 | bytes 524928 | tf_op jit(solution)/shard_map/scatter-add | solution.py:59
  92.1 0.9 copy-done.3
  93.1 2.5 %fusion.26 = bf16[18,18,1,18,32]{4,3,1,0,2:T(8,128)(2,1)S(1)} fusion(bf16[18,1,16,32]{3,2,1,0:T(8,128)(2,1)} %collective-permute-done.3, bf16[18,1,16,32]{3,2,1,0:T(8,128)(2,1)} %collective-permute-done.2, bf16[1,16,16,32]{3,2,1,0:T(8,128)(2,1)S(1)} %copy-done.5, bf16[16,16,16,32]{3,2,1,0:T(8,128)(2,1)S(1)} %bitcast.51, bf16[1,16,16,32]{3,2,1,0:T(8,128)(2,1)S(1)} %copy-done.3), kind=kLoop, calls=%fused_computation.40 | loop fusion | flops 3359232 | bytes 705024 | tf_op jit(solution)/shard_map/broadcast_in_dim | solution.py:26
  95.6 1.7 pad.10
  97.3 5.1 %reshape.65 = bf16[18,18,1,8,3,32]{5,4,3,1,0,2:T(4,128)(2,1)S(1)} reshape(bf16[18,18,1,24,32]{4,3,1,0,2:T(8,128)(2,1)} %pad.10) | data formatting | bytes 995328 | tf_op jit(solution)/shard_map/conv_general_dilated | solution.py:25
  102.4 0.3 copy.37
  102.8 0.3 slice.63
  103.2 0.3 copy-done.6
  103.5 4.6 %fusion.35 = f32[16,16,8,3,32]{4,2,3,1,0:T(8,128)S(1)} fusion(bf16[3,3,3,32,32]{4,3,2,1,0:T(8,128)(2,1)S(1)} %copy-done, bf16[18,18,1,7,2,32]{5,3,4,1,0,2:T(8,128)(2,1)S(1)} %slice.63, bf16[18,18,1,8,3,32]{5,3,4,1,0,2:T(8,128)(2,1)S(1)} %copy.37, pred[8,3]{0,1:T(4,128)(4,1)S(1)} %copy-done.6), kind=kOutput, calls=%fused_computation.48 | convolution fusion | flops 342423552 | bytes 1629720 | tf_op jit(solution)/shard_map/conv_general_dilated | solution.py:25
  108.1 0.5 copy.38
  108.7 1.0 slice-done
  109.7 1.1 fusion.19
  110.8 1.9 %collective-permute-start.4 = (bf16[1,16,16,32]{3,1,2,0:T(8,128)(2,1)S(1)}, bf16[1,16,16,32]{3,1,2,0:T(8,128)(2,1)S(1)}, u32[]{:S(2)}, u32[]{:S(2)}) collective-permute-start(bf16[1,16,16,32]{3,1,2,0:T(8,128)(2,1)S(1)} %get-tuple-element.11), channel_id=1, source_target_pairs={{0,8},{8,16},{16,24},{24,32},{32,40},{40,48},{48,56},{56,64},{64,7... | collective-permute-start | bytes 49160 | tf_op jit(solution)/shard_map/ppermute | solution.py:18
  112.8 5.8 %collective-permute-start.5 = (bf16[1,16,16,32]{3,1,2,0:T(8,128)(2,1)S(1)}, bf16[1,16,16,32]{3,1,2,0:T(8,128)(2,1)S(1)}, u32[]{:S(2)}, u32[]{:S(2)}) collective-permute-start(bf16[1,16,16,32]{3,1,2,0:T(8,128)(2,1)S(1)} %get-tuple-element.12), channel_id=1, source_target_pairs={{8,0},{16,8},{24,16},{32,24},{40,32},{48,40},{56,48},{64,56},{72,6... | collective-permute-start | bytes 49160 | tf_op jit(solution)/shard_map/ppermute | solution.py:19
  118.5 1.9 %collective-permute-done.5 = bf16[1,16,16,32]{3,1,2,0:T(8,128)(2,1)S(1)} collective-permute-done((bf16[1,16,16,32]{3,1,2,0:T(8,128)(2,1)S(1)}, bf16[1,16,16,32]{3,1,2,0:T(8,128)(2,1)S(1)}, u32[]{:S(2)}, u32[]{:S(2)}) %collective-permute-start.5) | collective-permute-done | bytes 16416 | tf_op jit(solution)/shard_map/ppermute | solution.py:19
  120.4 0.3 pad_maximum_fusion.2
  120.7 4.7 %collective-permute-start.6 = (bf16[18,1,16,32]{3,1,2,0:T(2,128)(2,1)S(1)}, bf16[18,1,16,32]{3,1,2,0:T(2,128)(2,1)S(1)}, u32[]{:S(2)}, u32[]{:S(2)}) collective-permute-start(bf16[18,1,16,32]{3,1,2,0:T(2,128)(2,1)S(1)} %get-tuple-element.5), channel_id=1, source_target_pairs={{0,1},{1,2},{2,3},{3,4},{4,5},{5,6},{6,7},{8,9},{9,10},{10,11},{11... | collective-permute-start | bytes 55304 | tf_op jit(solution)/shard_map/ppermute | solution.py:18
  125.4 1.5 collective-permute-start.7
  126.9 11.8 %gather_fusion.1 = f32[2048]{0:T(1024)S(1)} fusion(f32[4097]{0:T(1024)S(1)} %broadcast_maximum_fusion, s32[2048]{0:T(1024)S(1)} %broadcast_clamp_fusion), kind=kCustom, calls=%fused_computation.1 | custom fusion | bytes 24576 | tf_op jit(solution)/shard_map/gather | solution.py:69
  138.7 2.1 %fusion.20 = bf16[18,18,1,18,32]{4,1,3,0,2:T(8,128)(2,1)S(1)} fusion(bf16[18,1,16,32]{3,1,2,0:T(2,128)(2,1)S(1)} %collective-permute-done.7, bf16[18,1,16,32]{3,1,2,0:T(2,128)(2,1)S(1)} %collective-permute-done.6, bf16[1,16,16,32]{3,1,2,0:T(8,128)(2,1)S(1)} %collective-permute-done.5, bf16[16,16,16,32]{3,1,2,0:T(8,128)(2,1)S(1)} %fusion.19, ...), kind=kLoop, calls=%fused_computation.32 | loop fusion | flops 3359232 | bytes 705024 | tf_op jit(solution)/shard_map/broadcast_in_dim | solution.py:26
  140.8 0.7 pad.12
  141.5 0.3 copy.42
  141.8 0.3 slice.67
  142.1 4.6 %fusion.32 = f32[16,16,8,3,32]{4,2,3,1,0:T(8,128)S(1)} fusion(bf16[3,3,3,32,32]{4,3,2,1,0:T(8,128)(2,1)S(1)} %copy-done, bf16[18,18,1,7,2,32]{5,3,4,1,0,2:T(8,128)(2,1)S(1)} %slice.67, bf16[18,18,1,8,3,32]{5,3,4,1,0,2:T(8,128)(2,1)S(1)} %copy.42, pred[8,3]{0,1:T(4,128)(4,1)S(1)} %copy-done.6), kind=kOutput, calls=%fused_computation.47 | convolution fusion | flops 342423552 | bytes 1629720 | tf_op jit(solution)/shard_map/conv_general_dilated | solution.py:25
  146.8 0.5 copy.43
  147.3 0.2 slice.68
  147.5 0.7 copy.44
  148.3 5.5 %gather_fusion = f32[2048,32]{1,0:T(8,128)S(1)} fusion(f32[4097,32]{1,0:T(8,128)S(1)} %concatenate.19, s32[2048]{0:T(1024)S(1)} %broadcast_clamp_fusion), kind=kCustom, calls=%fused_computation | custom fusion | bytes 532480 | tf_op jit(solution)/shard_map/gather | solution.py:69
  153.8 0.3 copy.45
  154.1 17.9 %all_to_all.39 = bf16[8,256,32]{1,2,0:T(8,128)(2,1)S(1)} all-to-all(bf16[8,256,32]{1,2,0:T(8,128)(2,1)S(1)} %divide_convert_fusion.1), channel_id=1, replica_groups=mesh['space'=96,'group'=8] {'group'}, dimensions={0} | all-to-all | bytes 262144 | tf_op jit(solution)/shard_map/all_to_all | solution.py:70
  172.0 0.7 copy.55
  (31 shorter events, 0.5 us)
Async XLA Ops:
  0.0 103.2 %copy-start = (bf16[3,3,3,32,32]{4,3,2,1,0:T(8,128)(2,1)S(1)}, bf16[3,3,3,32,32]{4,3,2,1,0:T(8,128)(2,1)}, u32[]{:S(2)}) copy-start(bf16[3,3,3,32,32]{4,3,2,1,0:T(8,128)(2,1)} %param.7) | copy-start | bytes 165892
  0.0 15.0 %all-to-all-start = ((s32[8,256,1]{1,2,0:T(1,128)}), s32[8,256,1]{1,2,0:T(1,128)S(1)}, u32[]{:S(2)}, u32[]{:S(2)}) async-start(s32[8,256,1]{1,2,0:T(1,128)} %bitcast.69), calls=%async_computation | async-start | bytes 16384 | tf_op jit(solution)/shard_map/all_to_all | solution.py:49
  15.0 16.6 %all-to-all-start.2 = ((bf16[8,256,32]{1,2,0:T(8,128)(2,1)}), bf16[8,256,32]{1,2,0:T(8,128)(2,1)S(1)}, u32[]{:S(2)}, u32[]{:S(2)}) async-start(bf16[8,256,32]{1,2,0:T(8,128)(2,1)} %bitcast.47), calls=%async_computation.2 | async-start | bytes 262144 | tf_op jit(solution)/shard_map/all_to_all | solution.py:47
  31.6 45.1 %all-to-all-start.1 = ((bf16[8,256,32]{1,2,0:T(8,128)(2,1)}), bf16[8,256,32]{1,2,0:T(8,128)(2,1)S(1)}, u32[]{:S(2)}, u32[]{:S(2)}) async-start(bf16[8,256,32]{1,2,0:T(8,128)(2,1)} %bitcast.48), calls=%async_computation.1 | async-start | bytes 262144 | tf_op jit(solution)/shard_map/all_to_all | solution.py:48
  53.9 14.8 %collective-permute-start = (bf16[1,16,16,32]{3,2,1,0:T(8,128)(2,1)S(1)}, bf16[1,16,16,32]{3,2,1,0:T(8,128)(2,1)S(1)}, u32[]{:S(2)}, u32[]{:S(2)}) collective-permute-start(bf16[1,16,16,32]{3,2,1,0:T(8,128)(2,1)S(1)} %bitcast.63), channel_id=1, source_target_pairs={{0,8},{8,16},{16,24},{24,32},{32,40},{40,48},{48,56},{56,64},{64,7... | collective-permute-start | bytes 49160 | tf_op jit(solution)/shard_map/ppermute | solution.py:18
  55.8 14.7 %collective-permute-start.1 = (bf16[1,16,16,32]{3,2,1,0:T(8,128)(2,1)S(1)}, bf16[1,16,16,32]{3,2,1,0:T(8,128)(2,1)S(1)}, u32[]{:S(2)}, u32[]{:S(2)}) collective-permute-start(bf16[1,16,16,32]{3,2,1,0:T(8,128)(2,1)S(1)} %bitcast.62), channel_id=1, source_target_pairs={{8,0},{16,8},{24,16},{32,24},{40,32},{48,40},{56,48},{64,56},{72,6... | collective-permute-start | bytes 49160 | tf_op jit(solution)/shard_map/ppermute | solution.py:19
  68.7 9.1 %copy-start.2 = (bf16[1,16,16,32]{3,2,1,0:T(8,128)(2,1)}, bf16[1,16,16,32]{3,2,1,0:T(8,128)(2,1)S(1)}, u32[]{:S(2)}) copy-start(bf16[1,16,16,32]{3,2,1,0:T(8,128)(2,1)S(1)} %collective-permute-done) | copy-start | bytes 49156
  70.5 7.3 %copy-start.4 = (bf16[1,16,16,32]{3,2,1,0:T(8,128)(2,1)}, bf16[1,16,16,32]{3,2,1,0:T(8,128)(2,1)S(1)}, u32[]{:S(2)}) copy-start(bf16[1,16,16,32]{3,2,1,0:T(8,128)(2,1)S(1)} %collective-permute-done.1) | copy-start | bytes 49156
  71.2 20.9 %collective-permute-start.2 = (bf16[18,1,16,32]{3,2,1,0:T(8,128)(2,1)}, bf16[18,1,16,32]{3,2,1,0:T(8,128)(2,1)}, u32[]{:S(2)}, u32[]{:S(2)}) collective-permute-start(bf16[18,1,16,32]{3,2,1,0:T(8,128)(2,1)} %get-tuple-element.7), channel_id=1, source_target_pairs={{0,1},{1,2},{2,3},{3,4},{4,5},{5,6},{6,7},{8,9},{9,10},{10,11},{11... | collective-permute-start | bytes 55304 | tf_op jit(solution)/shard_map/ppermute | solution.py:18
  75.4 16.7 %collective-permute-start.3 = (bf16[18,1,16,32]{3,2,1,0:T(8,128)(2,1)}, bf16[18,1,16,32]{3,2,1,0:T(8,128)(2,1)}, u32[]{:S(2)}, u32[]{:S(2)}) collective-permute-start(bf16[18,1,16,32]{3,2,1,0:T(8,128)(2,1)} %get-tuple-element.8), channel_id=1, source_target_pairs={{1,0},{2,1},{3,2},{4,3},{5,4},{6,5},{7,6},{9,8},{10,9},{11,10},{12... | collective-permute-start | bytes 55304 | tf_op jit(solution)/shard_map/ppermute | solution.py:19
  92.0 3.6 %copy-start.1 = (f32[4097,32]{1,0:T(8,128)}, f32[4097,32]{1,0:T(8,128)S(1)}, u32[]{:S(2)}) copy-start(f32[4097,32]{1,0:T(8,128)S(1)} %scatter_custom_fusion) | copy-start | bytes 1573252
  92.1 0.9 copy-start.3
  92.1 1.0 copy-start.5
  102.8 0.7 copy-start.6
  108.1 1.6 slice-start
  110.8 7.7 %collective-permute-start.4 = (bf16[1,16,16,32]{3,1,2,0:T(8,128)(2,1)S(1)}, bf16[1,16,16,32]{3,1,2,0:T(8,128)(2,1)S(1)}, u32[]{:S(2)}, u32[]{:S(2)}) collective-permute-start(bf16[1,16,16,32]{3,1,2,0:T(8,128)(2,1)S(1)} %get-tuple-element.11), channel_id=1, source_target_pairs={{0,8},{8,16},{16,24},{24,32},{32,40},{40,48},{48,56},{56,64},{64,7... | collective-permute-start | bytes 49160 | tf_op jit(solution)/shard_map/ppermute | solution.py:18
  112.8 7.6 %collective-permute-start.5 = (bf16[1,16,16,32]{3,1,2,0:T(8,128)(2,1)S(1)}, bf16[1,16,16,32]{3,1,2,0:T(8,128)(2,1)S(1)}, u32[]{:S(2)}, u32[]{:S(2)}) collective-permute-start(bf16[1,16,16,32]{3,1,2,0:T(8,128)(2,1)S(1)} %get-tuple-element.12), channel_id=1, source_target_pairs={{8,0},{16,8},{24,16},{32,24},{40,32},{48,40},{56,48},{64,56},{72,6... | collective-permute-start | bytes 49160 | tf_op jit(solution)/shard_map/ppermute | solution.py:19
  120.7 18.0 %collective-permute-start.6 = (bf16[18,1,16,32]{3,1,2,0:T(2,128)(2,1)S(1)}, bf16[18,1,16,32]{3,1,2,0:T(2,128)(2,1)S(1)}, u32[]{:S(2)}, u32[]{:S(2)}) collective-permute-start(bf16[18,1,16,32]{3,1,2,0:T(2,128)(2,1)S(1)} %get-tuple-element.5), channel_id=1, source_target_pairs={{0,1},{1,2},{2,3},{3,4},{4,5},{5,6},{6,7},{8,9},{9,10},{10,11},{11... | collective-permute-start | bytes 55304 | tf_op jit(solution)/shard_map/ppermute | solution.py:18
  125.4 13.3 %collective-permute-start.7 = (bf16[18,1,16,32]{3,1,2,0:T(2,128)(2,1)S(1)}, bf16[18,1,16,32]{3,1,2,0:T(2,128)(2,1)S(1)}, u32[]{:S(2)}, u32[]{:S(2)}) collective-permute-start(bf16[18,1,16,32]{3,1,2,0:T(2,128)(2,1)S(1)} %get-tuple-element.6), channel_id=1, source_target_pairs={{1,0},{2,1},{3,2},{4,3},{5,4},{6,5},{7,6},{9,8},{10,9},{11,10},{12... | collective-permute-start | bytes 55304 | tf_op jit(solution)/shard_map/ppermute | solution.py:19
where the time goes:
time: 174 us; the launch traced here: 173 us
  starting transfers between devices  51.2 us (29%)
  other arithmetic  49.6 us (29%)
  local copies, waits for them, and re-layouts  36 us (21%)
  blocking collectives  17.9 us (10%)
  matrix products  9.29 us (5%)
  waiting for transfers between devices  8.28 us (5%)
    ppermute x4, starting transfers between devices, extended(): after = lax.ppermute(first, axis, down)  21.3 us
    all_to_all x1, blocking collectives, per_device(): lax.all_to_all(grads, 'group', split_axis=0, concat_axis=0, tiled=True)  17.9 us
    gather x3, local copies, waits for them, and re-layouts, per_device(): grads = (table[index] / divisor[index][:, None]).astype(jnp.bfloat16)  17.5 us
    scatter-add x1, other arithmetic, per_device(): jax.ops.segment_sum(cot_in.astype(jnp.float32), index, voxels + 1)[:voxels]  14.2 us
    scatter-add x1, other arithmetic, per_device(): sums = jax.ops.segment_sum(feats_in.astype(jnp.float32), index, voxels + 1)  13.6 us
    scatter-add x1, other arithmetic, per_device(): jax.ops.segment_sum(jnp.ones(index.shape, jnp.float32), index, voxels + 1)  13.2 us
    ppermute x4, starting transfers between devices, extended(): before = lax.ppermute(last, axis, up)  12.6 us
    conv_general_dilated x2, matrix products, convolve(): lax.conv_general_dilated(padded[None], weights, (1, 1, 1), 'VALID', dimen...  9.29 us
  transfers between devices with their start and end apart: 11, of which 3 were waited for; matrix products, arithmetic and copies ran while one was open for 35% of the time, Pallas kernels for 0%

commit v1 on v0

v1 whole, which is shorter than its diff:
```python
import functools

import jax
import jax.numpy as jnp
from jax import lax
from jax.experimental import pallas as pl
from jax.experimental.pallas import tpu as pltpu
from jax.sharding import PartitionSpec as P

XD = 16
YD = 16
ZB = 16
C = 32
V_DEV = XD * YD * ZB
HALF = 64
PW = 2 * C + 3
TV = 512
TK = 512
TP = 256
TC = 512


def extended(shard, sides, width):
    for axis, dim in sides:
        size, length = (lax.axis_size(axis), shard.shape[dim])
        up = [(i, (i + 1) % size) for i in range(size - 1)]
        down = [(j, i) for i, j in up]
        last = lax.slice_in_dim(shard, length - width, length, axis=dim)
        first = lax.slice_in_dim(shard, 0, width, axis=dim)
        before = lax.ppermute(last, axis, up)
        after = lax.ppermute(first, axis, down)
        shard = jnp.concatenate([before, shard, after], axis=dim)
    return shard


def convolve(padded, weights):
    return lax.conv_general_dilated(
        padded[None],
        weights,
        (1, 1, 1),
        "VALID",
        dimension_numbers=("NDHWC", "DHWIO", "NDHWC"),
        preferred_element_type=jnp.float32,
    )[0]


def pad_depth(field):
    return jnp.pad(field, ((0, 0), (0, 0), (1, 1), (0, 0)))


def scatter_kernel(idx_ref, p_ref, out_ref):
    base = pl.program_id(0) * TV
    npts = p_ref.shape[0]
    acc = jnp.zeros((TV, PW), jnp.float32)
    rows = lax.broadcasted_iota(jnp.int32, (TV, TK), 0) + base
    for k in range(npts // TK):
        ids = idx_ref[:, pl.ds(k * TK, TK)]
        hot = (rows == ids).astype(jnp.bfloat16)
        acc = acc + jnp.dot(hot, p_ref[pl.ds(k * TK, TK), :], preferred_element_type=jnp.float32)
    col = lax.broadcasted_iota(jnp.int32, (TV, PW), 1)
    div = jnp.maximum(acc[:, 2 * C : 2 * C + 1], 1.0)
    mean = (acc / div).astype(jnp.bfloat16).astype(jnp.float32)
    out_ref[...] = jnp.where(col < C, mean, jnp.where(col == 2 * C, div, acc))


def scatter_sums(idx_row, payload):
    npts = payload.shape[0]
    return pl.pallas_call(
        scatter_kernel,
        out_shape=jax.ShapeDtypeStruct((V_DEV, PW), jnp.float32),
        grid=(V_DEV // TV,),
        in_specs=[
            pl.BlockSpec((1, npts), lambda t: (0, 0)),
            pl.BlockSpec((npts, PW), lambda t: (0, 0)),
        ],
        out_specs=pl.BlockSpec((TV, PW), lambda t: (t, 0)),
        cost_estimate=pl.CostEstimate(
            flops=2 * V_DEV * npts * 128, transcendentals=0, bytes_accessed=npts * PW * 2 + V_DEV * PW * 4
        ),
    )(idx_row, payload)


def gather_kernel(idx_ref, t_ref, o_ref):
    ids = idx_ref[...]
    acc = jnp.zeros((TP, C), jnp.float32)
    cols = lax.broadcasted_iota(jnp.int32, (TP, TC), 1)
    for c in range(V_DEV // TC):
        hot = (cols + c * TC == ids).astype(jnp.bfloat16)
        acc = acc + jnp.dot(hot, t_ref[pl.ds(c * TC, TC), :], preferred_element_type=jnp.float32)
    o_ref[...] = acc.astype(o_ref.dtype)


def gather_rows(idx_col, table):
    npts = idx_col.shape[0]
    return pl.pallas_call(
        gather_kernel,
        out_shape=jax.ShapeDtypeStruct((npts, C), jnp.bfloat16),
        grid=(npts // TP,),
        in_specs=[
            pl.BlockSpec((TP, 1), lambda t: (t, 0)),
            pl.BlockSpec((V_DEV, C), lambda t: (0, 0)),
        ],
        out_specs=pl.BlockSpec((TP, C), lambda t: (t, 0)),
        cost_estimate=pl.CostEstimate(
            flops=2 * V_DEV * npts * 128, transcendentals=0, bytes_accessed=npts * C * 2 + V_DEV * C * 2
        ),
    )(idx_col, table)


def per_device(point_feats, point_voxel, cotangent, kernel):
    npts = point_feats.shape[0]
    live = point_voxel >= 0
    hi = jnp.where(live, point_voxel // HALF, -1).astype(jnp.bfloat16)
    lo = jnp.where(live, point_voxel % HALF, 0).astype(jnp.bfloat16)
    payload = jnp.concatenate(
        [point_feats, cotangent, jnp.ones((npts, 1), jnp.bfloat16), hi[:, None], lo[:, None]], axis=1
    )
    got = lax.all_to_all(payload, "group", split_axis=0, concat_axis=0, tiled=True)
    index = got[:, 2 * C + 1].astype(jnp.int32) * HALF + got[:, 2 * C + 2].astype(jnp.int32)
    stats = scatter_sums(index.reshape(1, npts), got)
    divisor = stats[:, 2 * C]
    field = stats[:, : 2 * C].reshape(XD, YD, ZB, 2 * C)
    wide = extended(field, (("space", 0), ("group", 1)), 2)
    mean = wide[..., :C].astype(jnp.bfloat16)
    out = convolve(pad_depth(mean), kernel)
    gy = wide[1:-1, 1:-1, :, C:]
    sig = jax.nn.sigmoid(out)
    gout = (gy * sig * (1.0 + out * (1.0 - sig))).astype(jnp.bfloat16)
    flipped = jnp.swapaxes(kernel[::-1, ::-1, ::-1], 3, 4)
    ggrid = convolve(pad_depth(gout), flipped)
    table = (ggrid.reshape(V_DEV, C) / divisor[:, None]).astype(jnp.bfloat16)
    grads = gather_rows(index.reshape(npts, 1), table)
    return lax.all_to_all(grads, "group", split_axis=0, concat_axis=0, tiled=True)


def solution(mesh):
    placed = (P(("space", "group"), None), P(("space", "group")), P(("space", "group"), None), P())
    return jax.shard_map(
        per_device,
        mesh=mesh,
        in_specs=placed,
        out_specs=P(("space", "group"), None),
        check_vma=False,
    )
```

time: 174 us -> 135 us (0.78)
  other arithmetic: 49.6 us -> 7.01 us
  starting transfers between devices: 51.2 us -> 17.2 us
  local copies, waits for them, and re-layouts: 36 us -> 8.4 us
  matrix products: 9.29 us -> 36.8 us
  Pallas kernels: 0 us -> 16.7 us
  blocking collectives: 17.9 us -> 33.5 us
  waiting for transfers between devices: 8.28 us -> 14.4 us
    scatter-add x3 -> x0, other arithmetic: 41 us -> none  [the longest x1 14.2 us: per_device(): jax.ops.segment_sum(cot_in.astype(jnp.float32), index, voxels + 1)[:voxels]]
    conv_general_dilated x2, matrix products: 9.29 us -> 36.8 us  [convolve(): lax.conv_general_dilated(padded[None], weights, (1, 1, 1), 'VALID', dimen...]
    all_to_all x0 -> x1, blocking collectives: none -> 19.5 us  [per_device(): lax.all_to_all(payload, 'group', split_axis=0, concat_axis=0, tiled=True)]
    gather x3 -> x0, local copies, waits for them, and re-layouts: 17.5 us -> none  [per_device(): grads = (table[index] / divisor[index][:, None]).astype(jnp.bfloat16)]
    all_to_all x3 -> x0, starting transfers between devices: 17.2 us -> none  [the longest x1 7.23 us: per_device(): lax.all_to_all(point_voxel, 'group', split_axis=0, concat_axis=0, tiled=T...]
    pallas_call x0 -> x2, Pallas kernels: none -> 16.7 us  [the longest x1 8.55 us: gather_rows(): pl.pallas_call(gather_kernel, out_shape=jax.ShapeDtypeStruct((npts, C), j...]
    ppermute x4 -> x2, starting transfers between devices: 12.6 us -> 3.52 us  [extended(): before = lax.ppermute(last, axis, up)]
    conv_general_dilated x9 -> x0, local copies, waits for them, and re-layouts: 8.32 us -> none  [convolve(): lax.conv_general_dilated(padded[None], weights, (1, 1, 1), 'VALID', dimen...]
  transfers between devices with their start and end apart: 11 -> 4, of which waited for: 3 -> 4; matrix products, arithmetic and copies ran while one was open for 35% -> 1% of each run, Pallas kernels for 0% -> 0%
where the time goes in v1:
time: 135 us; the launch traced here: 134 us
  matrix products  36.8 us (27%)
  blocking collectives  33.5 us (25%)
  starting transfers between devices  17.2 us (13%)
  Pallas kernels  16.7 us (12%)
  waiting for transfers between devices  14.4 us (11%)
  local copies, waits for them, and re-layouts  8.4 us (6%)
  other arithmetic  7.01 us (5%)
    conv_general_dilated x2, matrix products, convolve(): lax.conv_general_dilated(padded[None], weights, (1, 1, 1), 'VALID', dimen...  36.8 us
    all_to_all x1, blocking collectives, per_device(): lax.all_to_all(payload, 'group', split_axis=0, concat_axis=0, tiled=True)  19.5 us
    all_to_all x1, blocking collectives, per_device(): lax.all_to_all(grads, 'group', split_axis=0, concat_axis=0, tiled=True)  14.1 us
    ppermute x2, starting transfers between devices, extended(): after = lax.ppermute(first, axis, down)  13.7 us
    pallas_call x1, Pallas kernels, gather_rows(): pl.pallas_call(gather_kernel, out_shape=jax.ShapeDtypeStruct((npts, C), j...  8.55 us
    pallas_call x1, Pallas kernels, scatter_sums(): pl.pallas_call(scatter_kernel, out_shape=jax.ShapeDtypeStruct((V_DEV, PW)...  8.13 us
    ppermute x2, waiting for transfers between devices, extended(): before = lax.ppermute(last, axis, up)  8 us
    ppermute x2, waiting for transfers between devices, extended(): after = lax.ppermute(first, axis, down)  6.35 us
  transfers between devices with their start and end apart: 4, of which 4 were waited for; matrix products, arithmetic and copies ran while one was open for 1% of the time, Pallas kernels for 0%

profile of v1, /device:TPU:6, one launch (start us, length us, event | category | flops | bytes accessed | tf_op | source)
XLA Modules:
  0.0 134.2 jit_solution(2731370560372017467)
XLA Ops:
  0.0 0.0 copy-start
  0.0 0.8 fusion.9
  0.8 0.9 copy.34
  1.7 0.9 copy.35
  2.7 0.1 copy.24
  2.8 19.5 %all_to_all.20 = bf16[8,256,67]{1,2,0:T(8,128)(2,1)S(1)} all-to-all(bf16[8,256,67]{1,2,0:T(8,128)(2,1)S(1)} %copy.24), channel_id=1, replica_groups=mesh['space'=96,'group'=8] {'group'}, dimensions={0} | all-to-all | bytes 548864 | tf_op jit(solution)/shard_map/all_to_all | solution.py:118
  22.3 0.3 copy.25
  22.6 0.0 copy-start.2
  22.6 2.2 %fusion.12 = (s32[2048]{0:T(1024)}, s32[2048,1]{1,0:T(8,128)}) fusion(bf16[2048,67]{1,0:T(8,128)(2,1)S(1)} %bitcast.27), kind=kLoop, calls=%fused_computation.35 | loop fusion | flops 8192 | bytes 24576 | tf_op jit(solution)/shard_map/add | solution.py:119
  24.7 0.0 copy-done.2
  24.8 8.1 %shard_map.46 = f32[4096,67]{1,0:T(8,128)} custom-call(s32[1,2048]{1,0:T(1,128)} %bitcast.39, bf16[2048,67]{1,0:T(8,128)(2,1)} %bitcast.28), custom_call_target="tpu_custom_call" | custom-call | flops 2147483648 | bytes 1372160 | tf_op jit(solution)/shard_map/pallas_call | solution.py:68
  32.9 0.0 copy-start.1
  32.9 1.2 fusion.13
  34.1 12.4 %collective-permute-start.1 = (f32[2,16,16,64]{3,2,1,0:T(8,128)S(1)}, f32[2,16,16,64]{3,2,1,0:T(8,128)S(1)}, u32[]{:S(2)}, u32[]{:S(2)}) collective-permute-start(f32[2,16,16,64]{3,2,1,0:T(8,128)S(1)} %bitcast.36), channel_id=1, source_target_pairs={{8,0},{16,8},{24,16},{32,24},{40,32},{48,40},{56,48},{64,56},{72,6... | collective-permute-start | bytes 393224 | tf_op jit(solution)/shard_map/ppermute | solution.py:31
  46.5 1.9 %collective-permute-start = (f32[2,16,16,64]{3,2,1,0:T(8,128)S(1)}, f32[2,16,16,64]{3,2,1,0:T(8,128)S(1)}, u32[]{:S(2)}, u32[]{:S(2)}) collective-permute-start(f32[2,16,16,64]{3,2,1,0:T(8,128)S(1)} %bitcast.35), channel_id=1, source_target_pairs={{0,8},{8,16},{16,24},{24,32},{32,40},{40,48},{48,56},{56,64},{64,7... | collective-permute-start | bytes 393224 | tf_op jit(solution)/shard_map/ppermute | solution.py:30
  48.4 1.9 %collective-permute-done.1 = f32[2,16,16,64]{3,2,1,0:T(8,128)S(1)} collective-permute-done((f32[2,16,16,64]{3,2,1,0:T(8,128)S(1)}, f32[2,16,16,64]{3,2,1,0:T(8,128)S(1)}, u32[]{:S(2)}, u32[]{:S(2)}) %collective-permute-start.1) | collective-permute-done | bytes 131104 | tf_op jit(solution)/shard_map/ppermute | solution.py:31
  50.4 5.9 %collective-permute-done = f32[2,16,16,64]{3,2,1,0:T(8,128)S(1)} collective-permute-done((f32[2,16,16,64]{3,2,1,0:T(8,128)S(1)}, f32[2,16,16,64]{3,2,1,0:T(8,128)S(1)}, u32[]{:S(2)}, u32[]{:S(2)}) %collective-permute-start) | collective-permute-done | bytes 131104 | tf_op jit(solution)/shard_map/ppermute | solution.py:30
  56.3 1.1 pad_maximum_fusion.3
  57.4 1.6 %collective-permute-start.2 = (f32[20,2,16,64]{3,2,1,0:T(8,128)S(1)}, f32[20,2,16,64]{3,2,1,0:T(8,128)S(1)}, u32[]{:S(2)}, u32[]{:S(2)}) collective-permute-start(f32[20,2,16,64]{3,2,1,0:T(8,128)S(1)} %get-tuple-element.5), channel_id=1, source_target_pairs={{0,1},{1,2},{2,3},{3,4},{4,5},{5,6},{6,7},{8,9},{9,10},{10,11},{11... | collective-permute-start | bytes 491528 | tf_op jit(solution)/shard_map/ppermute | solution.py:30
  59.0 1.3 collective-permute-start.3
  60.3 0.0 copy-done.1
  60.3 1.2 slice_reduce_fusion
  61.5 2.1 %collective-permute-done.2 = f32[20,2,16,64]{3,2,1,0:T(8,128)S(1)} collective-permute-done((f32[20,2,16,64]{3,2,1,0:T(8,128)S(1)}, f32[20,2,16,64]{3,2,1,0:T(8,128)S(1)}, u32[]{:S(2)}, u32[]{:S(2)}) %collective-permute-start.2) | collective-permute-done | bytes 163872 | tf_op jit(solution)/shard_map/ppermute | solution.py:30
  63.6 4.4 %collective-permute-done.3 = f32[20,2,16,64]{3,2,1,0:T(8,128)S(1)} collective-permute-done((f32[20,2,16,64]{3,2,1,0:T(8,128)S(1)}, f32[20,2,16,64]{3,2,1,0:T(8,128)S(1)}, u32[]{:S(2)}, u32[]{:S(2)}) %collective-permute-start.3) | collective-permute-done | bytes 163872 | tf_op jit(solution)/shard_map/ppermute | solution.py:31
  68.0 0.4 pad_maximum_fusion
  68.4 0.3 slice.72
  68.6 0.9 pad_bitcast_fusion
  69.5 0.0 copy-done
  69.5 21.3 %fusion = f32[1,18,18,16,32]{4,0,3,2,1:T(1,128)S(1)} fusion(bf16[3,3,3,32,32]{4,3,2,1,0:T(8,128)(2,1)S(1)} %copy-done, bf16[1,20,20,18,32]{4,3,2,1,0:T(8,128)(2,1)S(1)} %pad_bitcast_fusion), kind=kOutput, calls=%fused_computation | convolution fusion | flops 286654464 | bytes 1179648 | tf_op jit(solution)/shard_map/conv_general_dilated | solution.py:37
  90.8 1.1 fusion.5
  91.9 0.7 pad_bitcast_fusion.1
  92.7 15.5 %fusion.2 = f32[1,16,16,16,32]{4,0,3,2,1:T(1,128)S(1)} fusion(bf16[3,3,3,32,32]{4,3,2,1,0:T(8,128)(2,1)S(1)} %copy-done, bf16[1,18,18,18,32]{4,3,2,1,0:T(8,128)(2,1)S(1)} %pad_bitcast_fusion.1), kind=kOutput, calls=%fused_computation.4 | convolution fusion | flops 226492416 | bytes 952832 | tf_op jit(solution)/shard_map/conv_general_dilated | solution.py:37
  108.2 1.5 %divide_convert_fusion.t_ref = bf16[4096,32]{1,0:T(8,128)(2,1)} fusion(f32[4096,32]{1,0:T(8,128)S(1)} %bitcast.30, f32[4096]{0:T(1024)S(1)} %slice_reduce_fusion), kind=kLoop, calls=%fused_computation.11 | loop fusion | flops 262144 | bytes 802816 | tf_op jit(solution)/shard_map/convert_element_type | solution.py:131
  109.7 8.6 %shard_map.47 = bf16[2048,32]{1,0:T(8,128)(2,1)} custom-call(s32[2048,1]{1,0:T(8,128)} %get-tuple-element.10.idx_ref, bf16[4096,32]{1,0:T(8,128)(2,1)} %divide_convert_fusion.t_ref), custom_call_target="tpu_custom_call" | custom-call | flops 2147483648 | bytes 393216 | tf_op jit(solution)/shard_map/pallas_call | solution.py:95
  118.3 1.2 copy.29
  119.5 14.1 %all_to_all.21 = bf16[8,256,32]{1,2,0:T(8,128)(2,1)S(1)} all-to-all(bf16[8,256,32]{1,2,0:T(8,128)(2,1)S(1)} %copy.29), channel_id=1, replica_groups=mesh['space'=96,'group'=8] {'group'}, dimensions={0} | all-to-all | bytes 262144 | tf_op jit(solution)/shard_map/all_to_all | solution.py:133
  133.6 0.7 copy.33
  (7 shorter events, 0.0 us)
Async XLA Ops:
  0.0 69.5 %copy-start = (bf16[3,3,3,32,32]{4,3,2,1,0:T(8,128)(2,1)S(1)}, bf16[3,3,3,32,32]{4,3,2,1,0:T(8,128)(2,1)}, u32[]{:S(2)}) copy-start(bf16[3,3,3,32,32]{4,3,2,1,0:T(8,128)(2,1)} %param.7) | copy-start | bytes 165892
  22.6 2.2 %copy-start.2 = (bf16[8,256,67]{2,1,0:T(8,128)(2,1)}, bf16[8,256,67]{2,1,0:T(8,128)(2,1)S(1)}, u32[]{:S(2)}) copy-start(bf16[8,256,67]{2,1,0:T(8,128)(2,1)S(1)} %copy.25) | copy-start | bytes 823300
  32.9 27.4 %copy-start.1 = (f32[4096,67]{1,0:T(8,128)S(1)}, f32[4096,67]{1,0:T(8,128)}, u32[]{:S(2)}) copy-start(f32[4096,67]{1,0:T(8,128)} %shard_map.46) | copy-start | bytes 3293188
  34.1 16.3 %collective-permute-start.1 = (f32[2,16,16,64]{3,2,1,0:T(8,128)S(1)}, f32[2,16,16,64]{3,2,1,0:T(8,128)S(1)}, u32[]{:S(2)}, u32[]{:S(2)}) collective-permute-start(f32[2,16,16,64]{3,2,1,0:T(8,128)S(1)} %bitcast.36), channel_id=1, source_target_pairs={{8,0},{16,8},{24,16},{32,24},{40,32},{48,40},{56,48},{64,56},{72,6... | collective-permute-start | bytes 393224 | tf_op jit(solution)/shard_map/ppermute | solution.py:31
  46.5 9.8 %collective-permute-start = (f32[2,16,16,64]{3,2,1,0:T(8,128)S(1)}, f32[2,16,16,64]{3,2,1,0:T(8,128)S(1)}, u32[]{:S(2)}, u32[]{:S(2)}) collective-permute-start(f32[2,16,16,64]{3,2,1,0:T(8,128)S(1)} %bitcast.35), channel_id=1, source_target_pairs={{0,8},{8,16},{16,24},{24,32},{32,40},{40,48},{48,56},{56,64},{64,7... | collective-permute-start | bytes 393224 | tf_op jit(solution)/shard_map/ppermute | solution.py:30
  57.4 6.2 %collective-permute-start.2 = (f32[20,2,16,64]{3,2,1,0:T(8,128)S(1)}, f32[20,2,16,64]{3,2,1,0:T(8,128)S(1)}, u32[]{:S(2)}, u32[]{:S(2)}) collective-permute-start(f32[20,2,16,64]{3,2,1,0:T(8,128)S(1)} %get-tuple-element.5), channel_id=1, source_target_pairs={{0,1},{1,2},{2,3},{3,4},{4,5},{5,6},{6,7},{8,9},{9,10},{10,11},{11... | collective-permute-start | bytes 491528 | tf_op jit(solution)/shard_map/ppermute | solution.py:30
  59.0 9.0 %collective-permute-start.3 = (f32[20,2,16,64]{3,2,1,0:T(8,128)S(1)}, f32[20,2,16,64]{3,2,1,0:T(8,128)S(1)}, u32[]{:S(2)}, u32[]{:S(2)}) collective-permute-start(f32[20,2,16,64]{3,2,1,0:T(8,128)S(1)} %get-tuple-element.6), channel_id=1, source_target_pairs={{1,0},{2,1},{3,2},{4,3},{5,4},{6,5},{7,6},{9,8},{10,9},{11,10},{12... | collective-permute-start | bytes 491528 | tf_op jit(solution)/shard_map/ppermute | solution.py:31

commit v2 on v0

v2 whole, which is shorter than its diff:
```python
import jax
import jax.numpy as jnp
from jax import lax
from jax.experimental import pallas as pl
from jax.experimental.pallas import tpu as pltpu
from jax.sharding import PartitionSpec as P

XD = 16
YD = 16
ZB = 16
C = 32
XY = XD * YD
ZC = ZB * C
HALF = 64
PW = 2 * C + 2
TK = 512
EX = XD + 4
EY = YD + 4
ER = EX * EY


def extended(shard, sides, width):
    for axis, dim in sides:
        size, length = (lax.axis_size(axis), shard.shape[dim])
        up = [(i, (i + 1) % size) for i in range(size - 1)]
        down = [(j, i) for i, j in up]
        last = lax.slice_in_dim(shard, length - width, length, axis=dim)
        first = lax.slice_in_dim(shard, 0, width, axis=dim)
        before = lax.ppermute(last, axis, up)
        after = lax.ppermute(first, axis, down)
        shard = jnp.concatenate([before, shard, after], axis=dim)
    return shard


def scatter_kernel(got_ref, xy_ref, z_ref, mean_ref, gy_ref, div_ref):
    npts = got_ref.shape[0]
    r = lax.broadcasted_iota(jnp.int32, (PW, ZC), 0)
    l = lax.broadcasted_iota(jnp.int32, (PW, ZC), 1)
    ef = (r == jnp.bitwise_and(l, C - 1)).astype(jnp.bfloat16)
    ec = (r == jnp.bitwise_and(l, C - 1) + C).astype(jnp.bfloat16)
    lane_z = lax.broadcasted_iota(jnp.int32, (TK, ZC), 1) >> 5
    rows = lax.broadcasted_iota(jnp.int32, (XY, TK), 0)
    sf = jnp.zeros((XY, ZC), jnp.float32)
    sc = jnp.zeros((XY, ZC), jnp.float32)
    sn = jnp.zeros((XY, ZC), jnp.float32)
    for k in range(npts // TK):
        g = got_ref[pl.ds(k * TK, TK), :]
        mask = lane_z == z_ref[pl.ds(k * TK, TK), :]
        tf = jnp.dot(g, ef, preferred_element_type=jnp.float32)
        tc = jnp.dot(g, ec, preferred_element_type=jnp.float32)
        qf = jnp.where(mask, tf, 0.0).astype(jnp.bfloat16)
        qc = jnp.where(mask, tc, 0.0).astype(jnp.bfloat16)
        qn = mask.astype(jnp.bfloat16)
        hot = (rows == xy_ref[:, pl.ds(k * TK, TK)]).astype(jnp.bfloat16)
        sf = sf + jnp.dot(hot, qf, preferred_element_type=jnp.float32)
        sc = sc + jnp.dot(hot, qc, preferred_element_type=jnp.float32)
        sn = sn + jnp.dot(hot, qn, preferred_element_type=jnp.float32)
    div = jnp.maximum(sn, 1.0)
    mean_ref[...] = (sf / div).astype(jnp.bfloat16).astype(jnp.float32)
    gy_ref[...] = sc
    div_ref[...] = div


def scatter_sums(got, xy_row, z_col):
    npts = got.shape[0]
    field = jax.ShapeDtypeStruct((XY, ZC), jnp.float32)
    return pl.pallas_call(
        scatter_kernel,
        out_shape=(field, field, field),
        cost_estimate=pl.CostEstimate(
            flops=2 * XY * npts * ZC * 3 + 4 * npts * PW * ZC, transcendentals=0,
            bytes_accessed=npts * PW * 2 + 3 * XY * ZC * 4,
        ),
    )(got, xy_row, z_col)


def conv_kernel(m_ref, g_ref, w_ref, o_ref):
    mean = m_ref[...]
    acc = jnp.zeros((ER, ZC), jnp.float32)
    for a in range(3):
        for b in range(3):
            off = (a - 1) * EY + (b - 1)
            part = jnp.dot(mean, w_ref[a * 3 + b], preferred_element_type=jnp.float32)
            acc = acc + pltpu.roll(part, (-off) % ER, 0)
    sig = 1.0 / (1.0 + jnp.exp(-acc))
    gout = (g_ref[...] * sig * (1.0 + acc * (1.0 - sig))).astype(jnp.bfloat16)
    acc = jnp.zeros((ER, ZC), jnp.float32)
    for a in range(3):
        for b in range(3):
            off = (a - 1) * EY + (b - 1)
            part = lax.dot_general(
                gout, w_ref[8 - (a * 3 + b)], (((1,), (1,)), ((), ())), preferred_element_type=jnp.float32
            )
            acc = acc + pltpu.roll(part, (-off) % ER, 0)
    o_ref[...] = acc


def conv_pair(mean_ext, gy_ext, banded):
    return pl.pallas_call(
        conv_kernel,
        out_shape=jax.ShapeDtypeStruct((ER, ZC), jnp.float32),
        compiler_params=pltpu.CompilerParams(vmem_limit_bytes=48 * 1024 * 1024),
        cost_estimate=pl.CostEstimate(
            flops=18 * 2 * ER * ZC * ZC, transcendentals=ER * ZC,
            bytes_accessed=ER * ZC * 10 + 9 * ZC * ZC * 2,
        ),
    )(mean_ext, gy_ext, banded)


def gather_kernel(t_ref, xy_ref, z_ref, o_ref):
    npts = o_ref.shape[0]
    r = lax.broadcasted_iota(jnp.int32, (ZC, C), 0)
    l = lax.broadcasted_iota(jnp.int32, (ZC, C), 1)
    fold = (jnp.bitwise_and(r, C - 1) == l).astype(jnp.bfloat16)
    lane_z = lax.broadcasted_iota(jnp.int32, (TK, ZC), 1) >> 5
    cols = lax.broadcasted_iota(jnp.int32, (TK, XY), 1)
    table = t_ref[...]
    for k in range(npts // TK):
        hot = (cols == xy_ref[pl.ds(k * TK, TK), :]).astype(jnp.bfloat16)
        rows = jnp.dot(hot, table, preferred_element_type=jnp.float32)
        mask = lane_z == z_ref[pl.ds(k * TK, TK), :]
        picked = jnp.where(mask, rows, 0.0).astype(jnp.bfloat16)
        o_ref[pl.ds(k * TK, TK), :] = jnp.dot(picked, fold, preferred_element_type=jnp.float32).astype(o_ref.dtype)


def gather_rows(table, xy_col, z_col):
    npts = xy_col.shape[0]
    return pl.pallas_call(
        gather_kernel,
        out_shape=jax.ShapeDtypeStruct((npts, C), jnp.bfloat16),
        cost_estimate=pl.CostEstimate(
            flops=2 * npts * XY * ZC + 2 * npts * ZC * C, transcendentals=0,
            bytes_accessed=npts * C * 2 + XY * ZC * 2,
        ),
    )(table, xy_col, z_col)


def banded_weights(kernel):
    zi = jnp.arange(ZB)
    shift = (zi[None, :, None] == zi[None, None, :] + jnp.arange(3)[:, None, None] - 1).astype(kernel.dtype)
    wide = jnp.einsum("dab,xydio->xyaibo", shift, kernel, preferred_element_type=jnp.float32)
    return wide.astype(kernel.dtype).reshape(9, ZC, ZC)


def per_device(point_feats, point_voxel, cotangent, kernel):
    npts = point_feats.shape[0]
    live = point_voxel >= 0
    hi = jnp.where(live, point_voxel // HALF, -1).astype(jnp.bfloat16)
    lo = jnp.where(live, point_voxel % HALF, 0).astype(jnp.bfloat16)
    payload = jnp.concatenate([point_feats, cotangent, hi[:, None], lo[:, None]], axis=1)
    got = lax.all_to_all(payload, "group", split_axis=0, concat_axis=0, tiled=True)
    index = got[:, 2 * C].astype(jnp.int32) * HALF + got[:, 2 * C + 1].astype(jnp.int32)
    xy = jnp.where(index >= 0, index >> 4, -1)
    z = jnp.bitwise_and(index, ZB - 1)
    mean, gy, divisor = scatter_sums(got, xy.reshape(1, npts), z.reshape(npts, 1))
    field = jnp.concatenate([mean, gy], axis=1).reshape(XD, YD, 2 * ZC)
    wide = extended(field, (("space", 0), ("group", 1)), 2)
    mean_ext = wide[..., :ZC].astype(jnp.bfloat16).reshape(ER, ZC)
    gy_ext = wide[..., ZC:].reshape(ER, ZC)
    ggrid = conv_pair(mean_ext, gy_ext, banded_weights(kernel))
    center = ggrid.reshape(EX, EY, ZC)[2 : 2 + XD, 2 : 2 + YD].reshape(XY, ZC)
    table = (center / divisor).astype(jnp.bfloat16)
    grads = gather_rows(table, xy.reshape(npts, 1), z.reshape(npts, 1))
    return lax.all_to_all(grads, "group", split_axis=0, concat_axis=0, tiled=True)


def solution(mesh):
    placed = (P(("space", "group"), None), P(("space", "group")), P(("space", "group"), None), P())
    return jax.shard_map(
        per_device,
        mesh=mesh,
        in_specs=placed,
        out_specs=P(("space", "group"), None),
        check_vma=False,
    )
```

time: 174 us -> 127 us (0.73)
  other arithmetic: 49.6 us -> 4.68 us
  starting transfers between devices: 51.2 us -> 17.4 us
  blocking collectives: 17.9 us -> 35.6 us
  Pallas kernels: 0 us -> 15.9 us
  local copies, waits for them, and re-layouts: 36 us -> 39.8 us
  matrix products: 9.29 us -> 5.98 us
  waiting for transfers between devices: 8.28 us -> 6.46 us
    scatter-add x3 -> x0, other arithmetic: 41 us -> none  [the longest x1 14.2 us: per_device(): jax.ops.segment_sum(cot_in.astype(jnp.float32), index, voxels + 1)[:voxels]]
    reshape x0 -> x4, local copies, waits for them, and re-layouts: none -> 25.5 us  [the longest x1 25.2 us: banded_weights(): return wide.astype(kernel.dtype).reshape(9, ZC, ZC)]
    all_to_all x0 -> x1, blocking collectives: none -> 19.5 us  [per_device(): lax.all_to_all(payload, 'group', split_axis=0, concat_axis=0, tiled=True)]
    gather x3 -> x0, local copies, waits for them, and re-layouts: 17.5 us -> none  [per_device(): grads = (table[index] / divisor[index][:, None]).astype(jnp.bfloat16)]
    all_to_all x3 -> x0, starting transfers between devices: 17.2 us -> none  [the longest x1 7.23 us: per_device(): lax.all_to_all(point_voxel, 'group', split_axis=0, concat_axis=0, tiled=T...]
    pallas_call x0 -> x3, Pallas kernels: none -> 15.9 us  [the longest x1 6.65 us: conv_pair(): pl.pallas_call(conv_kernel, out_shape=jax.ShapeDtypeStruct((ER, ZC), jnp....]
    conv_general_dilated x2 -> x0, matrix products: 9.29 us -> none  [convolve(): lax.conv_general_dilated(padded[None], weights, (1, 1, 1), 'VALID', dimen...]
    ppermute x4 -> x2, starting transfers between devices: 12.6 us -> 3.51 us  [extended(): before = lax.ppermute(last, axis, up)]
  transfers between devices with their start and end apart: 11 -> 4, of which waited for: 3 -> 2; matrix products, arithmetic and copies ran while one was open for 35% -> 30% of each run, Pallas kernels for 0% -> 0%
where the time goes in v2:
time: 127 us; the launch traced here: 126 us
  local copies, waits for them, and re-layouts  39.8 us (31%)
  blocking collectives  35.6 us (28%)
  starting transfers between devices  17.4 us (14%)
  Pallas kernels  15.9 us (13%)
  waiting for transfers between devices  6.46 us (5%)
  matrix products  5.98 us (5%)
  other arithmetic  4.68 us (4%)
    reshape x1, local copies, waits for them, and re-layouts, banded_weights(): return wide.astype(kernel.dtype).reshape(9, ZC, ZC)  25.2 us
    all_to_all x1, blocking collectives, per_device(): lax.all_to_all(payload, 'group', split_axis=0, concat_axis=0, tiled=True)  19.5 us
    all_to_all x1, blocking collectives, per_device(): lax.all_to_all(grads, 'group', split_axis=0, concat_axis=0, tiled=True)  16.2 us
    ppermute x2, starting transfers between devices, extended(): after = lax.ppermute(first, axis, down)  13.9 us
    convert_element_type x1, local copies, waits for them, and re-layouts, banded_weights(): return wide.astype(kernel.dtype).reshape(9, ZC, ZC)  6.9 us
    pallas_call x1, Pallas kernels, conv_pair(): pl.pallas_call(conv_kernel, out_shape=jax.ShapeDtypeStruct((ER, ZC), jnp....  6.65 us
    dot_general x1, matrix products, banded_weights(): jnp.einsum('dab,xydio->xyaibo', shift, kernel, preferred_element_type=jnp...  5.98 us
    ppermute x2, waiting for transfers between devices, extended(): before = lax.ppermute(last, axis, up)  5.9 us
  transfers between devices with their start and end apart: 4, of which 2 were waited for; matrix products, arithmetic and copies ran while one was open for 30% of the time, Pallas kernels for 0%

profile of v2, /device:TPU:6, one launch (start us, length us, event | category | flops | bytes accessed | tf_op | source)
XLA Modules:
  0.0 126.0 jit_solution(3424404662562855225)
XLA Ops:
  0.0 0.7 fusion.8
  0.7 0.9 copy.31
  1.7 0.9 copy.32
  2.6 0.1 pad_maximum_fusion.1
  2.7 0.1 copy.23
  2.7 19.5 %all_to_all.20 = bf16[8,256,66]{1,2,0:T(8,128)(2,1)S(1)} all-to-all(bf16[8,256,66]{1,2,0:T(8,128)(2,1)S(1)} %copy.23), channel_id=1, replica_groups=mesh['space'=96,'group'=8] {'group'}, dimensions={0} | all-to-all | bytes 540672 | tf_op jit(solution)/shard_map/all_to_all | solution.py:151
  22.2 0.3 copy.24
  22.5 0.0 copy-start
  22.5 2.7 %shift-right-arithmetic_select_fusion = (s32[2048,1]{1,0:T(8,128)}, s32[2048]{0:T(1024)}, s32[2048,1]{1,0:T(8,128)}) fusion(bf16[2048,66]{1,0:T(8,128)(2,1)S(1)} %bitcast.34), kind=kLoop, calls=%fused_computation.2 | loop fusion | flops 16384 | bytes 32768 | tf_op jit(solution)/shard_map/jit(_where)/select_n | solution.py:153
  25.2 0.0 copy-done
  25.2 5.4 %shard_map.46 = (f32[256,512]{1,0:T(8,128)}, f32[256,512]{1,0:T(8,128)}, f32[256,512]{1,0:T(8,128)}) custom-call(bf16[2048,66]{1,0:T(8,128)(2,1)} %bitcast.35, s32[1,2048]{1,0:T(1,128)} %bitcast.44, s32[2048,1]{1,0:T(8,128)} %get-tuple-element.17.z_ref), custom_call_target="tpu_custom_call" | custom-call | flops 1887436800 | bytes 1843200 | tf_op jit(solution)/shard_map/pallas_call | solution.py:67
  30.6 0.0 copy-start.2
  30.6 1.1 constant_dynamic-update-slice_fusion.1
  31.7 1.1 constant_dynamic-update-slice_fusion
  32.9 12.4 %collective-permute-start.1 = (f32[2,16,1024]{2,1,0:T(8,128)S(1)}, f32[2,16,1024]{2,1,0:T(8,128)S(1)}, u32[]{:S(2)}, u32[]{:S(2)}) collective-permute-start(f32[2,16,1024]{2,1,0:T(8,128)S(1)} %bitcast.43), channel_id=1, source_target_pairs={{8,0},{16,8},{24,16},{32,24},{40,32},{48,40},{56,48},{64,56},{72,6... | collective-permute-start | bytes 393224 | tf_op jit(solution)/shard_map/ppermute | solution.py:30
  45.3 1.9 %collective-permute-start = (f32[2,16,1024]{2,1,0:T(8,128)S(1)}, f32[2,16,1024]{2,1,0:T(8,128)S(1)}, u32[]{:S(2)}, u32[]{:S(2)}) collective-permute-start(f32[2,16,1024]{2,1,0:T(8,128)S(1)} %bitcast.42), channel_id=1, source_target_pairs={{0,8},{8,16},{16,24},{24,32},{32,40},{40,48},{48,56},{56,64},{64,7... | collective-permute-start | bytes 393224 | tf_op jit(solution)/shard_map/ppermute | solution.py:29
  47.2 0.6 collective-permute-done.1
  47.8 5.9 %collective-permute-done = f32[2,16,1024]{2,1,0:T(8,128)S(1)} collective-permute-done((f32[2,16,1024]{2,1,0:T(8,128)S(1)}, f32[2,16,1024]{2,1,0:T(8,128)S(1)}, u32[]{:S(2)}, u32[]{:S(2)}) %collective-permute-start) | collective-permute-done | bytes 131104 | tf_op jit(solution)/shard_map/ppermute | solution.py:29
  53.7 0.1 pad_maximum_fusion.4
  53.8 1.6 %collective-permute-start.2 = (f32[20,2,1024]{2,1,0:T(2,128)S(1)}, f32[20,2,1024]{2,1,0:T(2,128)S(1)}, u32[]{:S(2)}, u32[]{:S(2)}) collective-permute-start(f32[20,2,1024]{2,1,0:T(2,128)S(1)} %get-tuple-element.11), channel_id=1, source_target_pairs={{0,1},{1,2},{2,3},{3,4},{4,5},{5,6},{6,7},{8,9},{9,10},{10,11},{11... | collective-permute-start | bytes 491528 | tf_op jit(solution)/shard_map/ppermute | solution.py:29
  55.4 1.5 %collective-permute-start.3 = (f32[20,2,1024]{2,1,0:T(2,128)S(1)}, f32[20,2,1024]{2,1,0:T(2,128)S(1)}, u32[]{:S(2)}, u32[]{:S(2)}) collective-permute-start(f32[20,2,1024]{2,1,0:T(2,128)S(1)} %get-tuple-element.12), channel_id=1, source_target_pairs={{1,0},{2,1},{3,2},{4,3},{5,4},{6,5},{7,6},{9,8},{10,9},{11,10},{12... | collective-permute-start | bytes 491528 | tf_op jit(solution)/shard_map/ppermute | solution.py:30
  56.9 0.0 copy-done.2
  56.9 6.0 %convert_bitcast_fusion = bf16[3,3,16,32,16,32]{5,4,3,1,0,2:T(8,128)(2,1)S(1)} fusion(bf16[3,3,3,32,32]{4,3,2,1,0:T(8,128)(2,1)S(1)} %copy-done.2, s32[3,16]{1,0:T(4,128)S(1)} %add_add_fusion), kind=kOutput, calls=%fused_computation | convolution fusion | flops 16515840 | bytes 4774080 | tf_op jit(solution)/shard_map/dab,xydio->xyaibo/dot_general | solution.py:141
  62.9 6.9 %copy.26 = bf16[3,3,16,32,16,32]{5,4,3,2,1,0:T(8,128)(2,1)} copy(bf16[3,3,16,32,16,32]{5,4,3,1,0,2:T(8,128)(2,1)S(1)} %convert_bitcast_fusion) | data formatting | bytes 9437184 | tf_op jit(solution)/shard_map/convert_element_type | solution.py:142
  69.8 25.2 %reshape.97.w_ref = bf16[9,512,512]{2,1,0:T(8,128)(2,1)} reshape(bf16[3,3,16,32,16,32]{5,4,3,2,1,0:T(8,128)(2,1)} %copy.26) | data formatting | bytes 9437184 | tf_op jit(solution)/shard_map/reshape | solution.py:142
  95.0 0.0 collective-permute-done.2
  95.0 0.0 collective-permute-done.3
  95.0 0.3 pad_maximum_fusion
  95.3 0.1 slice.61
  95.4 0.1 slice.50
  95.5 0.1 reshape.96.g_ref
  95.5 0.1 reshape.95.m_ref
  95.6 6.7 %shard_map.47 = f32[400,512]{1,0:T(8,128)S(1)} custom-call(bf16[400,512]{1,0:T(8,128)(2,1)S(1)} %reshape.95.m_ref, f32[400,512]{1,0:T(8,128)S(1)} %reshape.96.g_ref, bf16[9,512,512]{2,1,0:T(8,128)(2,1)} %reshape.97.w_ref), custom_call_target="tpu_custom_call" | custom-call | flops 3774873600 | bytes 6766592 | tf_op jit(solution)/shard_map/pallas_call | solution.py:99
  102.3 0.0 copy-start.1
  102.3 0.1 reshape.98
  102.4 0.1 slice.51
  102.5 0.9 copy-done.1
  103.3 0.8 fusion.1.t_ref
  104.2 3.8 %shard_map.48 = bf16[2048,32]{1,0:T(8,128)(2,1)} custom-call(bf16[256,512]{1,0:T(8,128)(2,1)} %fusion.1.t_ref, s32[2048,1]{1,0:T(8,128)} %get-tuple-element.15.xy_ref, s32[2048,1]{1,0:T(8,128)} %get-tuple-element.17.z_ref), custom_call_target="tpu_custom_call" | custom-call | flops 603979776 | bytes 393216 | tf_op jit(solution)/shard_map/pallas_call | solution.py:128
  108.0 1.2 copy.27
  109.2 16.2 %all_to_all.21 = bf16[8,256,32]{1,2,0:T(8,128)(2,1)S(1)} all-to-all(bf16[8,256,32]{1,2,0:T(8,128)(2,1)S(1)} %copy.27), channel_id=1, replica_groups=mesh['space'=96,'group'=8] {'group'}, dimensions={0} | all-to-all | bytes 262144 | tf_op jit(solution)/shard_map/all_to_all | solution.py:164
  125.4 0.7 copy.30
  (4 shorter events, 0.0 us)
Async XLA Ops:
  22.5 2.7 %copy-start = (bf16[8,256,66]{2,1,0:T(8,128)(2,1)}, bf16[8,256,66]{2,1,0:T(8,128)(2,1)S(1)}, u32[]{:S(2)}) copy-start(bf16[8,256,66]{2,1,0:T(8,128)(2,1)S(1)} %copy.24) | copy-start | bytes 811012
  30.6 26.3 %copy-start.2 = (bf16[3,3,3,32,32]{4,3,2,1,0:T(8,128)(2,1)S(1)}, bf16[3,3,3,32,32]{4,3,2,1,0:T(8,128)(2,1)}, u32[]{:S(2)}) copy-start(bf16[3,3,3,32,32]{4,3,2,1,0:T(8,128)(2,1)} %param.7) | copy-start | bytes 165892
  32.9 14.9 %collective-permute-start.1 = (f32[2,16,1024]{2,1,0:T(8,128)S(1)}, f32[2,16,1024]{2,1,0:T(8,128)S(1)}, u32[]{:S(2)}, u32[]{:S(2)}) collective-permute-start(f32[2,16,1024]{2,1,0:T(8,128)S(1)} %bitcast.43), channel_id=1, source_target_pairs={{8,0},{16,8},{24,16},{32,24},{40,32},{48,40},{56,48},{64,56},{72,6... | collective-permute-start | bytes 393224 | tf_op jit(solution)/shard_map/ppermute | solution.py:30
  45.3 8.4 %collective-permute-start = (f32[2,16,1024]{2,1,0:T(8,128)S(1)}, f32[2,16,1024]{2,1,0:T(8,128)S(1)}, u32[]{:S(2)}, u32[]{:S(2)}) collective-permute-start(f32[2,16,1024]{2,1,0:T(8,128)S(1)} %bitcast.42), channel_id=1, source_target_pairs={{0,8},{8,16},{16,24},{24,32},{32,40},{40,48},{48,56},{56,64},{64,7... | collective-permute-start | bytes 393224 | tf_op jit(solution)/shard_map/ppermute | solution.py:29
  53.8 41.2 %collective-permute-start.2 = (f32[20,2,1024]{2,1,0:T(2,128)S(1)}, f32[20,2,1024]{2,1,0:T(2,128)S(1)}, u32[]{:S(2)}, u32[]{:S(2)}) collective-permute-start(f32[20,2,1024]{2,1,0:T(2,128)S(1)} %get-tuple-element.11), channel_id=1, source_target_pairs={{0,1},{1,2},{2,3},{3,4},{4,5},{5,6},{6,7},{8,9},{9,10},{10,11},{11... | collective-permute-start | bytes 491528 | tf_op jit(solution)/shard_map/ppermute | solution.py:29
  55.4 39.6 %collective-permute-start.3 = (f32[20,2,1024]{2,1,0:T(2,128)S(1)}, f32[20,2,1024]{2,1,0:T(2,128)S(1)}, u32[]{:S(2)}, u32[]{:S(2)}) collective-permute-start(f32[20,2,1024]{2,1,0:T(2,128)S(1)} %get-tuple-element.12), channel_id=1, source_target_pairs={{1,0},{2,1},{3,2},{4,3},{5,4},{6,5},{7,6},{9,8},{10,9},{11,10},{12... | collective-permute-start | bytes 491528 | tf_op jit(solution)/shard_map/ppermute | solution.py:30
  102.3 1.0 copy-start.1

commit v3 on v2

--- a/solution.py
+++ b/solution.py
@@ -11,7 +11,6 @@
 C = 32
 XY = XD * YD
 ZC = ZB * C
-HALF = 64
 PW = 2 * C + 2
 TK = 512
 EX = XD + 4
@@ -135,23 +134,45 @@
     )(table, xy_col, z_col)
 
 
+def band_kernel(w_ref, wb_ref):
+    rr = lax.broadcasted_iota(jnp.int32, (ZC, C), 0)
+    rc = lax.broadcasted_iota(jnp.int32, (ZC, C), 1)
+    rep_rows = (jnp.bitwise_and(rr, C - 1) == rc).astype(jnp.bfloat16)
+    lr = lax.broadcasted_iota(jnp.int32, (C, ZC), 0)
+    lc = lax.broadcasted_iota(jnp.int32, (C, ZC), 1)
+    rep_lanes = (lr == jnp.bitwise_and(lc, C - 1)).astype(jnp.bfloat16)
+    diff = (lax.broadcasted_iota(jnp.int32, (ZC, ZC), 0) >> 5) - (lax.broadcasted_iota(jnp.int32, (ZC, ZC), 1) >> 5)
+    acc = jnp.zeros((ZC, ZC), jnp.float32)
+    for dz in range(3):
+        wide = jnp.dot(w_ref[dz], rep_lanes, preferred_element_type=jnp.float32).astype(jnp.bfloat16)
+        tiled = jnp.dot(rep_rows, wide, preferred_element_type=jnp.float32)
+        acc = jnp.where(diff == dz - 1, tiled, acc)
+    wb_ref[...] = acc.astype(wb_ref.dtype)
+
+
 def banded_weights(kernel):
-    zi = jnp.arange(ZB)
-    shift = (zi[None, :, None] == zi[None, None, :] + jnp.arange(3)[:, None, None] - 1).astype(kernel.dtype)
-    wide = jnp.einsum("dab,xydio->xyaibo", shift, kernel, preferred_element_type=jnp.float32)
-    return wide.astype(kernel.dtype).reshape(9, ZC, ZC)
+    taps = kernel.reshape(27, C, C)
+    return pl.pallas_call(
+        band_kernel,
+        out_shape=jax.ShapeDtypeStruct((9, ZC, ZC), kernel.dtype),
+        grid=(9,),
+        in_specs=[pl.BlockSpec((3, C, C), lambda t: (t, 0, 0))],
+        out_specs=pl.BlockSpec((None, ZC, ZC), lambda t: (t, 0, 0)),
+        cost_estimate=pl.CostEstimate(
+            flops=9 * 3 * 2 * 2 * ZC * C * ZC, transcendentals=0, bytes_accessed=9 * ZC * ZC * 2
+        ),
+    )(taps)
 
 
 def per_device(point_feats, point_voxel, cotangent, kernel):
     npts = point_feats.shape[0]
     live = point_voxel >= 0
-    hi = jnp.where(live, point_voxel // HALF, -1).astype(jnp.bfloat16)
-    lo = jnp.where(live, point_voxel % HALF, 0).astype(jnp.bfloat16)
-    payload = jnp.concatenate([point_feats, cotangent, hi[:, None], lo[:, None]], axis=1)
+    xy_send = jnp.where(live, point_voxel >> 4, -1).astype(jnp.bfloat16)
+    z_send = jnp.bitwise_and(point_voxel, ZB - 1).astype(jnp.bfloat16)
+    payload = jnp.concatenate([point_feats, cotangent, xy_send[:, None], z_send[:, None]], axis=1)
     got = lax.all_to_all(payload, "group", split_axis=0, concat_axis=0, tiled=True)
-    index = got[:, 2 * C].astype(jnp.int32) * HALF + got[:, 2 * C + 1].astype(jnp.int32)
-    xy = jnp.where(index >= 0, index >> 4, -1)
-    z = jnp.bitwise_and(index, ZB - 1)
+    xy = got[:, 2 * C].astype(jnp.int32)
+    z = got[:, 2 * C + 1].astype(jnp.int32)
     mean, gy, divisor = scatter_sums(got, xy.reshape(1, npts), z.reshape(npts, 1))
     field = jnp.concatenate([mean, gy], axis=1).reshape(XD, YD, 2 * ZC)
     wide = extended(field, (("space", 0), ("group", 1)), 2)

time: 127 us -> 99.1 us (0.78)
  local copies, waits for them, and re-layouts: 39.8 us -> 7.62 us
  Pallas kernels: 15.9 us -> 26.4 us
  matrix products: 5.98 us -> 0 us
    reshape x1 -> x0, local copies, waits for them, and re-layouts: 25.2 us -> none  [banded_weights(): return wide.astype(kernel.dtype).reshape(9, ZC, ZC)]
    pallas_call x0 -> x1, Pallas kernels: none -> 10.5 us  [banded_weights(): pl.pallas_call(band_kernel, out_shape=jax.ShapeDtypeStruct((9, ZC, ZC), k...]
    convert_element_type x1 -> x0, local copies, waits for them, and re-layouts: 6.9 us -> none  [banded_weights(): return wide.astype(kernel.dtype).reshape(9, ZC, ZC)]
    dot_general x1 -> x0, matrix products: 5.98 us -> none  [banded_weights(): jnp.einsum('dab,xydio->xyaibo', shift, kernel, preferred_element_type=jnp...]
    convert_element_type x1 -> x3, other arithmetic: 0.71 us -> 3.61 us  [the longest x2 2.91 us: per_device(): xy = got[:, 2 * C].astype(jnp.int32)]
    select_n x1 -> x0, other arithmetic: 2.67 us -> none  [per_device(): xy = jnp.where(index >= 0, index >> 4, -1)]
    unnamed x9 -> x7, local copies, waits for them, and re-layouts: 3.85 us -> 3.81 us
  transfers between devices with their start and end apart: 4 -> 4, of which waited for: 2 -> 2; matrix products, arithmetic and copies ran while one was open for 30% -> 0% of each run, Pallas kernels for 0% -> 11%
where the time goes in v3:
time: 99.1 us; the launch traced here: 98.5 us
  blocking collectives  35.6 us (36%)
  Pallas kernels  26.4 us (27%)
  starting transfers between devices  17.2 us (17%)
  local copies, waits for them, and re-layouts  7.62 us (8%)
  waiting for transfers between devices  6.47 us (7%)
  other arithmetic  4.91 us (5%)
    all_to_all x1, blocking collectives, per_device(): lax.all_to_all(payload, 'group', split_axis=0, concat_axis=0, tiled=True)  19.5 us
    all_to_all x1, blocking collectives, per_device(): lax.all_to_all(grads, 'group', split_axis=0, concat_axis=0, tiled=True)  16.2 us
    ppermute x2, starting transfers between devices, extended(): after = lax.ppermute(first, axis, down)  13.7 us
    pallas_call x1, Pallas kernels, banded_weights(): pl.pallas_call(band_kernel, out_shape=jax.ShapeDtypeStruct((9, ZC, ZC), k...  10.5 us
    pallas_call x1, Pallas kernels, conv_pair(): pl.pallas_call(conv_kernel, out_shape=jax.ShapeDtypeStruct((ER, ZC), jnp....  6.65 us
    ppermute x2, waiting for transfers between devices, extended(): before = lax.ppermute(last, axis, up)  5.9 us
    pallas_call x1, Pallas kernels, scatter_sums(): pl.pallas_call(scatter_kernel, out_shape=(field, field, field), cost_esti...  5.46 us
    pallas_call x1, Pallas kernels, gather_rows(): pl.pallas_call(gather_kernel, out_shape=jax.ShapeDtypeStruct((npts, C), j...  3.83 us
  transfers between devices with their start and end apart: 4, of which 2 were waited for; matrix products, arithmetic and copies ran while one was open for 0% of the time, Pallas kernels for 11%

profile of v3, /device:TPU:6, one launch (start us, length us, event | category | flops | bytes accessed | tf_op | source)
XLA Modules:
  0.0 98.5 jit_solution(14455359068739602951)
XLA Ops:
  0.0 0.7 select_convert_fusion
  0.7 0.9 copy.22
  1.7 0.9 copy.23
  2.6 0.1 pad_maximum_fusion.1
  2.7 0.1 copy.17
  2.7 19.5 %all_to_all.20 = bf16[8,256,66]{1,2,0:T(8,128)(2,1)S(1)} all-to-all(bf16[8,256,66]{1,2,0:T(8,128)(2,1)S(1)} %copy.17), channel_id=1, replica_groups=mesh['space'=96,'group'=8] {'group'}, dimensions={0} | all-to-all | bytes 540672 | tf_op jit(solution)/shard_map/all_to_all | solution.py:173
  22.2 0.3 copy.18
  22.5 0.0 copy-start
  22.5 1.1 %fusion.1 = s32[2048]{0:T(1024)} fusion(bf16[2048,66]{1,0:T(8,128)(2,1)S(1)} %bitcast.21), kind=kLoop, calls=%fused_computation.7 | loop fusion | flops 2048 | bytes 12288 | tf_op jit(solution)/shard_map/convert_element_type | solution.py:174
  23.6 1.8 %slice_convert_fusion.2 = (s32[2048,1]{1,0:T(8,128)}, s32[2048,1]{1,0:T(8,128)}) fusion(bf16[2048,66]{1,0:T(8,128)(2,1)S(1)} %bitcast.22), kind=kLoop, calls=%fused_computation.3 | loop fusion | flops 4096 | bytes 24576 | tf_op jit(solution)/shard_map/convert_element_type | solution.py:174
  25.4 0.0 copy-done
  25.4 5.5 %shard_map.46 = (f32[256,512]{1,0:T(8,128)}, f32[256,512]{1,0:T(8,128)}, f32[256,512]{1,0:T(8,128)}) custom-call(bf16[2048,66]{1,0:T(8,128)(2,1)} %bitcast.23, s32[1,2048]{1,0:T(1,128)} %bitcast.35, s32[2048,1]{1,0:T(8,128)} %get-tuple-element.16.z_ref), custom_call_target="tpu_custom_call" | custom-call | flops 1887436800 | bytes 1843200 | tf_op jit(solution)/shard_map/pallas_call | solution.py:66
  30.9 1.1 %constant_dynamic-update-slice_fusion.1 = f32[256,1024]{1,0:T(8,128)S(1)} fusion(f32[256,512]{1,0:T(8,128)} %get-tuple-element.8), kind=kLoop, calls=%fused_computation.14 | loop fusion | bytes 1048576
  32.0 1.1 %constant_dynamic-update-slice_fusion = f32[256,1024]{1,0:T(8,128)S(1)} fusion(f32[256,1024]{1,0:T(8,128)S(1)} %constant_dynamic-update-slice_fusion.1, f32[256,512]{1,0:T(8,128)} %get-tuple-element.9), kind=kLoop, calls=%fused_computation.13 | loop fusion | bytes 1048576 | tf_op jit(solution)/shard_map/concatenate | solution.py:177
  33.1 12.4 %collective-permute-start.1 = (f32[2,16,1024]{2,1,0:T(8,128)S(1)}, f32[2,16,1024]{2,1,0:T(8,128)S(1)}, u32[]{:S(2)}, u32[]{:S(2)}) collective-permute-start(f32[2,16,1024]{2,1,0:T(8,128)S(1)} %bitcast.34), channel_id=1, source_target_pairs={{8,0},{16,8},{24,16},{32,24},{40,32},{48,40},{56,48},{64,56},{72,6... | collective-permute-start | bytes 393224 | tf_op jit(solution)/shard_map/ppermute | solution.py:29
  45.5 1.9 %collective-permute-start = (f32[2,16,1024]{2,1,0:T(8,128)S(1)}, f32[2,16,1024]{2,1,0:T(8,128)S(1)}, u32[]{:S(2)}, u32[]{:S(2)}) collective-permute-start(f32[2,16,1024]{2,1,0:T(8,128)S(1)} %bitcast.33), channel_id=1, source_target_pairs={{0,8},{8,16},{16,24},{24,32},{32,40},{40,48},{48,56},{56,64},{64,7... | collective-permute-start | bytes 393224 | tf_op jit(solution)/shard_map/ppermute | solution.py:28
  47.4 0.6 collective-permute-done.1
  48.0 5.9 %collective-permute-done = f32[2,16,1024]{2,1,0:T(8,128)S(1)} collective-permute-done((f32[2,16,1024]{2,1,0:T(8,128)S(1)}, f32[2,16,1024]{2,1,0:T(8,128)S(1)}, u32[]{:S(2)}, u32[]{:S(2)}) %collective-permute-start) | collective-permute-done | bytes 131104 | tf_op jit(solution)/shard_map/ppermute | solution.py:28
  53.9 0.1 pad_maximum_fusion.4
  54.0 1.6 %collective-permute-start.2 = (f32[20,2,1024]{2,1,0:T(2,128)S(1)}, f32[20,2,1024]{2,1,0:T(2,128)S(1)}, u32[]{:S(2)}, u32[]{:S(2)}) collective-permute-start(f32[20,2,1024]{2,1,0:T(2,128)S(1)} %get-tuple-element.11), channel_id=1, source_target_pairs={{0,1},{1,2},{2,3},{3,4},{4,5},{5,6},{6,7},{8,9},{9,10},{10,11},{11... | collective-permute-start | bytes 491528 | tf_op jit(solution)/shard_map/ppermute | solution.py:28
  55.6 1.3 %collective-permute-start.3 = (f32[20,2,1024]{2,1,0:T(2,128)S(1)}, f32[20,2,1024]{2,1,0:T(2,128)S(1)}, u32[]{:S(2)}, u32[]{:S(2)}) collective-permute-start(f32[20,2,1024]{2,1,0:T(2,128)S(1)} %get-tuple-element.12), channel_id=1, source_target_pairs={{1,0},{2,1},{3,2},{4,3},{5,4},{6,5},{7,6},{9,8},{10,9},{11,10},{12... | collective-permute-start | bytes 491528 | tf_op jit(solution)/shard_map/ppermute | solution.py:29
  56.9 10.5 %shard_map.47.w_ref = bf16[9,512,512]{2,1,0:T(8,128)(2,1)} custom-call(bf16[27,32,32]{2,1,0:T(8,128)(2,1)} %bitcast.30), custom_call_target="tpu_custom_call" | custom-call | flops 905969664 | bytes 4718592 | tf_op jit(solution)/shard_map/pallas_call | solution.py:155
  67.4 0.0 collective-permute-done.2
  67.4 0.0 collective-permute-done.3
  67.4 0.3 pad_maximum_fusion
  67.7 0.1 slice.57
  67.8 0.1 slice.50
  67.9 0.1 reshape.48.g_ref
  68.0 0.1 reshape.47.m_ref
  68.1 6.7 %shard_map.48 = f32[400,512]{1,0:T(8,128)S(1)} custom-call(bf16[400,512]{1,0:T(8,128)(2,1)S(1)} %reshape.47.m_ref, f32[400,512]{1,0:T(8,128)S(1)} %reshape.48.g_ref, bf16[9,512,512]{2,1,0:T(8,128)(2,1)} %shard_map.47.w_ref), custom_call_target="tpu_custom_call" | custom-call | flops 3774873600 | bytes 6766592 | tf_op jit(solution)/shard_map/pallas_call | solution.py:98
  74.7 0.0 copy-start.1
  74.7 0.1 reshape.50
  74.8 0.1 slice.51
  74.9 0.9 copy-done.1
  75.8 0.8 fusion.t_ref
  76.6 3.8 %shard_map.49 = bf16[2048,32]{1,0:T(8,128)(2,1)} custom-call(bf16[256,512]{1,0:T(8,128)(2,1)} %fusion.t_ref, s32[2048,1]{1,0:T(8,128)} %get-tuple-element.15.xy_ref, s32[2048,1]{1,0:T(8,128)} %get-tuple-element.16.z_ref), custom_call_target="tpu_custom_call" | custom-call | flops 603979776 | bytes 393216 | tf_op jit(solution)/shard_map/pallas_call | solution.py:127
  80.4 1.2 %copy.19 = bf16[8,256,32]{1,2,0:T(8,128)(2,1)S(1)} copy(bf16[8,256,32]{2,1,0:T(8,128)(2,1)} %bitcast.26) | data formatting | bytes 262144 | tf_op jit(solution)/shard_map/all_to_all | solution.py:185
  81.6 16.2 %all_to_all.21 = bf16[8,256,32]{1,2,0:T(8,128)(2,1)S(1)} all-to-all(bf16[8,256,32]{1,2,0:T(8,128)(2,1)S(1)} %copy.19), channel_id=1, replica_groups=mesh['space'=96,'group'=8] {'group'}, dimensions={0} | all-to-all | bytes 262144 | tf_op jit(solution)/shard_map/all_to_all | solution.py:185
  97.8 0.7 copy.21
  (3 shorter events, 0.0 us)
Async XLA Ops:
  22.5 2.9 %copy-start = (bf16[8,256,66]{2,1,0:T(8,128)(2,1)}, bf16[8,256,66]{2,1,0:T(8,128)(2,1)S(1)}, u32[]{:S(2)}) copy-start(bf16[8,256,66]{2,1,0:T(8,128)(2,1)S(1)} %copy.18) | copy-start | bytes 811012
  33.1 14.9 %collective-permute-start.1 = (f32[2,16,1024]{2,1,0:T(8,128)S(1)}, f32[2,16,1024]{2,1,0:T(8,128)S(1)}, u32[]{:S(2)}, u32[]{:S(2)}) collective-permute-start(f32[2,16,1024]{2,1,0:T(8,128)S(1)} %bitcast.34), channel_id=1, source_target_pairs={{8,0},{16,8},{24,16},{32,24},{40,32},{48,40},{56,48},{64,56},{72,6... | collective-permute-start | bytes 393224 | tf_op jit(solution)/shard_map/ppermute | solution.py:29
  45.5 8.4 %collective-permute-start = (f32[2,16,1024]{2,1,0:T(8,128)S(1)}, f32[2,16,1024]{2,1,0:T(8,128)S(1)}, u32[]{:S(2)}, u32[]{:S(2)}) collective-permute-start(f32[2,16,1024]{2,1,0:T(8,128)S(1)} %bitcast.33), channel_id=1, source_target_pairs={{0,8},{8,16},{16,24},{24,32},{32,40},{40,48},{48,56},{56,64},{64,7... | collective-permute-start | bytes 393224 | tf_op jit(solution)/shard_map/ppermute | solution.py:28
  54.0 13.4 %collective-permute-start.2 = (f32[20,2,1024]{2,1,0:T(2,128)S(1)}, f32[20,2,1024]{2,1,0:T(2,128)S(1)}, u32[]{:S(2)}, u32[]{:S(2)}) collective-permute-start(f32[20,2,1024]{2,1,0:T(2,128)S(1)} %get-tuple-element.11), channel_id=1, source_target_pairs={{0,1},{1,2},{2,3},{3,4},{4,5},{5,6},{6,7},{8,9},{9,10},{10,11},{11... | collective-permute-start | bytes 491528 | tf_op jit(solution)/shard_map/ppermute | solution.py:28
  55.6 11.8 %collective-permute-start.3 = (f32[20,2,1024]{2,1,0:T(2,128)S(1)}, f32[20,2,1024]{2,1,0:T(2,128)S(1)}, u32[]{:S(2)}, u32[]{:S(2)}) collective-permute-start(f32[20,2,1024]{2,1,0:T(2,128)S(1)} %get-tuple-element.12), channel_id=1, source_target_pairs={{1,0},{2,1},{3,2},{4,3},{5,4},{6,5},{7,6},{9,8},{10,9},{11,10},{12... | collective-permute-start | bytes 491528 | tf_op jit(solution)/shard_map/ppermute | solution.py:29
  74.7 1.0 %copy-start.1 = (f32[256,512]{1,0:T(8,128)S(1)}, f32[256,512]{1,0:T(8,128)}, u32[]{:S(2)}) copy-start(f32[256,512]{1,0:T(8,128)} %get-tuple-element.10) | copy-start | bytes 1572868

commit v4 on v3

--- a/solution.py
+++ b/solution.py
@@ -135,19 +135,16 @@
 
 
 def band_kernel(w_ref, wb_ref):
-    rr = lax.broadcasted_iota(jnp.int32, (ZC, C), 0)
-    rc = lax.broadcasted_iota(jnp.int32, (ZC, C), 1)
-    rep_rows = (jnp.bitwise_and(rr, C - 1) == rc).astype(jnp.bfloat16)
     lr = lax.broadcasted_iota(jnp.int32, (C, ZC), 0)
     lc = lax.broadcasted_iota(jnp.int32, (C, ZC), 1)
     rep_lanes = (lr == jnp.bitwise_and(lc, C - 1)).astype(jnp.bfloat16)
-    diff = (lax.broadcasted_iota(jnp.int32, (ZC, ZC), 0) >> 5) - (lax.broadcasted_iota(jnp.int32, (ZC, ZC), 1) >> 5)
-    acc = jnp.zeros((ZC, ZC), jnp.float32)
-    for dz in range(3):
-        wide = jnp.dot(w_ref[dz], rep_lanes, preferred_element_type=jnp.float32).astype(jnp.bfloat16)
-        tiled = jnp.dot(rep_rows, wide, preferred_element_type=jnp.float32)
-        acc = jnp.where(diff == dz - 1, tiled, acc)
-    wb_ref[...] = acc.astype(wb_ref.dtype)
+    lane_z = lc >> 5
+    wides = [jnp.dot(w_ref[dz], rep_lanes, preferred_element_type=jnp.float32) for dz in range(3)]
+    for zp in range(ZB):
+        block = jnp.zeros((C, ZC), jnp.float32)
+        for dz in range(3):
+            block = jnp.where(lane_z == zp + 1 - dz, wides[dz], block)
+        wb_ref[pl.ds(zp * C, C), :] = block.astype(wb_ref.dtype)
 
 
 def banded_weights(kernel):

time: 99.1 us -> 96 us (0.969)
  Pallas kernels: 26.4 us -> 22.8 us
    pallas_call x1, Pallas kernels: 10.5 us -> 6.9 us  [banded_weights(): pl.pallas_call(band_kernel, out_shape=jax.ShapeDtypeStruct((9, ZC, ZC), k...]
  transfers between devices with their start and end apart: 4 -> 4, of which waited for: 2 -> 2; matrix products, arithmetic and copies ran while one was open for 0% -> 0% of each run, Pallas kernels for 11% -> 7%
where the time goes in v4:
time: 96 us; the launch traced here: 94.9 us
  blocking collectives  35.6 us (37%)
  Pallas kernels  22.8 us (24%)
  starting transfers between devices  17.2 us (18%)
  local copies, waits for them, and re-layouts  7.62 us (8%)
  waiting for transfers between devices  6.47 us (7%)
  other arithmetic  4.91 us (5%)
    all_to_all x1, blocking collectives, per_device(): lax.all_to_all(payload, 'group', split_axis=0, concat_axis=0, tiled=True)  19.5 us
    all_to_all x1, blocking collectives, per_device(): lax.all_to_all(grads, 'group', split_axis=0, concat_axis=0, tiled=True)  16.2 us
    ppermute x2, starting transfers between devices, extended(): after = lax.ppermute(first, axis, down)  13.7 us
    pallas_call x1, Pallas kernels, banded_weights(): pl.pallas_call(band_kernel, out_shape=jax.ShapeDtypeStruct((9, ZC, ZC), k...  6.9 us
    pallas_call x1, Pallas kernels, conv_pair(): pl.pallas_call(conv_kernel, out_shape=jax.ShapeDtypeStruct((ER, ZC), jnp....  6.65 us
    ppermute x2, waiting for transfers between devices, extended(): before = lax.ppermute(last, axis, up)  5.9 us
    pallas_call x1, Pallas kernels, scatter_sums(): pl.pallas_call(scatter_kernel, out_shape=(field, field, field), cost_esti...  5.46 us
    pallas_call x1, Pallas kernels, gather_rows(): pl.pallas_call(gather_kernel, out_shape=jax.ShapeDtypeStruct((npts, C), j...  3.83 us
  transfers between devices with their start and end apart: 4, of which 2 were waited for; matrix products, arithmetic and copies ran while one was open for 0% of the time, Pallas kernels for 7%

profile of v4, /device:TPU:6, one launch (start us, length us, event | category | flops | bytes accessed | tf_op | source)
XLA Modules:
  0.0 94.9 jit_solution(7977932426559819123)
XLA Ops:
  0.0 0.7 select_convert_fusion
  0.7 0.9 copy.22
  1.7 0.9 copy.23
  2.6 0.1 pad_maximum_fusion.1
  2.7 0.1 copy.17
  2.7 19.5 %all_to_all.20 = bf16[8,256,66]{1,2,0:T(8,128)(2,1)S(1)} all-to-all(bf16[8,256,66]{1,2,0:T(8,128)(2,1)S(1)} %copy.17), channel_id=1, replica_groups=mesh['space'=96,'group'=8] {'group'}, dimensions={0} | all-to-all | bytes 540672 | tf_op jit(solution)/shard_map/all_to_all | solution.py:170
  22.2 0.3 copy.18
  22.5 0.0 copy-start
  22.5 1.1 %fusion.1 = s32[2048]{0:T(1024)} fusion(bf16[2048,66]{1,0:T(8,128)(2,1)S(1)} %bitcast.21), kind=kLoop, calls=%fused_computation.7 | loop fusion | flops 2048 | bytes 12288 | tf_op jit(solution)/shard_map/convert_element_type | solution.py:171
  23.6 1.8 %slice_convert_fusion.2 = (s32[2048,1]{1,0:T(8,128)}, s32[2048,1]{1,0:T(8,128)}) fusion(bf16[2048,66]{1,0:T(8,128)(2,1)S(1)} %bitcast.22), kind=kLoop, calls=%fused_computation.3 | loop fusion | flops 4096 | bytes 24576 | tf_op jit(solution)/shard_map/convert_element_type | solution.py:171
  25.4 0.0 copy-done
  25.4 5.5 %shard_map.46 = (f32[256,512]{1,0:T(8,128)}, f32[256,512]{1,0:T(8,128)}, f32[256,512]{1,0:T(8,128)}) custom-call(bf16[2048,66]{1,0:T(8,128)(2,1)} %bitcast.23, s32[1,2048]{1,0:T(1,128)} %bitcast.35, s32[2048,1]{1,0:T(8,128)} %get-tuple-element.16.z_ref), custom_call_target="tpu_custom_call" | custom-call | flops 1887436800 | bytes 1843200 | tf_op jit(solution)/shard_map/pallas_call | solution.py:66
  30.9 1.1 %constant_dynamic-update-slice_fusion.1 = f32[256,1024]{1,0:T(8,128)S(1)} fusion(f32[256,512]{1,0:T(8,128)} %get-tuple-element.8), kind=kLoop, calls=%fused_computation.14 | loop fusion | bytes 1048576
  32.0 1.1 %constant_dynamic-update-slice_fusion = f32[256,1024]{1,0:T(8,128)S(1)} fusion(f32[256,1024]{1,0:T(8,128)S(1)} %constant_dynamic-update-slice_fusion.1, f32[256,512]{1,0:T(8,128)} %get-tuple-element.9), kind=kLoop, calls=%fused_computation.13 | loop fusion | bytes 1048576 | tf_op jit(solution)/shard_map/concatenate | solution.py:174
  33.1 12.4 %collective-permute-start.1 = (f32[2,16,1024]{2,1,0:T(8,128)S(1)}, f32[2,16,1024]{2,1,0:T(8,128)S(1)}, u32[]{:S(2)}, u32[]{:S(2)}) collective-permute-start(f32[2,16,1024]{2,1,0:T(8,128)S(1)} %bitcast.34), channel_id=1, source_target_pairs={{8,0},{16,8},{24,16},{32,24},{40,32},{48,40},{56,48},{64,56},{72,6... | collective-permute-start | bytes 393224 | tf_op jit(solution)/shard_map/ppermute | solution.py:29
  45.5 1.9 %collective-permute-start = (f32[2,16,1024]{2,1,0:T(8,128)S(1)}, f32[2,16,1024]{2,1,0:T(8,128)S(1)}, u32[]{:S(2)}, u32[]{:S(2)}) collective-permute-start(f32[2,16,1024]{2,1,0:T(8,128)S(1)} %bitcast.33), channel_id=1, source_target_pairs={{0,8},{8,16},{16,24},{24,32},{32,40},{40,48},{48,56},{56,64},{64,7... | collective-permute-start | bytes 393224 | tf_op jit(solution)/shard_map/ppermute | solution.py:28
  47.4 0.6 collective-permute-done.1
  48.0 5.9 %collective-permute-done = f32[2,16,1024]{2,1,0:T(8,128)S(1)} collective-permute-done((f32[2,16,1024]{2,1,0:T(8,128)S(1)}, f32[2,16,1024]{2,1,0:T(8,128)S(1)}, u32[]{:S(2)}, u32[]{:S(2)}) %collective-permute-start) | collective-permute-done | bytes 131104 | tf_op jit(solution)/shard_map/ppermute | solution.py:28
  53.9 0.1 pad_maximum_fusion.4
  54.0 1.6 %collective-permute-start.2 = (f32[20,2,1024]{2,1,0:T(2,128)S(1)}, f32[20,2,1024]{2,1,0:T(2,128)S(1)}, u32[]{:S(2)}, u32[]{:S(2)}) collective-permute-start(f32[20,2,1024]{2,1,0:T(2,128)S(1)} %get-tuple-element.11), channel_id=1, source_target_pairs={{0,1},{1,2},{2,3},{3,4},{4,5},{5,6},{6,7},{8,9},{9,10},{10,11},{11... | collective-permute-start | bytes 491528 | tf_op jit(solution)/shard_map/ppermute | solution.py:28
  55.6 1.3 %collective-permute-start.3 = (f32[20,2,1024]{2,1,0:T(2,128)S(1)}, f32[20,2,1024]{2,1,0:T(2,128)S(1)}, u32[]{:S(2)}, u32[]{:S(2)}) collective-permute-start(f32[20,2,1024]{2,1,0:T(2,128)S(1)} %get-tuple-element.12), channel_id=1, source_target_pairs={{1,0},{2,1},{3,2},{4,3},{5,4},{6,5},{7,6},{9,8},{10,9},{11,10},{12... | collective-permute-start | bytes 491528 | tf_op jit(solution)/shard_map/ppermute | solution.py:29
  56.9 6.9 %shard_map.47.w_ref = bf16[9,512,512]{2,1,0:T(8,128)(2,1)} custom-call(bf16[27,32,32]{2,1,0:T(8,128)(2,1)} %bitcast.30), custom_call_target="tpu_custom_call" | custom-call | flops 905969664 | bytes 4718592 | tf_op jit(solution)/shard_map/pallas_call | solution.py:152
  63.8 0.0 collective-permute-done.2
  63.8 0.0 collective-permute-done.3
  63.8 0.3 pad_maximum_fusion
  64.1 0.1 slice.57
  64.2 0.1 slice.50
  64.3 0.1 reshape.48.g_ref
  64.4 0.1 reshape.47.m_ref
  64.5 6.7 %shard_map.48 = f32[400,512]{1,0:T(8,128)S(1)} custom-call(bf16[400,512]{1,0:T(8,128)(2,1)S(1)} %reshape.47.m_ref, f32[400,512]{1,0:T(8,128)S(1)} %reshape.48.g_ref, bf16[9,512,512]{2,1,0:T(8,128)(2,1)} %shard_map.47.w_ref), custom_call_target="tpu_custom_call" | custom-call | flops 3774873600 | bytes 6766592 | tf_op jit(solution)/shard_map/pallas_call | solution.py:98
  71.1 0.0 copy-start.1
  71.1 0.1 reshape.50
  71.2 0.1 slice.51
  71.3 0.9 copy-done.1
  72.2 0.8 fusion.t_ref
  73.0 3.8 %shard_map.49 = bf16[2048,32]{1,0:T(8,128)(2,1)} custom-call(bf16[256,512]{1,0:T(8,128)(2,1)} %fusion.t_ref, s32[2048,1]{1,0:T(8,128)} %get-tuple-element.15.xy_ref, s32[2048,1]{1,0:T(8,128)} %get-tuple-element.16.z_ref), custom_call_target="tpu_custom_call" | custom-call | flops 603979776 | bytes 393216 | tf_op jit(solution)/shard_map/pallas_call | solution.py:127
  76.8 1.2 %copy.19 = bf16[8,256,32]{1,2,0:T(8,128)(2,1)S(1)} copy(bf16[8,256,32]{2,1,0:T(8,128)(2,1)} %bitcast.26) | data formatting | bytes 262144 | tf_op jit(solution)/shard_map/all_to_all | solution.py:182
  78.0 16.2 %all_to_all.21 = bf16[8,256,32]{1,2,0:T(8,128)(2,1)S(1)} all-to-all(bf16[8,256,32]{1,2,0:T(8,128)(2,1)S(1)} %copy.19), channel_id=1, replica_groups=mesh['space'=96,'group'=8] {'group'}, dimensions={0} | all-to-all | bytes 262144 | tf_op jit(solution)/shard_map/all_to_all | solution.py:182
  94.2 0.7 copy.21
  (3 shorter events, 0.0 us)
Async XLA Ops:
  22.5 2.9 %copy-start = (bf16[8,256,66]{2,1,0:T(8,128)(2,1)}, bf16[8,256,66]{2,1,0:T(8,128)(2,1)S(1)}, u32[]{:S(2)}) copy-start(bf16[8,256,66]{2,1,0:T(8,128)(2,1)S(1)} %copy.18) | copy-start | bytes 811012
  33.1 14.9 %collective-permute-start.1 = (f32[2,16,1024]{2,1,0:T(8,128)S(1)}, f32[2,16,1024]{2,1,0:T(8,128)S(1)}, u32[]{:S(2)}, u32[]{:S(2)}) collective-permute-start(f32[2,16,1024]{2,1,0:T(8,128)S(1)} %bitcast.34), channel_id=1, source_target_pairs={{8,0},{16,8},{24,16},{32,24},{40,32},{48,40},{56,48},{64,56},{72,6... | collective-permute-start | bytes 393224 | tf_op jit(solution)/shard_map/ppermute | solution.py:29
  45.5 8.4 %collective-permute-start = (f32[2,16,1024]{2,1,0:T(8,128)S(1)}, f32[2,16,1024]{2,1,0:T(8,128)S(1)}, u32[]{:S(2)}, u32[]{:S(2)}) collective-permute-start(f32[2,16,1024]{2,1,0:T(8,128)S(1)} %bitcast.33), channel_id=1, source_target_pairs={{0,8},{8,16},{16,24},{24,32},{32,40},{40,48},{48,56},{56,64},{64,7... | collective-permute-start | bytes 393224 | tf_op jit(solution)/shard_map/ppermute | solution.py:28
  54.0 9.8 %collective-permute-start.2 = (f32[20,2,1024]{2,1,0:T(2,128)S(1)}, f32[20,2,1024]{2,1,0:T(2,128)S(1)}, u32[]{:S(2)}, u32[]{:S(2)}) collective-permute-start(f32[20,2,1024]{2,1,0:T(2,128)S(1)} %get-tuple-element.11), channel_id=1, source_target_pairs={{0,1},{1,2},{2,3},{3,4},{4,5},{5,6},{6,7},{8,9},{9,10},{10,11},{11... | collective-permute-start | bytes 491528 | tf_op jit(solution)/shard_map/ppermute | solution.py:28
  55.6 8.2 %collective-permute-start.3 = (f32[20,2,1024]{2,1,0:T(2,128)S(1)}, f32[20,2,1024]{2,1,0:T(2,128)S(1)}, u32[]{:S(2)}, u32[]{:S(2)}) collective-permute-start(f32[20,2,1024]{2,1,0:T(2,128)S(1)} %get-tuple-element.12), channel_id=1, source_target_pairs={{1,0},{2,1},{3,2},{4,3},{5,4},{6,5},{7,6},{9,8},{10,9},{11,10},{12... | collective-permute-start | bytes 491528 | tf_op jit(solution)/shard_map/ppermute | solution.py:29
  71.1 1.0 %copy-start.1 = (f32[256,512]{1,0:T(8,128)S(1)}, f32[256,512]{1,0:T(8,128)}, u32[]{:S(2)}) copy-start(f32[256,512]{1,0:T(8,128)} %get-tuple-element.10) | copy-start | bytes 1572868

commit v5 on v4

--- a/solution.py
+++ b/solution.py
@@ -31,7 +31,7 @@
     return shard
 
 
-def scatter_kernel(got_ref, xy_ref, z_ref, mean_ref, gy_ref, div_ref):
+def scatter_kernel(got_ref, xy_ref, z_ref, field_ref, div_ref):
     npts = got_ref.shape[0]
     r = lax.broadcasted_iota(jnp.int32, (PW, ZC), 0)
     l = lax.broadcasted_iota(jnp.int32, (PW, ZC), 1)
@@ -55,17 +55,16 @@
         sc = sc + jnp.dot(hot, qc, preferred_element_type=jnp.float32)
         sn = sn + jnp.dot(hot, qn, preferred_element_type=jnp.float32)
     div = jnp.maximum(sn, 1.0)
-    mean_ref[...] = (sf / div).astype(jnp.bfloat16).astype(jnp.float32)
-    gy_ref[...] = sc
+    field_ref[:, :ZC] = (sf / div).astype(jnp.bfloat16).astype(jnp.float32)
+    field_ref[:, ZC:] = sc
     div_ref[...] = div
 
 
 def scatter_sums(got, xy_row, z_col):
     npts = got.shape[0]
-    field = jax.ShapeDtypeStruct((XY, ZC), jnp.float32)
     return pl.pallas_call(
         scatter_kernel,
-        out_shape=(field, field, field),
+        out_shape=(jax.ShapeDtypeStruct((XY, 2 * ZC), jnp.float32), jax.ShapeDtypeStruct((XY, ZC), jnp.float32)),
         cost_estimate=pl.CostEstimate(
             flops=2 * XY * npts * ZC * 3 + 4 * npts * PW * ZC, transcendentals=0,
             bytes_accessed=npts * PW * 2 + 3 * XY * ZC * 4,
@@ -138,13 +137,14 @@
     lr = lax.broadcasted_iota(jnp.int32, (C, ZC), 0)
     lc = lax.broadcasted_iota(jnp.int32, (C, ZC), 1)
     rep_lanes = (lr == jnp.bitwise_and(lc, C - 1)).astype(jnp.bfloat16)
-    lane_z = lc >> 5
-    wides = [jnp.dot(w_ref[dz], rep_lanes, preferred_element_type=jnp.float32) for dz in range(3)]
+    lane_z = (lc >> 5).astype(jnp.float32).astype(jnp.bfloat16)
+    wides = [jnp.dot(w_ref[dz], rep_lanes, preferred_element_type=jnp.float32).astype(jnp.bfloat16) for dz in range(3)]
+    zero = jnp.zeros((C, ZC), jnp.bfloat16)
     for zp in range(ZB):
-        block = jnp.zeros((C, ZC), jnp.float32)
+        block = zero
         for dz in range(3):
-            block = jnp.where(lane_z == zp + 1 - dz, wides[dz], block)
-        wb_ref[pl.ds(zp * C, C), :] = block.astype(wb_ref.dtype)
+            block = jnp.where(lane_z == jnp.bfloat16(zp + 1 - dz), wides[dz], block)
+        wb_ref[pl.ds(zp * C, C), :] = block
 
 
 def banded_weights(kernel):
@@ -170,8 +170,8 @@
     got = lax.all_to_all(payload, "group", split_axis=0, concat_axis=0, tiled=True)
     xy = got[:, 2 * C].astype(jnp.int32)
     z = got[:, 2 * C + 1].astype(jnp.int32)
-    mean, gy, divisor = scatter_sums(got, xy.reshape(1, npts), z.reshape(npts, 1))
-    field = jnp.concatenate([mean, gy], axis=1).reshape(XD, YD, 2 * ZC)
+    field, divisor = scatter_sums(got, xy.reshape(1, npts), z.reshape(npts, 1))
+    field = field.reshape(XD, YD, 2 * ZC)
     wide = extended(field, (("space", 0), ("group", 1)), 2)
     mean_ext = wide[..., :ZC].astype(jnp.bfloat16).reshape(ER, ZC)
     gy_ext = wide[..., ZC:].reshape(ER, ZC)

time: 96 us -> 95.7 us (level)
  other arithmetic: 4.91 us -> 6.11 us
  local copies, waits for them, and re-layouts: 7.62 us -> 6.43 us
    slice x1, other arithmetic: 0.12 us -> 1.32 us  [extended(): last = lax.slice_in_dim(shard, length - width, length, axis=dim)]
    concatenate x1 -> x0, local copies, waits for them, and re-layouts: 1.08 us -> none  [per_device(): field = jnp.concatenate([mean, gy], axis=1).reshape(XD, YD, 2 * ZC)]
    unnamed x7 -> x8, local copies, waits for them, and re-layouts: 3.81 us -> 2.74 us
    slice x1, local copies, waits for them, and re-layouts: 0.02 us -> 0.99 us  [extended(): last = lax.slice_in_dim(shard, length - width, length, axis=dim)]
where the time goes in v5:
time: 95.7 us; the launch traced here: 94.7 us
  blocking collectives  35.6 us (37%)
  Pallas kernels  22.7 us (24%)
  starting transfers between devices  17.2 us (18%)
  waiting for transfers between devices  6.47 us (7%)
  local copies, waits for them, and re-layouts  6.43 us (7%)
  other arithmetic  6.11 us (6%)
    all_to_all x1, blocking collectives, per_device(): lax.all_to_all(payload, 'group', split_axis=0, concat_axis=0, tiled=True)  19.5 us
    all_to_all x1, blocking collectives, per_device(): lax.all_to_all(grads, 'group', split_axis=0, concat_axis=0, tiled=True)  16.1 us
    ppermute x2, starting transfers between devices, extended(): after = lax.ppermute(first, axis, down)  13.7 us
    pallas_call x1, Pallas kernels, conv_pair(): pl.pallas_call(conv_kernel, out_shape=jax.ShapeDtypeStruct((ER, ZC), jnp....  6.66 us
    pallas_call x1, Pallas kernels, banded_weights(): pl.pallas_call(band_kernel, out_shape=jax.ShapeDtypeStruct((9, ZC, ZC), k...  6.62 us
    ppermute x2, waiting for transfers between devices, extended(): before = lax.ppermute(last, axis, up)  5.9 us
    pallas_call x1, Pallas kernels, scatter_sums(): pl.pallas_call(scatter_kernel, out_shape=(jax.ShapeDtypeStruct((XY, 2 * Z...  5.56 us
    pallas_call x1, Pallas kernels, gather_rows(): pl.pallas_call(gather_kernel, out_shape=jax.ShapeDtypeStruct((npts, C), j...  3.82 us
  transfers between devices with their start and end apart: 4, of which 2 were waited for; matrix products, arithmetic and copies ran while one was open for 0% of the time, Pallas kernels for 7%

profile of v5, /device:TPU:6, one launch (start us, length us, event | category | flops | bytes accessed | tf_op | source)
XLA Modules:
  0.0 94.7 jit_solution(16852763031920789995)
XLA Ops:
  0.0 0.7 select_convert_fusion
  0.7 0.9 copy.22
  1.7 0.9 copy.23
  2.6 0.1 pad_maximum_fusion.1
  2.7 0.1 copy.17
  2.7 19.5 %all_to_all.20 = bf16[8,256,66]{1,2,0:T(8,128)(2,1)S(1)} all-to-all(bf16[8,256,66]{1,2,0:T(8,128)(2,1)S(1)} %copy.17), channel_id=1, replica_groups=mesh['space'=96,'group'=8] {'group'}, dimensions={0} | all-to-all | bytes 540672 | tf_op jit(solution)/shard_map/all_to_all | solution.py:170
  22.2 0.3 copy.18
  22.5 0.0 copy-start
  22.5 1.1 %fusion.1 = s32[2048]{0:T(1024)} fusion(bf16[2048,66]{1,0:T(8,128)(2,1)S(1)} %bitcast.21), kind=kLoop, calls=%fused_computation.7 | loop fusion | flops 2048 | bytes 12288 | tf_op jit(solution)/shard_map/convert_element_type | solution.py:171
  23.6 1.8 %slice_convert_fusion.2 = (s32[2048,1]{1,0:T(8,128)}, s32[2048,1]{1,0:T(8,128)}) fusion(bf16[2048,66]{1,0:T(8,128)(2,1)S(1)} %bitcast.22), kind=kLoop, calls=%fused_computation.3 | loop fusion | flops 4096 | bytes 24576 | tf_op jit(solution)/shard_map/convert_element_type | solution.py:171
  25.4 0.0 copy-done
  25.4 5.6 %shard_map.46 = (f32[256,1024]{1,0:T(8,128)}, f32[256,512]{1,0:T(8,128)}) custom-call(bf16[2048,66]{1,0:T(8,128)(2,1)} %bitcast.23, s32[1,2048]{1,0:T(1,128)} %bitcast.35, s32[2048,1]{1,0:T(8,128)} %get-tuple-element.14.z_ref), custom_call_target="tpu_custom_call" | custom-call | flops 1887436800 | bytes 1843200 | tf_op jit(solution)/shard_map/pallas_call | solution.py:65
  31.0 1.0 %fusion.2 = (f32[32,1024]{1,0:T(8,128)S(1)}, f32[32,1024]{1,0:T(8,128)S(1)}) fusion(f32[256,1024]{1,0:T(8,128)} %get-tuple-element.7), kind=kLoop, calls=%fused_computation.13 | loop fusion | bytes 524288 | tf_op jit(solution)/shard_map/slice | solution.py:26
  32.0 12.4 %collective-permute-start.1 = (f32[2,16,1024]{2,1,0:T(8,128)S(1)}, f32[2,16,1024]{2,1,0:T(8,128)S(1)}, u32[]{:S(2)}, u32[]{:S(2)}) collective-permute-start(f32[2,16,1024]{2,1,0:T(8,128)S(1)} %bitcast.34), channel_id=1, source_target_pairs={{8,0},{16,8},{24,16},{32,24},{40,32},{48,40},{56,48},{64,56},{72,6... | collective-permute-start | bytes 393224 | tf_op jit(solution)/shard_map/ppermute | solution.py:29
  44.4 1.9 %collective-permute-start = (f32[2,16,1024]{2,1,0:T(8,128)S(1)}, f32[2,16,1024]{2,1,0:T(8,128)S(1)}, u32[]{:S(2)}, u32[]{:S(2)}) collective-permute-start(f32[2,16,1024]{2,1,0:T(8,128)S(1)} %bitcast.33), channel_id=1, source_target_pairs={{0,8},{8,16},{16,24},{24,32},{32,40},{40,48},{48,56},{56,64},{64,7... | collective-permute-start | bytes 393224 | tf_op jit(solution)/shard_map/ppermute | solution.py:28
  46.3 0.6 collective-permute-done.1
  46.9 5.9 %collective-permute-done = f32[2,16,1024]{2,1,0:T(8,128)S(1)} collective-permute-done((f32[2,16,1024]{2,1,0:T(8,128)S(1)}, f32[2,16,1024]{2,1,0:T(8,128)S(1)}, u32[]{:S(2)}, u32[]{:S(2)}) %collective-permute-start) | collective-permute-done | bytes 131104 | tf_op jit(solution)/shard_map/ppermute | solution.py:28
  52.8 1.3 %pad_maximum_fusion.4 = (f32[20,2,1024]{2,1,0:T(2,128)S(1)}, f32[20,2,1024]{2,1,0:T(2,128)S(1)}) fusion(f32[2,16,1024]{2,1,0:T(8,128)S(1)} %collective-permute-done.1, f32[16,16,1024]{2,1,0:T(8,128)} %bitcast.24, f32[2,16,1024]{2,1,0:T(8,128)S(1)} %collective-permute-done), kind=kLoop, calls=%fused_computation.10 | loop fusion | flops 163840 | bytes 1638400 | tf_op jit(solution)/shard_map/slice | solution.py:26
  54.1 1.6 %collective-permute-start.2 = (f32[20,2,1024]{2,1,0:T(2,128)S(1)}, f32[20,2,1024]{2,1,0:T(2,128)S(1)}, u32[]{:S(2)}, u32[]{:S(2)}) collective-permute-start(f32[20,2,1024]{2,1,0:T(2,128)S(1)} %get-tuple-element.9), channel_id=1, source_target_pairs={{0,1},{1,2},{2,3},{3,4},{4,5},{5,6},{6,7},{8,9},{9,10},{10,11},{11... | collective-permute-start | bytes 491528 | tf_op jit(solution)/shard_map/ppermute | solution.py:28
  55.7 1.3 %collective-permute-start.3 = (f32[20,2,1024]{2,1,0:T(2,128)S(1)}, f32[20,2,1024]{2,1,0:T(2,128)S(1)}, u32[]{:S(2)}, u32[]{:S(2)}) collective-permute-start(f32[20,2,1024]{2,1,0:T(2,128)S(1)} %get-tuple-element.10), channel_id=1, source_target_pairs={{1,0},{2,1},{3,2},{4,3},{5,4},{6,5},{7,6},{9,8},{10,9},{11,10},{12... | collective-permute-start | bytes 491528 | tf_op jit(solution)/shard_map/ppermute | solution.py:29
  57.0 0.0 copy-start.1
  57.0 6.6 %shard_map.47.w_ref = bf16[9,512,512]{2,1,0:T(8,128)(2,1)} custom-call(bf16[27,32,32]{2,1,0:T(8,128)(2,1)} %bitcast.30), custom_call_target="tpu_custom_call" | custom-call | flops 905969664 | bytes 4718592 | tf_op jit(solution)/shard_map/pallas_call | solution.py:152
  63.6 0.0 collective-permute-done.2
  63.6 0.0 collective-permute-done.3
  63.6 0.0 copy-done.1
  63.7 0.3 pad_maximum_fusion
  64.0 0.1 slice.55
  64.0 0.1 slice.48
  64.1 0.1 reshape.48.g_ref
  64.2 0.1 reshape.47.m_ref
  64.3 6.7 %shard_map.48 = f32[400,512]{1,0:T(8,128)S(1)} custom-call(bf16[400,512]{1,0:T(8,128)(2,1)S(1)} %reshape.47.m_ref, f32[400,512]{1,0:T(8,128)S(1)} %reshape.48.g_ref, bf16[9,512,512]{2,1,0:T(8,128)(2,1)} %shard_map.47.w_ref), custom_call_target="tpu_custom_call" | custom-call | flops 3774873600 | bytes 6766592 | tf_op jit(solution)/shard_map/pallas_call | solution.py:97
  71.0 0.0 copy-start.2
  71.0 0.1 reshape.50
  71.1 0.1 slice.49
  71.2 0.9 copy-done.2
  72.0 0.8 fusion.t_ref
  72.8 3.8 %shard_map.49 = bf16[2048,32]{1,0:T(8,128)(2,1)} custom-call(bf16[256,512]{1,0:T(8,128)(2,1)} %fusion.t_ref, s32[2048,1]{1,0:T(8,128)} %get-tuple-element.13.xy_ref, s32[2048,1]{1,0:T(8,128)} %get-tuple-element.14.z_ref), custom_call_target="tpu_custom_call" | custom-call | flops 603979776 | bytes 393216 | tf_op jit(solution)/shard_map/pallas_call | solution.py:126
  76.7 1.2 %copy.19 = bf16[8,256,32]{1,2,0:T(8,128)(2,1)S(1)} copy(bf16[8,256,32]{2,1,0:T(8,128)(2,1)} %bitcast.26) | data formatting | bytes 262144 | tf_op jit(solution)/shard_map/all_to_all | solution.py:182
  77.9 16.1 %all_to_all.21 = bf16[8,256,32]{1,2,0:T(8,128)(2,1)S(1)} all-to-all(bf16[8,256,32]{1,2,0:T(8,128)(2,1)S(1)} %copy.19), channel_id=1, replica_groups=mesh['space'=96,'group'=8] {'group'}, dimensions={0} | all-to-all | bytes 262144 | tf_op jit(solution)/shard_map/all_to_all | solution.py:182
  94.0 0.7 copy.21
  (2 shorter events, 0.0 us)
Async XLA Ops:
  22.5 2.9 %copy-start = (bf16[8,256,66]{2,1,0:T(8,128)(2,1)}, bf16[8,256,66]{2,1,0:T(8,128)(2,1)S(1)}, u32[]{:S(2)}) copy-start(bf16[8,256,66]{2,1,0:T(8,128)(2,1)S(1)} %copy.18) | copy-start | bytes 811012
  32.0 14.9 %collective-permute-start.1 = (f32[2,16,1024]{2,1,0:T(8,128)S(1)}, f32[2,16,1024]{2,1,0:T(8,128)S(1)}, u32[]{:S(2)}, u32[]{:S(2)}) collective-permute-start(f32[2,16,1024]{2,1,0:T(8,128)S(1)} %bitcast.34), channel_id=1, source_target_pairs={{8,0},{16,8},{24,16},{32,24},{40,32},{48,40},{56,48},{64,56},{72,6... | collective-permute-start | bytes 393224 | tf_op jit(solution)/shard_map/ppermute | solution.py:29
  44.4 8.4 %collective-permute-start = (f32[2,16,1024]{2,1,0:T(8,128)S(1)}, f32[2,16,1024]{2,1,0:T(8,128)S(1)}, u32[]{:S(2)}, u32[]{:S(2)}) collective-permute-start(f32[2,16,1024]{2,1,0:T(8,128)S(1)} %bitcast.33), channel_id=1, source_target_pairs={{0,8},{8,16},{16,24},{24,32},{32,40},{40,48},{48,56},{56,64},{64,7... | collective-permute-start | bytes 393224 | tf_op jit(solution)/shard_map/ppermute | solution.py:28
  54.1 9.5 %collective-permute-start.2 = (f32[20,2,1024]{2,1,0:T(2,128)S(1)}, f32[20,2,1024]{2,1,0:T(2,128)S(1)}, u32[]{:S(2)}, u32[]{:S(2)}) collective-permute-start(f32[20,2,1024]{2,1,0:T(2,128)S(1)} %get-tuple-element.9), channel_id=1, source_target_pairs={{0,1},{1,2},{2,3},{3,4},{4,5},{5,6},{6,7},{8,9},{9,10},{10,11},{11... | collective-permute-start | bytes 491528 | tf_op jit(solution)/shard_map/ppermute | solution.py:28
  55.7 7.9 %collective-permute-start.3 = (f32[20,2,1024]{2,1,0:T(2,128)S(1)}, f32[20,2,1024]{2,1,0:T(2,128)S(1)}, u32[]{:S(2)}, u32[]{:S(2)}) collective-permute-start(f32[20,2,1024]{2,1,0:T(2,128)S(1)} %get-tuple-element.10), channel_id=1, source_target_pairs={{1,0},{2,1},{3,2},{4,3},{5,4},{6,5},{7,6},{9,8},{10,9},{11,10},{12... | collective-permute-start | bytes 491528 | tf_op jit(solution)/shard_map/ppermute | solution.py:29
  57.0 6.6 %copy-start.1 = (f32[256,1024]{1,0:T(8,128)S(1)}, f32[256,1024]{1,0:T(8,128)}, u32[]{:S(2)}) copy-start(f32[256,1024]{1,0:T(8,128)} %get-tuple-element.7) | copy-start | bytes 3145732
  71.0 1.0 %copy-start.2 = (f32[256,512]{1,0:T(8,128)S(1)}, f32[256,512]{1,0:T(8,128)}, u32[]{:S(2)}) copy-start(f32[256,512]{1,0:T(8,128)} %get-tuple-element.8) | copy-start | bytes 1572868

commit v6 on v5

--- a/solution.py
+++ b/solution.py
@@ -18,17 +18,32 @@
 ER = EX * EY
 
 
-def extended(shard, sides, width):
-    for axis, dim in sides:
-        size, length = (lax.axis_size(axis), shard.shape[dim])
-        up = [(i, (i + 1) % size) for i in range(size - 1)]
-        down = [(j, i) for i, j in up]
-        last = lax.slice_in_dim(shard, length - width, length, axis=dim)
-        first = lax.slice_in_dim(shard, 0, width, axis=dim)
-        before = lax.ppermute(last, axis, up)
-        after = lax.ppermute(first, axis, down)
-        shard = jnp.concatenate([before, shard, after], axis=dim)
-    return shard
+def neighbour(block, shift_s, shift_g):
+    ns, ng = lax.axis_size("space"), lax.axis_size("group")
+    pairs = []
+    for s in range(ns):
+        for g in range(ng):
+            t, h = s + shift_s, g + shift_g
+            if 0 <= t < ns and 0 <= h < ng:
+                pairs.append((s * ng + g, t * ng + h))
+    return lax.ppermute(block, ("space", "group"), pairs)
+
+
+def extended(field, width):
+    lo, hi = slice(0, width), slice(field.shape[0] - width, field.shape[0])
+    yl, yh = slice(0, width), slice(field.shape[1] - width, field.shape[1])
+    x_before = neighbour(field[hi], 1, 0)
+    x_after = neighbour(field[lo], -1, 0)
+    y_before = neighbour(field[:, yh], 0, 1)
+    y_after = neighbour(field[:, yl], 0, -1)
+    c_mm = neighbour(field[hi, yh], 1, 1)
+    c_mp = neighbour(field[hi, yl], 1, -1)
+    c_pm = neighbour(field[lo, yh], -1, 1)
+    c_pp = neighbour(field[lo, yl], -1, -1)
+    top = jnp.concatenate([c_mm, x_before, c_mp], axis=1)
+    mid = jnp.concatenate([y_before, field, y_after], axis=1)
+    bot = jnp.concatenate([c_pm, x_after, c_pp], axis=1)
+    return jnp.concatenate([top, mid, bot], axis=0)
 
 
 def scatter_kernel(got_ref, xy_ref, z_ref, field_ref, div_ref):
@@ -172,9 +187,9 @@
     z = got[:, 2 * C + 1].astype(jnp.int32)
     field, divisor = scatter_sums(got, xy.reshape(1, npts), z.reshape(npts, 1))
     field = field.reshape(XD, YD, 2 * ZC)
-    wide = extended(field, (("space", 0), ("group", 1)), 2)
+    wide = extended(field, 2)
     mean_ext = wide[..., :ZC].astype(jnp.bfloat16).reshape(ER, ZC)
-    gy_ext = wide[..., ZC:].reshape(ER, ZC)
+    gy_ext = wide[..., ZC:].astype(jnp.float32).reshape(ER, ZC)
     ggrid = conv_pair(mean_ext, gy_ext, banded_weights(kernel))
     center = ggrid.reshape(EX, EY, ZC)[2 : 2 + XD, 2 : 2 + YD].reshape(XY, ZC)
     table = (center / divisor).astype(jnp.bfloat16)

time: 95.7 us -> 110 us (1.15)
  starting transfers between devices: 17.2 us -> 32.1 us
  local copies, waits for them, and re-layouts: 6.43 us -> 8.71 us
  other arithmetic: 6.11 us -> 4.81 us
  waiting for transfers between devices: 6.47 us -> 5.31 us
    ppermute x4 -> x8, starting transfers between devices: 17.2 us -> 32.1 us  [neighbour(): return lax.ppermute(block, ('space', 'group'), pairs)]
    slice x2 -> x4, local copies, waits for them, and re-layouts: 1.05 us -> 3.33 us  [the longest x1 1.3 us: extended(): y_before = neighbour(field[:, yh], 0, 1)]
    slice x1 -> x0, other arithmetic: 1.32 us -> none  [extended(): last = lax.slice_in_dim(shard, length - width, length, axis=dim)]
    ppermute x4 -> x8, waiting for transfers between devices: 6.47 us -> 5.31 us  [neighbour(): return lax.ppermute(block, ('space', 'group'), pairs)]
  transfers between devices with their start and end apart: 4 -> 8, of which waited for: 2 -> 3; matrix products, arithmetic and copies ran while one was open for 0% -> 1% of each run, Pallas kernels for 7% -> 6%
where the time goes in v6:
time: 110 us; the launch traced here: 108 us
  blocking collectives  34.6 us (31%)
  starting transfers between devices  32.1 us (29%)
  Pallas kernels  22.7 us (21%)
  local copies, waits for them, and re-layouts  8.71 us (8%)
  waiting for transfers between devices  5.31 us (5%)
  other arithmetic  4.81 us (4%)
    ppermute x8, starting transfers between devices, neighbour(): return lax.ppermute(block, ('space', 'group'), pairs)  32.1 us
    all_to_all x1, blocking collectives, per_device(): lax.all_to_all(payload, 'group', split_axis=0, concat_axis=0, tiled=True)  19.5 us
    all_to_all x1, blocking collectives, per_device(): lax.all_to_all(grads, 'group', split_axis=0, concat_axis=0, tiled=True)  15.1 us
    pallas_call x1, Pallas kernels, conv_pair(): pl.pallas_call(conv_kernel, out_shape=jax.ShapeDtypeStruct((ER, ZC), jnp....  6.65 us
    pallas_call x1, Pallas kernels, banded_weights(): pl.pallas_call(band_kernel, out_shape=jax.ShapeDtypeStruct((9, ZC, ZC), k...  6.64 us
    pallas_call x1, Pallas kernels, scatter_sums(): pl.pallas_call(scatter_kernel, out_shape=(jax.ShapeDtypeStruct((XY, 2 * Z...  5.56 us
    ppermute x8, waiting for transfers between devices, neighbour(): return lax.ppermute(block, ('space', 'group'), pairs)  5.31 us
    pallas_call x1, Pallas kernels, gather_rows(): pl.pallas_call(gather_kernel, out_shape=jax.ShapeDtypeStruct((npts, C), j...  3.82 us
  transfers between devices with their start and end apart: 8, of which 3 were waited for; matrix products, arithmetic and copies ran while one was open for 1% of the time, Pallas kernels for 6%

profile of v6, /device:TPU:6, one launch (start us, length us, event | category | flops | bytes accessed | tf_op | source)
XLA Modules:
  0.0 108.4 jit_solution(7987569576098799345)
XLA Ops:
  0.0 0.7 select_convert_fusion
  0.7 0.9 copy.22
  1.7 0.9 copy.23
  2.6 0.1 pad_maximum_fusion
  2.7 0.1 copy.17
  2.7 19.5 %all_to_all.20 = bf16[8,256,66]{1,2,0:T(8,128)(2,1)S(1)} all-to-all(bf16[8,256,66]{1,2,0:T(8,128)(2,1)S(1)} %copy.17), channel_id=1, replica_groups=mesh['space'=96,'group'=8] {'group'}, dimensions={0} | all-to-all | bytes 540672 | tf_op jit(solution)/shard_map/all_to_all | solution.py:185
  22.2 0.3 copy.18
  22.5 1.1 %fusion.1 = s32[2048]{0:T(1024)} fusion(bf16[2048,66]{1,0:T(8,128)(2,1)S(1)} %bitcast.21), kind=kLoop, calls=%fused_computation.7 | loop fusion | flops 2048 | bytes 12288 | tf_op jit(solution)/shard_map/convert_element_type | solution.py:186
  23.6 1.8 %slice_convert_fusion.2 = (s32[2048,1]{1,0:T(8,128)}, s32[2048,1]{1,0:T(8,128)}) fusion(bf16[2048,66]{1,0:T(8,128)(2,1)S(1)} %bitcast.22), kind=kLoop, calls=%fused_computation.3 | loop fusion | flops 4096 | bytes 24576 | tf_op jit(solution)/shard_map/convert_element_type | solution.py:186
  25.4 0.0 copy-done
  25.4 5.6 %shard_map.46 = (f32[256,1024]{1,0:T(8,128)}, f32[256,512]{1,0:T(8,128)}) custom-call(bf16[2048,66]{1,0:T(8,128)(2,1)} %bitcast.23, s32[1,2048]{1,0:T(1,128)} %bitcast.36, s32[2048,1]{1,0:T(8,128)} %get-tuple-element.18.z_ref), custom_call_target="tpu_custom_call" | custom-call | flops 1887436800 | bytes 1843200 | tf_op jit(solution)/shard_map/pallas_call | solution.py:80
  31.0 1.0 fusion.2
  31.9 1.3 %fusion.4 = (f32[16,2,1024]{2,1,0:T(2,128)S(1)}, f32[16,2,1024]{2,1,0:T(2,128)S(1)}) fusion(f32[16,16,1024]{2,1,0:T(8,128)} %bitcast.25), kind=kLoop, calls=%fused_computation.12 | loop fusion | bytes 524288 | tf_op jit(solution)/shard_map/slice | solution.py:37
  33.2 1.3 %collective-permute-start = (f32[2,2,1024]{2,1,0:T(2,128)S(1)}, f32[2,2,1024]{2,1,0:T(2,128)S(1)}, u32[]{:S(2)}, u32[]{:S(2)}) collective-permute-start(f32[2,2,1024]{2,1,0:T(2,128)S(1)} %get-tuple-element.9), channel_id=1, source_target_pairs={{0,9},{1,10},{2,11},{3,12},{4,13},{5,14},{6,15},{8,17},{9,18},{10,... | collective-permute-start | bytes 49160 | tf_op jit(solution)/shard_map/ppermute | solution.py:29
  34.5 1.0 fusion.3
  35.5 3.1 %collective-permute-start.3 = (f32[16,2,1024]{2,1,0:T(2,128)S(1)}, f32[16,2,1024]{2,1,0:T(2,128)S(1)}, u32[]{:S(2)}, u32[]{:S(2)}) collective-permute-start(f32[16,2,1024]{2,1,0:T(2,128)S(1)} %get-tuple-element.15), channel_id=1, source_target_pairs={{0,1},{1,2},{2,3},{3,4},{4,5},{5,6},{6,7},{8,9},{9,10},{10,11},{11... | collective-permute-start | bytes 393224 | tf_op jit(solution)/shard_map/ppermute | solution.py:29
  38.7 1.3 %collective-permute-start.4 = (f32[16,2,1024]{2,1,0:T(2,128)S(1)}, f32[16,2,1024]{2,1,0:T(2,128)S(1)}, u32[]{:S(2)}, u32[]{:S(2)}) collective-permute-start(f32[16,2,1024]{2,1,0:T(2,128)S(1)} %get-tuple-element.16), channel_id=1, source_target_pairs={{1,0},{2,1},{3,2},{4,3},{5,4},{6,5},{7,6},{9,8},{10,9},{11,10},{12... | collective-permute-start | bytes 393224 | tf_op jit(solution)/shard_map/ppermute | solution.py:29
  40.0 11.2 %collective-permute-start.6 = (f32[2,16,1024]{2,1,0:T(8,128)S(1)}, f32[2,16,1024]{2,1,0:T(8,128)S(1)}, u32[]{:S(2)}, u32[]{:S(2)}) collective-permute-start(f32[2,16,1024]{2,1,0:T(8,128)S(1)} %bitcast.35), channel_id=1, source_target_pairs={{8,0},{9,1},{10,2},{11,3},{12,4},{13,5},{14,6},{15,7},{16,8},{17,9... | collective-permute-start | bytes 393224 | tf_op jit(solution)/shard_map/ppermute | solution.py:29
  51.2 1.9 %collective-permute-start.1 = (f32[2,16,1024]{2,1,0:T(8,128)S(1)}, f32[2,16,1024]{2,1,0:T(8,128)S(1)}, u32[]{:S(2)}, u32[]{:S(2)}) collective-permute-start(f32[2,16,1024]{2,1,0:T(8,128)S(1)} %bitcast.34), channel_id=1, source_target_pairs={{0,8},{1,9},{2,10},{3,11},{4,12},{5,13},{6,14},{7,15},{8,16},{9,17... | collective-permute-start | bytes 393224 | tf_op jit(solution)/shard_map/ppermute | solution.py:29
  53.1 0.0 collective-permute-done
  53.1 1.3 %collective-permute-start.7 = (f32[2,2,1024]{2,1,0:T(2,128)S(1)}, f32[2,2,1024]{2,1,0:T(2,128)S(1)}, u32[]{:S(2)}, u32[]{:S(2)}) collective-permute-start(f32[2,2,1024]{2,1,0:T(2,128)S(1)} %get-tuple-element.10), channel_id=1, source_target_pairs={{9,0},{10,1},{11,2},{12,3},{13,4},{14,5},{15,6},{17,8},{18,9},{19,... | collective-permute-start | bytes 49160 | tf_op jit(solution)/shard_map/ppermute | solution.py:29
  54.4 3.8 %collective-permute-done.7 = f32[2,2,1024]{2,1,0:T(2,128)S(1)} collective-permute-done((f32[2,2,1024]{2,1,0:T(2,128)S(1)}, f32[2,2,1024]{2,1,0:T(2,128)S(1)}, u32[]{:S(2)}, u32[]{:S(2)}) %collective-permute-start.7) | collective-permute-done | bytes 16416 | tf_op jit(solution)/shard_map/ppermute | solution.py:29
  58.2 10.7 %collective-permute-start.5 = (f32[2,2,1024]{2,1,0:T(2,128)S(1)}, f32[2,2,1024]{2,1,0:T(2,128)S(1)}, u32[]{:S(2)}, u32[]{:S(2)}) collective-permute-start(f32[2,2,1024]{2,1,0:T(2,128)S(1)} %get-tuple-element.11), channel_id=1, source_target_pairs={{8,1},{9,2},{10,3},{11,4},{12,5},{13,6},{14,7},{16,9},{17,10},{18,... | collective-permute-start | bytes 49160 | tf_op jit(solution)/shard_map/ppermute | solution.py:29
  68.9 1.4 %collective-permute-done.5 = f32[2,2,1024]{2,1,0:T(2,128)S(1)} collective-permute-done((f32[2,2,1024]{2,1,0:T(2,128)S(1)}, f32[2,2,1024]{2,1,0:T(2,128)S(1)}, u32[]{:S(2)}, u32[]{:S(2)}) %collective-permute-start.5) | collective-permute-done | bytes 16416 | tf_op jit(solution)/shard_map/ppermute | solution.py:29
  70.3 1.3 %collective-permute-start.2 = (f32[2,2,1024]{2,1,0:T(2,128)S(1)}, f32[2,2,1024]{2,1,0:T(2,128)S(1)}, u32[]{:S(2)}, u32[]{:S(2)}) collective-permute-start(f32[2,2,1024]{2,1,0:T(2,128)S(1)} %get-tuple-element.12), channel_id=1, source_target_pairs={{1,8},{2,9},{3,10},{4,11},{5,12},{6,13},{7,14},{9,16},{10,17},{11,... | collective-permute-start | bytes 49160 | tf_op jit(solution)/shard_map/ppermute | solution.py:29
  71.6 0.0 copy-start.1
  71.6 6.6 %shard_map.47.w_ref = bf16[9,512,512]{2,1,0:T(8,128)(2,1)} custom-call(bf16[27,32,32]{2,1,0:T(8,128)(2,1)} %bitcast.31), custom_call_target="tpu_custom_call" | custom-call | flops 905969664 | bytes 4718592 | tf_op jit(solution)/shard_map/pallas_call | solution.py:167
  78.3 0.1 collective-permute-done.2
  78.4 0.0 collective-permute-done.3
  78.4 0.0 collective-permute-done.4
  78.4 0.0 collective-permute-done.6
  78.4 0.0 collective-permute-done.1
  78.4 0.0 copy-done.1
  78.4 0.3 maximum_maximum_fusion
  78.8 0.1 slice.77
  78.8 0.1 slice.70
  78.9 0.1 reshape.48.g_ref
  79.0 0.1 reshape.47.m_ref
  79.1 6.6 %shard_map.48 = f32[400,512]{1,0:T(8,128)S(1)} custom-call(bf16[400,512]{1,0:T(8,128)(2,1)S(1)} %reshape.47.m_ref, f32[400,512]{1,0:T(8,128)S(1)} %reshape.48.g_ref, bf16[9,512,512]{2,1,0:T(8,128)(2,1)} %shard_map.47.w_ref), custom_call_target="tpu_custom_call" | custom-call | flops 3774873600 | bytes 6766592 | tf_op jit(solution)/shard_map/pallas_call | solution.py:112
  85.8 0.0 copy-start.2
  85.8 0.1 reshape.50
  85.9 0.1 slice.71
  85.9 0.9 copy-done.2
  86.8 0.8 fusion.t_ref
  87.6 3.8 %shard_map.49 = bf16[2048,32]{1,0:T(8,128)(2,1)} custom-call(bf16[256,512]{1,0:T(8,128)(2,1)} %fusion.t_ref, s32[2048,1]{1,0:T(8,128)} %get-tuple-element.17.xy_ref, s32[2048,1]{1,0:T(8,128)} %get-tuple-element.18.z_ref), custom_call_target="tpu_custom_call" | custom-call | flops 603979776 | bytes 393216 | tf_op jit(solution)/shard_map/pallas_call | solution.py:141
  91.4 1.2 %copy.19 = bf16[8,256,32]{1,2,0:T(8,128)(2,1)S(1)} copy(bf16[8,256,32]{2,1,0:T(8,128)(2,1)} %bitcast.27) | data formatting | bytes 262144 | tf_op jit(solution)/shard_map/all_to_all | solution.py:197
  92.7 15.1 %all_to_all.21 = bf16[8,256,32]{1,2,0:T(8,128)(2,1)S(1)} all-to-all(bf16[8,256,32]{1,2,0:T(8,128)(2,1)S(1)} %copy.19), channel_id=1, replica_groups=mesh['space'=96,'group'=8] {'group'}, dimensions={0} | all-to-all | bytes 262144 | tf_op jit(solution)/shard_map/all_to_all | solution.py:197
  107.8 0.7 copy.21
  (3 shorter events, 0.0 us)
Async XLA Ops:
  22.5 2.9 %copy-start = (bf16[8,256,66]{2,1,0:T(8,128)(2,1)}, bf16[8,256,66]{2,1,0:T(8,128)(2,1)S(1)}, u32[]{:S(2)}) copy-start(bf16[8,256,66]{2,1,0:T(8,128)(2,1)S(1)} %copy.18) | copy-start | bytes 811012
  33.2 19.9 %collective-permute-start = (f32[2,2,1024]{2,1,0:T(2,128)S(1)}, f32[2,2,1024]{2,1,0:T(2,128)S(1)}, u32[]{:S(2)}, u32[]{:S(2)}) collective-permute-start(f32[2,2,1024]{2,1,0:T(2,128)S(1)} %get-tuple-element.9), channel_id=1, source_target_pairs={{0,9},{1,10},{2,11},{3,12},{4,13},{5,14},{6,15},{8,17},{9,18},{10,... | collective-permute-start | bytes 49160 | tf_op jit(solution)/shard_map/ppermute | solution.py:29
  35.5 42.9 %collective-permute-start.3 = (f32[16,2,1024]{2,1,0:T(2,128)S(1)}, f32[16,2,1024]{2,1,0:T(2,128)S(1)}, u32[]{:S(2)}, u32[]{:S(2)}) collective-permute-start(f32[16,2,1024]{2,1,0:T(2,128)S(1)} %get-tuple-element.15), channel_id=1, source_target_pairs={{0,1},{1,2},{2,3},{3,4},{4,5},{5,6},{6,7},{8,9},{9,10},{10,11},{11... | collective-permute-start | bytes 393224 | tf_op jit(solution)/shard_map/ppermute | solution.py:29
  38.7 39.7 %collective-permute-start.4 = (f32[16,2,1024]{2,1,0:T(2,128)S(1)}, f32[16,2,1024]{2,1,0:T(2,128)S(1)}, u32[]{:S(2)}, u32[]{:S(2)}) collective-permute-start(f32[16,2,1024]{2,1,0:T(2,128)S(1)} %get-tuple-element.16), channel_id=1, source_target_pairs={{1,0},{2,1},{3,2},{4,3},{5,4},{6,5},{7,6},{9,8},{10,9},{11,10},{12... | collective-permute-start | bytes 393224 | tf_op jit(solution)/shard_map/ppermute | solution.py:29
  40.0 38.4 %collective-permute-start.6 = (f32[2,16,1024]{2,1,0:T(8,128)S(1)}, f32[2,16,1024]{2,1,0:T(8,128)S(1)}, u32[]{:S(2)}, u32[]{:S(2)}) collective-permute-start(f32[2,16,1024]{2,1,0:T(8,128)S(1)} %bitcast.35), channel_id=1, source_target_pairs={{8,0},{9,1},{10,2},{11,3},{12,4},{13,5},{14,6},{15,7},{16,8},{17,9... | collective-permute-start | bytes 393224 | tf_op jit(solution)/shard_map/ppermute | solution.py:29
  51.2 27.2 %collective-permute-start.1 = (f32[2,16,1024]{2,1,0:T(8,128)S(1)}, f32[2,16,1024]{2,1,0:T(8,128)S(1)}, u32[]{:S(2)}, u32[]{:S(2)}) collective-permute-start(f32[2,16,1024]{2,1,0:T(8,128)S(1)} %bitcast.34), channel_id=1, source_target_pairs={{0,8},{1,9},{2,10},{3,11},{4,12},{5,13},{6,14},{7,15},{8,16},{9,17... | collective-permute-start | bytes 393224 | tf_op jit(solution)/shard_map/ppermute | solution.py:29
  53.1 5.1 %collective-permute-start.7 = (f32[2,2,1024]{2,1,0:T(2,128)S(1)}, f32[2,2,1024]{2,1,0:T(2,128)S(1)}, u32[]{:S(2)}, u32[]{:S(2)}) collective-permute-start(f32[2,2,1024]{2,1,0:T(2,128)S(1)} %get-tuple-element.10), channel_id=1, source_target_pairs={{9,0},{10,1},{11,2},{12,3},{13,4},{14,5},{15,6},{17,8},{18,9},{19,... | collective-permute-start | bytes 49160 | tf_op jit(solution)/shard_map/ppermute | solution.py:29
  58.2 12.1 %collective-permute-start.5 = (f32[2,2,1024]{2,1,0:T(2,128)S(1)}, f32[2,2,1024]{2,1,0:T(2,128)S(1)}, u32[]{:S(2)}, u32[]{:S(2)}) collective-permute-start(f32[2,2,1024]{2,1,0:T(2,128)S(1)} %get-tuple-element.11), channel_id=1, source_target_pairs={{8,1},{9,2},{10,3},{11,4},{12,5},{13,6},{14,7},{16,9},{17,10},{18,... | collective-permute-start | bytes 49160 | tf_op jit(solution)/shard_map/ppermute | solution.py:29
  70.3 8.1 %collective-permute-start.2 = (f32[2,2,1024]{2,1,0:T(2,128)S(1)}, f32[2,2,1024]{2,1,0:T(2,128)S(1)}, u32[]{:S(2)}, u32[]{:S(2)}) collective-permute-start(f32[2,2,1024]{2,1,0:T(2,128)S(1)} %get-tuple-element.12), channel_id=1, source_target_pairs={{1,8},{2,9},{3,10},{4,11},{5,12},{6,13},{7,14},{9,16},{10,17},{11,... | collective-permute-start | bytes 49160 | tf_op jit(solution)/shard_map/ppermute | solution.py:29
  71.6 6.8 %copy-start.1 = (f32[256,1024]{1,0:T(8,128)S(1)}, f32[256,1024]{1,0:T(8,128)}, u32[]{:S(2)}) copy-start(f32[256,1024]{1,0:T(8,128)} %get-tuple-element.7) | copy-start | bytes 3145732
  85.8 1.0 copy-start.2

commit v7 on v5

--- a/solution.py
+++ b/solution.py
@@ -31,36 +31,38 @@
     return shard
 
 
-def scatter_kernel(got_ref, xy_ref, z_ref, field_ref, div_ref):
+def scatter_kernel(got_ref, field_ref, div_ref):
     npts = got_ref.shape[0]
     r = lax.broadcasted_iota(jnp.int32, (PW, ZC), 0)
     l = lax.broadcasted_iota(jnp.int32, (PW, ZC), 1)
     ef = (r == jnp.bitwise_and(l, C - 1)).astype(jnp.bfloat16)
     ec = (r == jnp.bitwise_and(l, C - 1) + C).astype(jnp.bfloat16)
-    lane_z = lax.broadcasted_iota(jnp.int32, (TK, ZC), 1) >> 5
-    rows = lax.broadcasted_iota(jnp.int32, (XY, TK), 0)
+    lane_z = (lax.broadcasted_iota(jnp.int32, (TK, ZC), 1) >> 5).astype(jnp.float32)
+    lane_xy = lax.broadcasted_iota(jnp.int32, (TK, XY), 1).astype(jnp.float32)
     sf = jnp.zeros((XY, ZC), jnp.float32)
     sc = jnp.zeros((XY, ZC), jnp.float32)
     sn = jnp.zeros((XY, ZC), jnp.float32)
+    over_points = (((0,), (0,)), ((), ()))
     for k in range(npts // TK):
         g = got_ref[pl.ds(k * TK, TK), :]
-        mask = lane_z == z_ref[pl.ds(k * TK, TK), :]
+        wide = g.astype(jnp.float32)
+        mask = lane_z == wide[:, 2 * C + 1 : 2 * C + 2]
+        hot = (lane_xy == wide[:, 2 * C : 2 * C + 1]).astype(jnp.bfloat16)
         tf = jnp.dot(g, ef, preferred_element_type=jnp.float32)
         tc = jnp.dot(g, ec, preferred_element_type=jnp.float32)
         qf = jnp.where(mask, tf, 0.0).astype(jnp.bfloat16)
         qc = jnp.where(mask, tc, 0.0).astype(jnp.bfloat16)
         qn = mask.astype(jnp.bfloat16)
-        hot = (rows == xy_ref[:, pl.ds(k * TK, TK)]).astype(jnp.bfloat16)
-        sf = sf + jnp.dot(hot, qf, preferred_element_type=jnp.float32)
-        sc = sc + jnp.dot(hot, qc, preferred_element_type=jnp.float32)
-        sn = sn + jnp.dot(hot, qn, preferred_element_type=jnp.float32)
+        sf = sf + lax.dot_general(hot, qf, over_points, preferred_element_type=jnp.float32)
+        sc = sc + lax.dot_general(hot, qc, over_points, preferred_element_type=jnp.float32)
+        sn = sn + lax.dot_general(hot, qn, over_points, preferred_element_type=jnp.float32)
     div = jnp.maximum(sn, 1.0)
     field_ref[:, :ZC] = (sf / div).astype(jnp.bfloat16).astype(jnp.float32)
     field_ref[:, ZC:] = sc
     div_ref[...] = div
 
 
-def scatter_sums(got, xy_row, z_col):
+def scatter_sums(got):
     npts = got.shape[0]
     return pl.pallas_call(
         scatter_kernel,
@@ -69,7 +71,7 @@
             flops=2 * XY * npts * ZC * 3 + 4 * npts * PW * ZC, transcendentals=0,
             bytes_accessed=npts * PW * 2 + 3 * XY * ZC * 4,
         ),
-    )(got, xy_row, z_col)
+    )(got)
 
 
 def conv_kernel(m_ref, g_ref, w_ref, o_ref):
@@ -105,32 +107,33 @@
     )(mean_ext, gy_ext, banded)
 
 
-def gather_kernel(t_ref, xy_ref, z_ref, o_ref):
+def gather_kernel(t_ref, got_ref, o_ref):
     npts = o_ref.shape[0]
     r = lax.broadcasted_iota(jnp.int32, (ZC, C), 0)
     l = lax.broadcasted_iota(jnp.int32, (ZC, C), 1)
     fold = (jnp.bitwise_and(r, C - 1) == l).astype(jnp.bfloat16)
-    lane_z = lax.broadcasted_iota(jnp.int32, (TK, ZC), 1) >> 5
-    cols = lax.broadcasted_iota(jnp.int32, (TK, XY), 1)
+    lane_z = (lax.broadcasted_iota(jnp.int32, (TK, ZC), 1) >> 5).astype(jnp.float32)
+    lane_xy = lax.broadcasted_iota(jnp.int32, (TK, XY), 1).astype(jnp.float32)
     table = t_ref[...]
     for k in range(npts // TK):
-        hot = (cols == xy_ref[pl.ds(k * TK, TK), :]).astype(jnp.bfloat16)
+        wide = got_ref[pl.ds(k * TK, TK), :].astype(jnp.float32)
+        hot = (lane_xy == wide[:, 2 * C : 2 * C + 1]).astype(jnp.bfloat16)
         rows = jnp.dot(hot, table, preferred_element_type=jnp.float32)
-        mask = lane_z == z_ref[pl.ds(k * TK, TK), :]
+        mask = lane_z == wide[:, 2 * C + 1 : 2 * C + 2]
         picked = jnp.where(mask, rows, 0.0).astype(jnp.bfloat16)
         o_ref[pl.ds(k * TK, TK), :] = jnp.dot(picked, fold, preferred_element_type=jnp.float32).astype(o_ref.dtype)
 
 
-def gather_rows(table, xy_col, z_col):
-    npts = xy_col.shape[0]
+def gather_rows(table, got):
+    npts = got.shape[0]
     return pl.pallas_call(
         gather_kernel,
         out_shape=jax.ShapeDtypeStruct((npts, C), jnp.bfloat16),
         cost_estimate=pl.CostEstimate(
             flops=2 * npts * XY * ZC + 2 * npts * ZC * C, transcendentals=0,
-            bytes_accessed=npts * C * 2 + XY * ZC * 2,
+            bytes_accessed=npts * C * 2 + XY * ZC * 2 + npts * PW * 2,
         ),
-    )(table, xy_col, z_col)
+    )(table, got)
 
 
 def band_kernel(w_ref, wb_ref):
@@ -168,9 +171,7 @@
     z_send = jnp.bitwise_and(point_voxel, ZB - 1).astype(jnp.bfloat16)
     payload = jnp.concatenate([point_feats, cotangent, xy_send[:, None], z_send[:, None]], axis=1)
     got = lax.all_to_all(payload, "group", split_axis=0, concat_axis=0, tiled=True)
-    xy = got[:, 2 * C].astype(jnp.int32)
-    z = got[:, 2 * C + 1].astype(jnp.int32)
-    field, divisor = scatter_sums(got, xy.reshape(1, npts), z.reshape(npts, 1))
+    field, divisor = scatter_sums(got)
     field = field.reshape(XD, YD, 2 * ZC)
     wide = extended(field, (("space", 0), ("group", 1)), 2)
     mean_ext = wide[..., :ZC].astype(jnp.bfloat16).reshape(ER, ZC)
@@ -178,7 +179,7 @@
     ggrid = conv_pair(mean_ext, gy_ext, banded_weights(kernel))
     center = ggrid.reshape(EX, EY, ZC)[2 : 2 + XD, 2 : 2 + YD].reshape(XY, ZC)
     table = (center / divisor).astype(jnp.bfloat16)
-    grads = gather_rows(table, xy.reshape(npts, 1), z.reshape(npts, 1))
+    grads = gather_rows(table, got)
     return lax.all_to_all(grads, "group", split_axis=0, concat_axis=0, tiled=True)
 
 

time: 95.7 us -> 92.8 us (0.970)
  other arithmetic: 6.11 us -> 3.19 us
    convert_element_type x2 -> x0, other arithmetic: 2.92 us -> none  [per_device(): xy = got[:, 2 * C].astype(jnp.int32)]
    unnamed x8 -> x6, local copies, waits for them, and re-layouts: 2.74 us -> 2.73 us
where the time goes in v7:
time: 92.8 us; the launch traced here: 91.8 us
  blocking collectives  35.6 us (38%)
  Pallas kernels  21.9 us (24%)
  starting transfers between devices  17.2 us (19%)
  local copies, waits for them, and re-layouts  7.15 us (8%)
  waiting for transfers between devices  6.47 us (7%)
  other arithmetic  3.19 us (3%)
    all_to_all x1, blocking collectives, per_device(): lax.all_to_all(payload, 'group', split_axis=0, concat_axis=0, tiled=True)  19.5 us
    all_to_all x1, blocking collectives, per_device(): lax.all_to_all(grads, 'group', split_axis=0, concat_axis=0, tiled=True)  16.2 us
    ppermute x2, starting transfers between devices, extended(): after = lax.ppermute(first, axis, down)  13.7 us
    pallas_call x1, Pallas kernels, conv_pair(): pl.pallas_call(conv_kernel, out_shape=jax.ShapeDtypeStruct((ER, ZC), jnp....  6.65 us
    pallas_call x1, Pallas kernels, banded_weights(): pl.pallas_call(band_kernel, out_shape=jax.ShapeDtypeStruct((9, ZC, ZC), k...  6.62 us
    ppermute x2, waiting for transfers between devices, extended(): before = lax.ppermute(last, axis, up)  5.9 us
    pallas_call x1, Pallas kernels, scatter_sums(): pl.pallas_call(scatter_kernel, out_shape=(jax.ShapeDtypeStruct((XY, 2 * Z...  5.25 us
    ppermute x2, starting transfers between devices, extended(): before = lax.ppermute(last, axis, up)  3.51 us
  transfers between devices with their start and end apart: 4, of which 2 were waited for; matrix products, arithmetic and copies ran while one was open for 0% of the time, Pallas kernels for 7%

profile of v7, /device:TPU:6, one launch (start us, length us, event | category | flops | bytes accessed | tf_op | source)
XLA Modules:
  0.0 91.8 jit_solution(6187916469006091544)
XLA Ops:
  0.0 0.7 select_convert_fusion
  0.7 0.9 %copy.22 = bf16[4,8,8,256]{3,2,1,0:T(8,128)(2,1)S(1)} copy(bf16[4,8,8,256]{3,1,2,0:T(8,128)(2,1)} %bitcast.29) | data formatting | bytes 262144
  1.7 0.9 %copy.23 = bf16[4,8,8,256]{3,2,1,0:T(8,128)(2,1)S(1)} copy(bf16[4,8,8,256]{3,1,2,0:T(8,128)(2,1)} %bitcast.30) | data formatting | bytes 262144
  2.6 0.1 pad_maximum_fusion.1
  2.7 0.1 copy.17
  2.7 19.5 %all_to_all.20 = bf16[8,256,66]{1,2,0:T(8,128)(2,1)S(1)} all-to-all(bf16[8,256,66]{1,2,0:T(8,128)(2,1)S(1)} %copy.17), channel_id=1, replica_groups=mesh['space'=96,'group'=8] {'group'}, dimensions={0} | all-to-all | bytes 540672 | tf_op jit(solution)/shard_map/all_to_all | solution.py:173
  22.2 1.0 %copy.18 = bf16[8,256,66]{2,1,0:T(8,128)(2,1)} copy(bf16[8,256,66]{1,2,0:T(8,128)(2,1)S(1)} %all_to_all.20) | data formatting | bytes 540672 | tf_op jit(solution)/shard_map/all_to_all | solution.py:173
  23.2 5.3 %shard_map.46 = (f32[256,1024]{1,0:T(8,128)}, f32[256,512]{1,0:T(8,128)}) custom-call(bf16[2048,66]{1,0:T(8,128)(2,1)} %bitcast.23), custom_call_target="tpu_custom_call" | custom-call | flops 1887436800 | bytes 1843200 | tf_op jit(solution)/shard_map/pallas_call | solution.py:67
  28.5 1.0 %fusion.1 = (f32[32,1024]{1,0:T(8,128)S(1)}, f32[32,1024]{1,0:T(8,128)S(1)}) fusion(f32[256,1024]{1,0:T(8,128)} %get-tuple-element.7), kind=kLoop, calls=%fused_computation.10 | loop fusion | bytes 524288 | tf_op jit(solution)/shard_map/slice | solution.py:26
  29.5 12.4 %collective-permute-start.1 = (f32[2,16,1024]{2,1,0:T(8,128)S(1)}, f32[2,16,1024]{2,1,0:T(8,128)S(1)}, u32[]{:S(2)}, u32[]{:S(2)}) collective-permute-start(f32[2,16,1024]{2,1,0:T(8,128)S(1)} %bitcast.32), channel_id=1, source_target_pairs={{8,0},{16,8},{24,16},{32,24},{40,32},{48,40},{56,48},{64,56},{72,6... | collective-permute-start | bytes 393224 | tf_op jit(solution)/shard_map/ppermute | solution.py:29
  41.9 1.9 %collective-permute-start = (f32[2,16,1024]{2,1,0:T(8,128)S(1)}, f32[2,16,1024]{2,1,0:T(8,128)S(1)}, u32[]{:S(2)}, u32[]{:S(2)}) collective-permute-start(f32[2,16,1024]{2,1,0:T(8,128)S(1)} %bitcast.31), channel_id=1, source_target_pairs={{0,8},{8,16},{16,24},{24,32},{32,40},{40,48},{48,56},{56,64},{64,7... | collective-permute-start | bytes 393224 | tf_op jit(solution)/shard_map/ppermute | solution.py:28
  43.8 0.6 collective-permute-done.1
  44.4 5.9 %collective-permute-done = f32[2,16,1024]{2,1,0:T(8,128)S(1)} collective-permute-done((f32[2,16,1024]{2,1,0:T(8,128)S(1)}, f32[2,16,1024]{2,1,0:T(8,128)S(1)}, u32[]{:S(2)}, u32[]{:S(2)}) %collective-permute-start) | collective-permute-done | bytes 131104 | tf_op jit(solution)/shard_map/ppermute | solution.py:28
  50.3 1.3 %pad_maximum_fusion.4 = (f32[20,2,1024]{2,1,0:T(2,128)S(1)}, f32[20,2,1024]{2,1,0:T(2,128)S(1)}) fusion(f32[2,16,1024]{2,1,0:T(8,128)S(1)} %collective-permute-done.1, f32[16,16,1024]{2,1,0:T(8,128)} %bitcast.20, f32[2,16,1024]{2,1,0:T(8,128)S(1)} %collective-permute-done), kind=kLoop, calls=%fused_computation.7 | loop fusion | flops 163840 | bytes 1638400 | tf_op jit(solution)/shard_map/slice | solution.py:26
  51.6 1.6 %collective-permute-start.2 = (f32[20,2,1024]{2,1,0:T(2,128)S(1)}, f32[20,2,1024]{2,1,0:T(2,128)S(1)}, u32[]{:S(2)}, u32[]{:S(2)}) collective-permute-start(f32[20,2,1024]{2,1,0:T(2,128)S(1)} %get-tuple-element.9), channel_id=1, source_target_pairs={{0,1},{1,2},{2,3},{3,4},{4,5},{5,6},{6,7},{8,9},{9,10},{10,11},{11... | collective-permute-start | bytes 491528 | tf_op jit(solution)/shard_map/ppermute | solution.py:28
  53.2 1.3 %collective-permute-start.3 = (f32[20,2,1024]{2,1,0:T(2,128)S(1)}, f32[20,2,1024]{2,1,0:T(2,128)S(1)}, u32[]{:S(2)}, u32[]{:S(2)}) collective-permute-start(f32[20,2,1024]{2,1,0:T(2,128)S(1)} %get-tuple-element.10), channel_id=1, source_target_pairs={{1,0},{2,1},{3,2},{4,3},{5,4},{6,5},{7,6},{9,8},{10,9},{11,10},{12... | collective-permute-start | bytes 491528 | tf_op jit(solution)/shard_map/ppermute | solution.py:29
  54.5 0.0 copy-start
  54.5 6.6 %shard_map.47.w_ref = bf16[9,512,512]{2,1,0:T(8,128)(2,1)} custom-call(bf16[27,32,32]{2,1,0:T(8,128)(2,1)} %bitcast.28), custom_call_target="tpu_custom_call" | custom-call | flops 905969664 | bytes 4718592 | tf_op jit(solution)/shard_map/pallas_call | solution.py:155
  61.1 0.0 collective-permute-done.2
  61.1 0.0 collective-permute-done.3
  61.1 0.0 copy-done
  61.1 0.3 pad_maximum_fusion
  61.4 0.1 slice.41
  61.5 0.1 slice.38
  61.6 0.1 reshape.32.g_ref
  61.7 0.1 reshape.31.m_ref
  61.8 6.7 %shard_map.48 = f32[400,512]{1,0:T(8,128)S(1)} custom-call(bf16[400,512]{1,0:T(8,128)(2,1)S(1)} %reshape.31.m_ref, f32[400,512]{1,0:T(8,128)S(1)} %reshape.32.g_ref, bf16[9,512,512]{2,1,0:T(8,128)(2,1)} %shard_map.47.w_ref), custom_call_target="tpu_custom_call" | custom-call | flops 3774873600 | bytes 6766592 | tf_op jit(solution)/shard_map/pallas_call | solution.py:99
  68.4 0.0 copy-start.1
  68.4 0.1 reshape.34
  68.5 0.1 slice.39
  68.6 0.9 copy-done.1
  69.5 0.8 fusion.t_ref
  70.3 3.4 %shard_map.49 = bf16[2048,32]{1,0:T(8,128)(2,1)} custom-call(bf16[256,512]{1,0:T(8,128)(2,1)} %fusion.t_ref, bf16[2048,66]{1,0:T(8,128)(2,1)} %bitcast.24), custom_call_target="tpu_custom_call" | custom-call | flops 603979776 | bytes 663552 | tf_op jit(solution)/shard_map/pallas_call | solution.py:129
  73.7 1.2 %copy.19 = bf16[8,256,32]{1,2,0:T(8,128)(2,1)S(1)} copy(bf16[8,256,32]{2,1,0:T(8,128)(2,1)} %bitcast.22) | data formatting | bytes 262144 | tf_op jit(solution)/shard_map/all_to_all | solution.py:183
  74.9 16.2 %all_to_all.21 = bf16[8,256,32]{1,2,0:T(8,128)(2,1)S(1)} all-to-all(bf16[8,256,32]{1,2,0:T(8,128)(2,1)S(1)} %copy.19), channel_id=1, replica_groups=mesh['space'=96,'group'=8] {'group'}, dimensions={0} | all-to-all | bytes 262144 | tf_op jit(solution)/shard_map/all_to_all | solution.py:183
  91.1 0.7 copy.21
  (2 shorter events, 0.0 us)
Async XLA Ops:
  29.5 14.9 %collective-permute-start.1 = (f32[2,16,1024]{2,1,0:T(8,128)S(1)}, f32[2,16,1024]{2,1,0:T(8,128)S(1)}, u32[]{:S(2)}, u32[]{:S(2)}) collective-permute-start(f32[2,16,1024]{2,1,0:T(8,128)S(1)} %bitcast.32), channel_id=1, source_target_pairs={{8,0},{16,8},{24,16},{32,24},{40,32},{48,40},{56,48},{64,56},{72,6... | collective-permute-start | bytes 393224 | tf_op jit(solution)/shard_map/ppermute | solution.py:29
  41.9 8.4 %collective-permute-start = (f32[2,16,1024]{2,1,0:T(8,128)S(1)}, f32[2,16,1024]{2,1,0:T(8,128)S(1)}, u32[]{:S(2)}, u32[]{:S(2)}) collective-permute-start(f32[2,16,1024]{2,1,0:T(8,128)S(1)} %bitcast.31), channel_id=1, source_target_pairs={{0,8},{8,16},{16,24},{24,32},{32,40},{40,48},{48,56},{56,64},{64,7... | collective-permute-start | bytes 393224 | tf_op jit(solution)/shard_map/ppermute | solution.py:28
  51.6 9.5 %collective-permute-start.2 = (f32[20,2,1024]{2,1,0:T(2,128)S(1)}, f32[20,2,1024]{2,1,0:T(2,128)S(1)}, u32[]{:S(2)}, u32[]{:S(2)}) collective-permute-start(f32[20,2,1024]{2,1,0:T(2,128)S(1)} %get-tuple-element.9), channel_id=1, source_target_pairs={{0,1},{1,2},{2,3},{3,4},{4,5},{5,6},{6,7},{8,9},{9,10},{10,11},{11... | collective-permute-start | bytes 491528 | tf_op jit(solution)/shard_map/ppermute | solution.py:28
  53.2 7.9 %collective-permute-start.3 = (f32[20,2,1024]{2,1,0:T(2,128)S(1)}, f32[20,2,1024]{2,1,0:T(2,128)S(1)}, u32[]{:S(2)}, u32[]{:S(2)}) collective-permute-start(f32[20,2,1024]{2,1,0:T(2,128)S(1)} %get-tuple-element.10), channel_id=1, source_target_pairs={{1,0},{2,1},{3,2},{4,3},{5,4},{6,5},{7,6},{9,8},{10,9},{11,10},{12... | collective-permute-start | bytes 491528 | tf_op jit(solution)/shard_map/ppermute | solution.py:29
  54.5 6.6 %copy-start = (f32[256,1024]{1,0:T(8,128)S(1)}, f32[256,1024]{1,0:T(8,128)}, u32[]{:S(2)}) copy-start(f32[256,1024]{1,0:T(8,128)} %get-tuple-element.7) | copy-start | bytes 3145732
  68.4 1.0 %copy-start.1 = (f32[256,512]{1,0:T(8,128)S(1)}, f32[256,512]{1,0:T(8,128)}, u32[]{:S(2)}) copy-start(f32[256,512]{1,0:T(8,128)} %get-tuple-element.8) | copy-start | bytes 1572868

commit v8 on v7

--- a/solution.py
+++ b/solution.py
@@ -107,33 +107,40 @@
     )(mean_ext, gy_ext, banded)
 
 
-def gather_kernel(t_ref, got_ref, o_ref):
-    npts = o_ref.shape[0]
-    r = lax.broadcasted_iota(jnp.int32, (ZC, C), 0)
-    l = lax.broadcasted_iota(jnp.int32, (ZC, C), 1)
-    fold = (jnp.bitwise_and(r, C - 1) == l).astype(jnp.bfloat16)
+def gather_kernel(g_ref, d_ref, got_ref, o_ref, t_ref):
+    npts = got_ref.shape[0]
+    for x in range(XD):
+        start = (x + 2) * EY + 2
+        t_ref[pl.ds(x * YD, YD), :] = (g_ref[pl.ds(start, YD), :] / d_ref[pl.ds(x * YD, YD), :]).astype(t_ref.dtype)
+    r = lax.broadcasted_iota(jnp.int32, (C, ZC), 0)
+    l = lax.broadcasted_iota(jnp.int32, (C, ZC), 1)
+    fold = (jnp.bitwise_and(l, C - 1) == r).astype(jnp.bfloat16)
     lane_z = (lax.broadcasted_iota(jnp.int32, (TK, ZC), 1) >> 5).astype(jnp.float32)
     lane_xy = lax.broadcasted_iota(jnp.int32, (TK, XY), 1).astype(jnp.float32)
     table = t_ref[...]
+    block = o_ref.shape[2]
     for k in range(npts // TK):
         wide = got_ref[pl.ds(k * TK, TK), :].astype(jnp.float32)
         hot = (lane_xy == wide[:, 2 * C : 2 * C + 1]).astype(jnp.bfloat16)
         rows = jnp.dot(hot, table, preferred_element_type=jnp.float32)
         mask = lane_z == wide[:, 2 * C + 1 : 2 * C + 2]
         picked = jnp.where(mask, rows, 0.0).astype(jnp.bfloat16)
-        o_ref[pl.ds(k * TK, TK), :] = jnp.dot(picked, fold, preferred_element_type=jnp.float32).astype(o_ref.dtype)
-
-
-def gather_rows(table, got):
+        out = lax.dot_general(fold, picked, (((1,), (1,)), ((), ())), preferred_element_type=jnp.float32)
+        for j in range(TK // block):
+            o_ref[k * (TK // block) + j] = out[:, j * block : (j + 1) * block].astype(o_ref.dtype)
+
+
+def gather_rows(ggrid, divisor, got, parts):
     npts = got.shape[0]
     return pl.pallas_call(
         gather_kernel,
-        out_shape=jax.ShapeDtypeStruct((npts, C), jnp.bfloat16),
+        out_shape=jax.ShapeDtypeStruct((parts, C, npts // parts), jnp.bfloat16),
+        scratch_shapes=[pltpu.VMEM((XY, ZC), jnp.bfloat16)],
         cost_estimate=pl.CostEstimate(
             flops=2 * npts * XY * ZC + 2 * npts * ZC * C, transcendentals=0,
-            bytes_accessed=npts * C * 2 + XY * ZC * 2 + npts * PW * 2,
-        ),
-    )(table, got)
+            bytes_accessed=npts * C * 2 + ER * ZC * 4 + XY * ZC * 4 + npts * PW * 2,
+        ),
+    )(ggrid, divisor, got)
 
 
 def band_kernel(w_ref, wb_ref):
@@ -177,10 +184,10 @@
     mean_ext = wide[..., :ZC].astype(jnp.bfloat16).reshape(ER, ZC)
     gy_ext = wide[..., ZC:].reshape(ER, ZC)
     ggrid = conv_pair(mean_ext, gy_ext, banded_weights(kernel))
-    center = ggrid.reshape(EX, EY, ZC)[2 : 2 + XD, 2 : 2 + YD].reshape(XY, ZC)
-    table = (center / divisor).astype(jnp.bfloat16)
-    grads = gather_rows(table, got)
-    return lax.all_to_all(grads, "group", split_axis=0, concat_axis=0, tiled=True)
+    parts = lax.axis_size("group")
+    grads = gather_rows(ggrid, divisor, got, parts)
+    back = lax.all_to_all(grads, "group", split_axis=0, concat_axis=0, tiled=True)
+    return jnp.swapaxes(back, 1, 2).reshape(npts, C)
 
 
 def solution(mesh):

time: 92.8 us -> 91.1 us (0.982)
  local copies, waits for them, and re-layouts: 7.15 us -> 5.81 us
    all_to_all x2 -> x0, local copies, waits for them, and re-layouts: 1.88 us -> none  [per_device(): lax.all_to_all(grads, 'group', split_axis=0, concat_axis=0, tiled=True)]
where the time goes in v8:
time: 91.1 us; the launch traced here: 90.1 us
  blocking collectives  35.8 us (39%)
  Pallas kernels  22.2 us (24%)
  starting transfers between devices  17.2 us (19%)
  waiting for transfers between devices  6.47 us (7%)
  local copies, waits for them, and re-layouts  5.81 us (6%)
  other arithmetic  2.38 us (3%)
    all_to_all x1, blocking collectives, per_device(): lax.all_to_all(payload, 'group', split_axis=0, concat_axis=0, tiled=True)  19.5 us
    all_to_all x1, blocking collectives, per_device(): lax.all_to_all(grads, 'group', split_axis=0, concat_axis=0, tiled=True)  16.4 us
    ppermute x2, starting transfers between devices, extended(): after = lax.ppermute(first, axis, down)  13.7 us
    pallas_call x1, Pallas kernels, conv_pair(): pl.pallas_call(conv_kernel, out_shape=jax.ShapeDtypeStruct((ER, ZC), jnp....  6.65 us
    pallas_call x1, Pallas kernels, banded_weights(): pl.pallas_call(band_kernel, out_shape=jax.ShapeDtypeStruct((9, ZC, ZC), k...  6.62 us
    ppermute x2, waiting for transfers between devices, extended(): before = lax.ppermute(last, axis, up)  5.9 us
    pallas_call x1, Pallas kernels, scatter_sums(): pl.pallas_call(scatter_kernel, out_shape=(jax.ShapeDtypeStruct((XY, 2 * Z...  5.25 us
    pallas_call x1, Pallas kernels, gather_rows(): pl.pallas_call(gather_kernel, out_shape=jax.ShapeDtypeStruct((parts, C, n...  3.72 us
  transfers between devices with their start and end apart: 4, of which 2 were waited for; matrix products, arithmetic and copies ran while one was open for 0% of the time, Pallas kernels for 7%

profile of v8, /device:TPU:6, one launch (start us, length us, event | category | flops | bytes accessed | tf_op | source)
XLA Modules:
  0.0 90.1 jit_solution(12921281013057291362)
XLA Ops:
  0.0 0.7 select_convert_fusion
  0.7 0.9 %copy.20 = bf16[4,8,8,256]{3,2,1,0:T(8,128)(2,1)S(1)} copy(bf16[4,8,8,256]{3,1,2,0:T(8,128)(2,1)} %bitcast.24) | data formatting | bytes 262144
  1.7 0.9 %copy.21 = bf16[4,8,8,256]{3,2,1,0:T(8,128)(2,1)S(1)} copy(bf16[4,8,8,256]{3,1,2,0:T(8,128)(2,1)} %bitcast.25) | data formatting | bytes 262144
  2.6 0.1 pad_maximum_fusion.1
  2.7 0.1 copy.16
  2.7 19.5 %all_to_all.13 = bf16[8,256,66]{1,2,0:T(8,128)(2,1)S(1)} all-to-all(bf16[8,256,66]{1,2,0:T(8,128)(2,1)S(1)} %copy.16), channel_id=1, replica_groups=mesh['space'=96,'group'=8] {'group'}, dimensions={0} | all-to-all | bytes 540672 | tf_op jit(solution)/shard_map/all_to_all | solution.py:180
  22.2 1.0 %copy.17 = bf16[8,256,66]{2,1,0:T(8,128)(2,1)} copy(bf16[8,256,66]{1,2,0:T(8,128)(2,1)S(1)} %all_to_all.13) | data formatting | bytes 540672 | tf_op jit(solution)/shard_map/all_to_all | solution.py:180
  23.2 5.3 %shard_map.46 = (f32[256,1024]{1,0:T(8,128)}, f32[256,512]{1,0:T(8,128)}) custom-call(bf16[2048,66]{1,0:T(8,128)(2,1)} %bitcast.18), custom_call_target="tpu_custom_call" | custom-call | flops 1887436800 | bytes 1843200 | tf_op jit(solution)/shard_map/pallas_call | solution.py:67
  28.5 1.0 %fusion = (f32[32,1024]{1,0:T(8,128)S(1)}, f32[32,1024]{1,0:T(8,128)S(1)}) fusion(f32[256,1024]{1,0:T(8,128)} %get-tuple-element.7), kind=kLoop, calls=%fused_computation.8 | loop fusion | bytes 524288 | tf_op jit(solution)/shard_map/slice | solution.py:26
  29.5 12.4 %collective-permute-start.1 = (f32[2,16,1024]{2,1,0:T(8,128)S(1)}, f32[2,16,1024]{2,1,0:T(8,128)S(1)}, u32[]{:S(2)}, u32[]{:S(2)}) collective-permute-start(f32[2,16,1024]{2,1,0:T(8,128)S(1)} %bitcast.27), channel_id=1, source_target_pairs={{8,0},{16,8},{24,16},{32,24},{40,32},{48,40},{56,48},{64,56},{72,6... | collective-permute-start | bytes 393224 | tf_op jit(solution)/shard_map/ppermute | solution.py:29
  41.9 1.9 %collective-permute-start = (f32[2,16,1024]{2,1,0:T(8,128)S(1)}, f32[2,16,1024]{2,1,0:T(8,128)S(1)}, u32[]{:S(2)}, u32[]{:S(2)}) collective-permute-start(f32[2,16,1024]{2,1,0:T(8,128)S(1)} %bitcast.26), channel_id=1, source_target_pairs={{0,8},{8,16},{16,24},{24,32},{32,40},{40,48},{48,56},{56,64},{64,7... | collective-permute-start | bytes 393224 | tf_op jit(solution)/shard_map/ppermute | solution.py:28
  43.8 0.6 collective-permute-done.1
  44.4 5.9 %collective-permute-done = f32[2,16,1024]{2,1,0:T(8,128)S(1)} collective-permute-done((f32[2,16,1024]{2,1,0:T(8,128)S(1)}, f32[2,16,1024]{2,1,0:T(8,128)S(1)}, u32[]{:S(2)}, u32[]{:S(2)}) %collective-permute-start) | collective-permute-done | bytes 131104 | tf_op jit(solution)/shard_map/ppermute | solution.py:28
  50.3 1.3 %pad_maximum_fusion.4 = (f32[20,2,1024]{2,1,0:T(2,128)S(1)}, f32[20,2,1024]{2,1,0:T(2,128)S(1)}) fusion(f32[2,16,1024]{2,1,0:T(8,128)S(1)} %collective-permute-done.1, f32[16,16,1024]{2,1,0:T(8,128)} %bitcast.16, f32[2,16,1024]{2,1,0:T(8,128)S(1)} %collective-permute-done), kind=kLoop, calls=%fused_computation.5 | loop fusion | flops 163840 | bytes 1638400 | tf_op jit(solution)/shard_map/slice | solution.py:26
  51.6 1.6 %collective-permute-start.2 = (f32[20,2,1024]{2,1,0:T(2,128)S(1)}, f32[20,2,1024]{2,1,0:T(2,128)S(1)}, u32[]{:S(2)}, u32[]{:S(2)}) collective-permute-start(f32[20,2,1024]{2,1,0:T(2,128)S(1)} %get-tuple-element.9), channel_id=1, source_target_pairs={{0,1},{1,2},{2,3},{3,4},{4,5},{5,6},{6,7},{8,9},{9,10},{10,11},{11... | collective-permute-start | bytes 491528 | tf_op jit(solution)/shard_map/ppermute | solution.py:28
  53.2 1.3 %collective-permute-start.3 = (f32[20,2,1024]{2,1,0:T(2,128)S(1)}, f32[20,2,1024]{2,1,0:T(2,128)S(1)}, u32[]{:S(2)}, u32[]{:S(2)}) collective-permute-start(f32[20,2,1024]{2,1,0:T(2,128)S(1)} %get-tuple-element.10), channel_id=1, source_target_pairs={{1,0},{2,1},{3,2},{4,3},{5,4},{6,5},{7,6},{9,8},{10,9},{11,10},{12... | collective-permute-start | bytes 491528 | tf_op jit(solution)/shard_map/ppermute | solution.py:29
  54.5 0.0 copy-start.1
  54.5 6.6 %shard_map.47.w_ref = bf16[9,512,512]{2,1,0:T(8,128)(2,1)} custom-call(bf16[27,32,32]{2,1,0:T(8,128)(2,1)} %bitcast.23), custom_call_target="tpu_custom_call" | custom-call | flops 905969664 | bytes 4718592 | tf_op jit(solution)/shard_map/pallas_call | solution.py:162
  61.1 0.0 collective-permute-done.2
  61.1 0.0 collective-permute-done.3
  61.1 0.0 copy-done.1
  61.1 0.3 pad_maximum_fusion
  61.4 0.1 slice.36
  61.5 0.1 slice.34
  61.6 0.1 reshape.27.g_ref
  61.7 0.1 reshape.26.m_ref
  61.8 6.7 %shard_map.48.g_ref = f32[400,512]{1,0:T(8,128)S(1)} custom-call(bf16[400,512]{1,0:T(8,128)(2,1)S(1)} %reshape.26.m_ref, f32[400,512]{1,0:T(8,128)S(1)} %reshape.27.g_ref, bf16[9,512,512]{2,1,0:T(8,128)(2,1)} %shard_map.47.w_ref), custom_call_target="tpu_custom_call" | custom-call | flops 3774873600 | bytes 6766592 | tf_op jit(solution)/shard_map/pallas_call | solution.py:99
  68.4 0.0 copy-start
  68.4 0.9 copy-done
  69.3 3.7 %shard_map.49 = bf16[8,32,256]{2,1,0:T(8,128)(2,1)} custom-call(f32[400,512]{1,0:T(8,128)} %copy-done, f32[256,512]{1,0:T(8,128)} %get-tuple-element.8.d_ref, bf16[2048,66]{1,0:T(8,128)(2,1)} %bitcast.19), custom_call_target="tpu_custom_call" | custom-call | flops 603979776 | bytes 1744896 | tf_op jit(solution)/shard_map/pallas_call | solution.py:135
  73.1 16.4 %all_to_all.14 = bf16[8,32,256]{2,1,0:T(8,128)(2,1)S(1)} all-to-all(bf16[8,32,256]{2,1,0:T(8,128)(2,1)} %shard_map.49), channel_id=1, replica_groups=mesh['space'=96,'group'=8] {'group'}, dimensions={0} | all-to-all | bytes 262144 | tf_op jit(solution)/shard_map/all_to_all | solution.py:189
  89.4 0.7 copy.19
  (2 shorter events, 0.0 us)
Async XLA Ops:
  29.5 14.9 %collective-permute-start.1 = (f32[2,16,1024]{2,1,0:T(8,128)S(1)}, f32[2,16,1024]{2,1,0:T(8,128)S(1)}, u32[]{:S(2)}, u32[]{:S(2)}) collective-permute-start(f32[2,16,1024]{2,1,0:T(8,128)S(1)} %bitcast.27), channel_id=1, source_target_pairs={{8,0},{16,8},{24,16},{32,24},{40,32},{48,40},{56,48},{64,56},{72,6... | collective-permute-start | bytes 393224 | tf_op jit(solution)/shard_map/ppermute | solution.py:29
  41.9 8.4 %collective-permute-start = (f32[2,16,1024]{2,1,0:T(8,128)S(1)}, f32[2,16,1024]{2,1,0:T(8,128)S(1)}, u32[]{:S(2)}, u32[]{:S(2)}) collective-permute-start(f32[2,16,1024]{2,1,0:T(8,128)S(1)} %bitcast.26), channel_id=1, source_target_pairs={{0,8},{8,16},{16,24},{24,32},{32,40},{40,48},{48,56},{56,64},{64,7... | collective-permute-start | bytes 393224 | tf_op jit(solution)/shard_map/ppermute | solution.py:28
  51.6 9.5 %collective-permute-start.2 = (f32[20,2,1024]{2,1,0:T(2,128)S(1)}, f32[20,2,1024]{2,1,0:T(2,128)S(1)}, u32[]{:S(2)}, u32[]{:S(2)}) collective-permute-start(f32[20,2,1024]{2,1,0:T(2,128)S(1)} %get-tuple-element.9), channel_id=1, source_target_pairs={{0,1},{1,2},{2,3},{3,4},{4,5},{5,6},{6,7},{8,9},{9,10},{10,11},{11... | collective-permute-start | bytes 491528 | tf_op jit(solution)/shard_map/ppermute | solution.py:28
  53.2 7.9 %collective-permute-start.3 = (f32[20,2,1024]{2,1,0:T(2,128)S(1)}, f32[20,2,1024]{2,1,0:T(2,128)S(1)}, u32[]{:S(2)}, u32[]{:S(2)}) collective-permute-start(f32[20,2,1024]{2,1,0:T(2,128)S(1)} %get-tuple-element.10), channel_id=1, source_target_pairs={{1,0},{2,1},{3,2},{4,3},{5,4},{6,5},{7,6},{9,8},{10,9},{11,10},{12... | collective-permute-start | bytes 491528 | tf_op jit(solution)/shard_map/ppermute | solution.py:29
  54.5 6.6 %copy-start.1 = (f32[256,1024]{1,0:T(8,128)S(1)}, f32[256,1024]{1,0:T(8,128)}, u32[]{:S(2)}) copy-start(f32[256,1024]{1,0:T(8,128)} %get-tuple-element.7) | copy-start | bytes 3145732
  68.4 0.9 copy-start

commit v9 on v8

--- a/solution.py
+++ b/solution.py
@@ -74,12 +74,16 @@
     )(got)
 
 
-def conv_kernel(m_ref, g_ref, w_ref, o_ref):
+def conv_kernel(m_ref, g_ref, w_hbm, o_ref, w_ref, sems):
+    copies = [pltpu.make_async_copy(w_hbm.at[t], w_ref.at[t], sems.at[t]) for t in range(9)]
+    for cp in copies:
+        cp.start()
     mean = m_ref[...]
     acc = jnp.zeros((ER, ZC), jnp.float32)
     for a in range(3):
         for b in range(3):
             off = (a - 1) * EY + (b - 1)
+            copies[a * 3 + b].wait()
             part = jnp.dot(mean, w_ref[a * 3 + b], preferred_element_type=jnp.float32)
             acc = acc + pltpu.roll(part, (-off) % ER, 0)
     sig = 1.0 / (1.0 + jnp.exp(-acc))
@@ -96,9 +100,13 @@
 
 
 def conv_pair(mean_ext, gy_ext, banded):
+    vmem = pl.BlockSpec(memory_space=pltpu.VMEM)
     return pl.pallas_call(
         conv_kernel,
         out_shape=jax.ShapeDtypeStruct((ER, ZC), jnp.float32),
+        in_specs=[vmem, vmem, pl.BlockSpec(memory_space=pl.ANY)],
+        out_specs=vmem,
+        scratch_shapes=[pltpu.VMEM((9, ZC, ZC), jnp.bfloat16), pltpu.SemaphoreType.DMA((9,))],
         compiler_params=pltpu.CompilerParams(vmem_limit_bytes=48 * 1024 * 1024),
         cost_estimate=pl.CostEstimate(
             flops=18 * 2 * ER * ZC * ZC, transcendentals=ER * ZC,

time: 91.1 us -> 91.2 us (level)
  no operation moved by 1% of the time
where the time goes in v9:
time: 91.2 us; the launch traced here: 90.2 us
  blocking collectives  35.8 us (39%)
  Pallas kernels  22.4 us (25%)
  starting transfers between devices  17.2 us (19%)
  waiting for transfers between devices  6.47 us (7%)
  local copies, waits for them, and re-layouts  5.81 us (6%)
  other arithmetic  2.38 us (3%)
    all_to_all x1, blocking collectives, per_device(): lax.all_to_all(payload, 'group', split_axis=0, concat_axis=0, tiled=True)  19.5 us
    all_to_all x1, blocking collectives, per_device(): lax.all_to_all(grads, 'group', split_axis=0, concat_axis=0, tiled=True)  16.4 us
    ppermute x2, starting transfers between devices, extended(): after = lax.ppermute(first, axis, down)  13.7 us
    pallas_call x1, Pallas kernels, conv_pair(): pl.pallas_call(conv_kernel, out_shape=jax.ShapeDtypeStruct((ER, ZC), jnp....  6.79 us
    pallas_call x1, Pallas kernels, banded_weights(): pl.pallas_call(band_kernel, out_shape=jax.ShapeDtypeStruct((9, ZC, ZC), k...  6.62 us
    ppermute x2, waiting for transfers between devices, extended(): before = lax.ppermute(last, axis, up)  5.9 us
    pallas_call x1, Pallas kernels, scatter_sums(): pl.pallas_call(scatter_kernel, out_shape=(jax.ShapeDtypeStruct((XY, 2 * Z...  5.25 us
    pallas_call x1, Pallas kernels, gather_rows(): pl.pallas_call(gather_kernel, out_shape=jax.ShapeDtypeStruct((parts, C, n...  3.72 us
  transfers between devices with their start and end apart: 4, of which 2 were waited for; matrix products, arithmetic and copies ran while one was open for 0% of the time, Pallas kernels for 7%

profile of v9, /device:TPU:6, one launch (start us, length us, event | category | flops | bytes accessed | tf_op | source)
XLA Modules:
  0.0 90.2 jit_solution(577120547446136168)
XLA Ops:
  0.0 0.7 select_convert_fusion
  0.7 0.9 %copy.20 = bf16[4,8,8,256]{3,2,1,0:T(8,128)(2,1)S(1)} copy(bf16[4,8,8,256]{3,1,2,0:T(8,128)(2,1)} %bitcast.24) | data formatting | bytes 262144
  1.7 0.9 %copy.21 = bf16[4,8,8,256]{3,2,1,0:T(8,128)(2,1)S(1)} copy(bf16[4,8,8,256]{3,1,2,0:T(8,128)(2,1)} %bitcast.25) | data formatting | bytes 262144
  2.6 0.1 pad_maximum_fusion.1
  2.7 0.1 copy.16
  2.7 19.5 %all_to_all.13 = bf16[8,256,66]{1,2,0:T(8,128)(2,1)S(1)} all-to-all(bf16[8,256,66]{1,2,0:T(8,128)(2,1)S(1)} %copy.16), channel_id=1, replica_groups=mesh['space'=96,'group'=8] {'group'}, dimensions={0} | all-to-all | bytes 540672 | tf_op jit(solution)/shard_map/all_to_all | solution.py:188
  22.2 1.0 %copy.17 = bf16[8,256,66]{2,1,0:T(8,128)(2,1)} copy(bf16[8,256,66]{1,2,0:T(8,128)(2,1)S(1)} %all_to_all.13) | data formatting | bytes 540672 | tf_op jit(solution)/shard_map/all_to_all | solution.py:188
  23.2 5.3 %shard_map.46 = (f32[256,1024]{1,0:T(8,128)}, f32[256,512]{1,0:T(8,128)}) custom-call(bf16[2048,66]{1,0:T(8,128)(2,1)} %bitcast.18), custom_call_target="tpu_custom_call" | custom-call | flops 1887436800 | bytes 1843200 | tf_op jit(solution)/shard_map/pallas_call | solution.py:67
  28.5 1.0 %fusion = (f32[32,1024]{1,0:T(8,128)S(1)}, f32[32,1024]{1,0:T(8,128)S(1)}) fusion(f32[256,1024]{1,0:T(8,128)} %get-tuple-element.7), kind=kLoop, calls=%fused_computation.8 | loop fusion | bytes 524288 | tf_op jit(solution)/shard_map/slice | solution.py:26
  29.5 12.4 %collective-permute-start.1 = (f32[2,16,1024]{2,1,0:T(8,128)S(1)}, f32[2,16,1024]{2,1,0:T(8,128)S(1)}, u32[]{:S(2)}, u32[]{:S(2)}) collective-permute-start(f32[2,16,1024]{2,1,0:T(8,128)S(1)} %bitcast.27), channel_id=1, source_target_pairs={{8,0},{16,8},{24,16},{32,24},{40,32},{48,40},{56,48},{64,56},{72,6... | collective-permute-start | bytes 393224 | tf_op jit(solution)/shard_map/ppermute | solution.py:29
  41.9 1.9 %collective-permute-start = (f32[2,16,1024]{2,1,0:T(8,128)S(1)}, f32[2,16,1024]{2,1,0:T(8,128)S(1)}, u32[]{:S(2)}, u32[]{:S(2)}) collective-permute-start(f32[2,16,1024]{2,1,0:T(8,128)S(1)} %bitcast.26), channel_id=1, source_target_pairs={{0,8},{8,16},{16,24},{24,32},{32,40},{40,48},{48,56},{56,64},{64,7... | collective-permute-start | bytes 393224 | tf_op jit(solution)/shard_map/ppermute | solution.py:28
  43.8 0.6 collective-permute-done.1
  44.4 5.9 %collective-permute-done = f32[2,16,1024]{2,1,0:T(8,128)S(1)} collective-permute-done((f32[2,16,1024]{2,1,0:T(8,128)S(1)}, f32[2,16,1024]{2,1,0:T(8,128)S(1)}, u32[]{:S(2)}, u32[]{:S(2)}) %collective-permute-start) | collective-permute-done | bytes 131104 | tf_op jit(solution)/shard_map/ppermute | solution.py:28
  50.3 1.3 %pad_maximum_fusion.4 = (f32[20,2,1024]{2,1,0:T(2,128)S(1)}, f32[20,2,1024]{2,1,0:T(2,128)S(1)}) fusion(f32[2,16,1024]{2,1,0:T(8,128)S(1)} %collective-permute-done.1, f32[16,16,1024]{2,1,0:T(8,128)} %bitcast.16, f32[2,16,1024]{2,1,0:T(8,128)S(1)} %collective-permute-done), kind=kLoop, calls=%fused_computation.5 | loop fusion | flops 163840 | bytes 1638400 | tf_op jit(solution)/shard_map/slice | solution.py:26
  51.6 1.6 %collective-permute-start.2 = (f32[20,2,1024]{2,1,0:T(2,128)S(1)}, f32[20,2,1024]{2,1,0:T(2,128)S(1)}, u32[]{:S(2)}, u32[]{:S(2)}) collective-permute-start(f32[20,2,1024]{2,1,0:T(2,128)S(1)} %get-tuple-element.9), channel_id=1, source_target_pairs={{0,1},{1,2},{2,3},{3,4},{4,5},{5,6},{6,7},{8,9},{9,10},{10,11},{11... | collective-permute-start | bytes 491528 | tf_op jit(solution)/shard_map/ppermute | solution.py:28
  53.2 1.3 %collective-permute-start.3 = (f32[20,2,1024]{2,1,0:T(2,128)S(1)}, f32[20,2,1024]{2,1,0:T(2,128)S(1)}, u32[]{:S(2)}, u32[]{:S(2)}) collective-permute-start(f32[20,2,1024]{2,1,0:T(2,128)S(1)} %get-tuple-element.10), channel_id=1, source_target_pairs={{1,0},{2,1},{3,2},{4,3},{5,4},{6,5},{7,6},{9,8},{10,9},{11,10},{12... | collective-permute-start | bytes 491528 | tf_op jit(solution)/shard_map/ppermute | solution.py:29
  54.5 0.0 copy-start.1
  54.5 6.6 %shard_map.47.w_hbm = bf16[9,512,512]{2,1,0:T(8,128)(2,1)} custom-call(bf16[27,32,32]{2,1,0:T(8,128)(2,1)} %bitcast.23), custom_call_target="tpu_custom_call" | custom-call | flops 905969664 | bytes 4718592 | tf_op jit(solution)/shard_map/pallas_call | solution.py:170
  61.1 0.0 collective-permute-done.2
  61.1 0.0 collective-permute-done.3
  61.1 0.0 copy-done.1
  61.1 0.3 pad_maximum_fusion
  61.4 0.1 slice.36
  61.5 0.1 slice.34
  61.6 0.1 reshape.27.g_ref
  61.7 0.1 reshape.26.m_ref
  61.8 6.8 %shard_map.48.g_ref = f32[400,512]{1,0:T(8,128)S(1)} custom-call(bf16[400,512]{1,0:T(8,128)(2,1)S(1)} %reshape.26.m_ref, f32[400,512]{1,0:T(8,128)S(1)} %reshape.27.g_ref, bf16[9,512,512]{2,1,0:T(8,128)(2,1)} %shard_map.47.w_hbm), custom_call_target="tpu_custom_call" | custom-call | flops 3774873600 | bytes 6766592 | tf_op jit(solution)/shard_map/pallas_call | solution.py:104
  68.6 0.0 copy-start
  68.6 0.9 copy-done
  69.5 3.7 %shard_map.49 = bf16[8,32,256]{2,1,0:T(8,128)(2,1)} custom-call(f32[400,512]{1,0:T(8,128)} %copy-done, f32[256,512]{1,0:T(8,128)} %get-tuple-element.8.d_ref, bf16[2048,66]{1,0:T(8,128)(2,1)} %bitcast.19), custom_call_target="tpu_custom_call" | custom-call | flops 603979776 | bytes 1744896 | tf_op jit(solution)/shard_map/pallas_call | solution.py:143
  73.2 16.4 %all_to_all.14 = bf16[8,32,256]{2,1,0:T(8,128)(2,1)S(1)} all-to-all(bf16[8,32,256]{2,1,0:T(8,128)(2,1)} %shard_map.49), channel_id=1, replica_groups=mesh['space'=96,'group'=8] {'group'}, dimensions={0} | all-to-all | bytes 262144 | tf_op jit(solution)/shard_map/all_to_all | solution.py:197
  89.6 0.7 copy.19
  (2 shorter events, 0.0 us)
Async XLA Ops:
  29.5 14.9 %collective-permute-start.1 = (f32[2,16,1024]{2,1,0:T(8,128)S(1)}, f32[2,16,1024]{2,1,0:T(8,128)S(1)}, u32[]{:S(2)}, u32[]{:S(2)}) collective-permute-start(f32[2,16,1024]{2,1,0:T(8,128)S(1)} %bitcast.27), channel_id=1, source_target_pairs={{8,0},{16,8},{24,16},{32,24},{40,32},{48,40},{56,48},{64,56},{72,6... | collective-permute-start | bytes 393224 | tf_op jit(solution)/shard_map/ppermute | solution.py:29
  41.9 8.4 %collective-permute-start = (f32[2,16,1024]{2,1,0:T(8,128)S(1)}, f32[2,16,1024]{2,1,0:T(8,128)S(1)}, u32[]{:S(2)}, u32[]{:S(2)}) collective-permute-start(f32[2,16,1024]{2,1,0:T(8,128)S(1)} %bitcast.26), channel_id=1, source_target_pairs={{0,8},{8,16},{16,24},{24,32},{32,40},{40,48},{48,56},{56,64},{64,7... | collective-permute-start | bytes 393224 | tf_op jit(solution)/shard_map/ppermute | solution.py:28
  51.6 9.5 %collective-permute-start.2 = (f32[20,2,1024]{2,1,0:T(2,128)S(1)}, f32[20,2,1024]{2,1,0:T(2,128)S(1)}, u32[]{:S(2)}, u32[]{:S(2)}) collective-permute-start(f32[20,2,1024]{2,1,0:T(2,128)S(1)} %get-tuple-element.9), channel_id=1, source_target_pairs={{0,1},{1,2},{2,3},{3,4},{4,5},{5,6},{6,7},{8,9},{9,10},{10,11},{11... | collective-permute-start | bytes 491528 | tf_op jit(solution)/shard_map/ppermute | solution.py:28
  53.2 7.9 %collective-permute-start.3 = (f32[20,2,1024]{2,1,0:T(2,128)S(1)}, f32[20,2,1024]{2,1,0:T(2,128)S(1)}, u32[]{:S(2)}, u32[]{:S(2)}) collective-permute-start(f32[20,2,1024]{2,1,0:T(2,128)S(1)} %get-tuple-element.10), channel_id=1, source_target_pairs={{1,0},{2,1},{3,2},{4,3},{5,4},{6,5},{7,6},{9,8},{10,9},{11,10},{12... | collective-permute-start | bytes 491528 | tf_op jit(solution)/shard_map/ppermute | solution.py:29
  54.5 6.6 %copy-start.1 = (f32[256,1024]{1,0:T(8,128)S(1)}, f32[256,1024]{1,0:T(8,128)}, u32[]{:S(2)}) copy-start(f32[256,1024]{1,0:T(8,128)} %get-tuple-element.7) | copy-start | bytes 3145732
  68.6 0.9 copy-start

commit v10 on v8

--- a/solution.py
+++ b/solution.py
@@ -31,7 +31,7 @@
     return shard
 
 
-def scatter_kernel(got_ref, field_ref, div_ref):
+def scatter_kernel(got_ref, field_ref, lo_ref, hi_ref, div_ref):
     npts = got_ref.shape[0]
     r = lax.broadcasted_iota(jnp.int32, (PW, ZC), 0)
     l = lax.broadcasted_iota(jnp.int32, (PW, ZC), 1)
@@ -57,8 +57,14 @@
         sc = sc + lax.dot_general(hot, qc, over_points, preferred_element_type=jnp.float32)
         sn = sn + lax.dot_general(hot, qn, over_points, preferred_element_type=jnp.float32)
     div = jnp.maximum(sn, 1.0)
-    field_ref[:, :ZC] = (sf / div).astype(jnp.bfloat16).astype(jnp.float32)
+    mean = (sf / div).astype(jnp.bfloat16).astype(jnp.float32)
+    field_ref[:, :ZC] = mean
     field_ref[:, ZC:] = sc
+    face = lo_ref.shape[0]
+    lo_ref[:, :ZC] = mean[:face]
+    lo_ref[:, ZC:] = sc[:face]
+    hi_ref[:, :ZC] = mean[XY - face :]
+    hi_ref[:, ZC:] = sc[XY - face :]
     div_ref[...] = div
 
 
@@ -66,7 +72,12 @@
     npts = got.shape[0]
     return pl.pallas_call(
         scatter_kernel,
-        out_shape=(jax.ShapeDtypeStruct((XY, 2 * ZC), jnp.float32), jax.ShapeDtypeStruct((XY, ZC), jnp.float32)),
+        out_shape=(
+            jax.ShapeDtypeStruct((XY, 2 * ZC), jnp.float32),
+            jax.ShapeDtypeStruct((2 * YD, 2 * ZC), jnp.float32),
+            jax.ShapeDtypeStruct((2 * YD, 2 * ZC), jnp.float32),
+            jax.ShapeDtypeStruct((XY, ZC), jnp.float32),
+        ),
         cost_estimate=pl.CostEstimate(
             flops=2 * XY * npts * ZC * 3 + 4 * npts * PW * ZC, transcendentals=0,
             bytes_accessed=npts * PW * 2 + 3 * XY * ZC * 4,
@@ -178,9 +189,14 @@
     z_send = jnp.bitwise_and(point_voxel, ZB - 1).astype(jnp.bfloat16)
     payload = jnp.concatenate([point_feats, cotangent, xy_send[:, None], z_send[:, None]], axis=1)
     got = lax.all_to_all(payload, "group", split_axis=0, concat_axis=0, tiled=True)
-    field, divisor = scatter_sums(got)
+    field, lo, hi, divisor = scatter_sums(got)
     field = field.reshape(XD, YD, 2 * ZC)
-    wide = extended(field, (("space", 0), ("group", 1)), 2)
+    size = lax.axis_size("space")
+    up = [(i, i + 1) for i in range(size - 1)]
+    down = [(j, i) for i, j in up]
+    before = lax.ppermute(hi.reshape(2, YD, 2 * ZC), "space", up)
+    after = lax.ppermute(lo.reshape(2, YD, 2 * ZC), "space", down)
+    wide = extended(jnp.concatenate([before, field, after], axis=0), (("group", 1),), 2)
     mean_ext = wide[..., :ZC].astype(jnp.bfloat16).reshape(ER, ZC)
     gy_ext = wide[..., ZC:].reshape(ER, ZC)
     ggrid = conv_pair(mean_ext, gy_ext, banded_weights(kernel))

time: 91.1 us -> 86.4 us (0.948)
  waiting for transfers between devices: 6.47 us -> 2.82 us
  local copies, waits for them, and re-layouts: 5.81 us -> 4.81 us
    ppermute x0 -> x2, starting transfers between devices: none -> 14.3 us  [the longest x1 12.4 us: per_device(): after = lax.ppermute(lo.reshape(2, YD, 2 * ZC), 'space', down)]
    ppermute x2 -> x1, starting transfers between devices: 13.7 us -> 1.29 us  [extended(): after = lax.ppermute(first, axis, down)]
    ppermute x2 -> x1, waiting for transfers between devices: 5.9 us -> 0.01 us  [extended(): before = lax.ppermute(last, axis, up)]
    ppermute x0 -> x2, waiting for transfers between devices: none -> 2.81 us  [the longest x1 1.9 us: per_device(): after = lax.ppermute(lo.reshape(2, YD, 2 * ZC), 'space', down)]
    ppermute x2 -> x1, starting transfers between devices: 3.51 us -> 1.6 us  [extended(): before = lax.ppermute(last, axis, up)]
    slice x1 -> x0, local copies, waits for them, and re-layouts: 0.99 us -> none  [extended(): last = lax.slice_in_dim(shard, length - width, length, axis=dim)]
  transfers between devices with their start and end apart: 4 -> 4, of which waited for: 2 -> 2; matrix products, arithmetic and copies ran while one was open for 0% -> 0% of each run, Pallas kernels for 7% -> 8%
where the time goes in v10:
time: 86.4 us; the launch traced here: 85.4 us
  blocking collectives  35.8 us (41%)
  Pallas kernels  22.3 us (26%)
  starting transfers between devices  17.2 us (20%)
  local copies, waits for them, and re-layouts  4.81 us (6%)
  waiting for transfers between devices  2.82 us (3%)
  other arithmetic  2.38 us (3%)
    all_to_all x1, blocking collectives, per_device(): lax.all_to_all(payload, 'group', split_axis=0, concat_axis=0, tiled=True)  19.5 us
    all_to_all x1, blocking collectives, per_device(): lax.all_to_all(grads, 'group', split_axis=0, concat_axis=0, tiled=True)  16.3 us
    ppermute x1, starting transfers between devices, per_device(): after = lax.ppermute(lo.reshape(2, YD, 2 * ZC), 'space', down)  12.4 us
    pallas_call x1, Pallas kernels, conv_pair(): pl.pallas_call(conv_kernel, out_shape=jax.ShapeDtypeStruct((ER, ZC), jnp....  6.65 us
    pallas_call x1, Pallas kernels, banded_weights(): pl.pallas_call(band_kernel, out_shape=jax.ShapeDtypeStruct((9, ZC, ZC), k...  6.64 us
    pallas_call x1, Pallas kernels, scatter_sums(): pl.pallas_call(scatter_kernel, out_shape=(jax.ShapeDtypeStruct((XY, 2 * Z...  5.24 us
    pallas_call x1, Pallas kernels, gather_rows(): pl.pallas_call(gather_kernel, out_shape=jax.ShapeDtypeStruct((parts, C, n...  3.72 us
    unnamed x6, local copies, waits for them, and re-layouts  2.75 us
  transfers between devices with their start and end apart: 4, of which 2 were waited for; matrix products, arithmetic and copies ran while one was open for 0% of the time, Pallas kernels for 8%

profile of v10, /device:TPU:6, one launch (start us, length us, event | category | flops | bytes accessed | tf_op | source)
XLA Modules:
  0.0 85.4 jit_solution(18197306766415664209)
XLA Ops:
  0.0 0.7 select_convert_fusion
  0.7 0.9 %copy.20 = bf16[4,8,8,256]{3,2,1,0:T(8,128)(2,1)S(1)} copy(bf16[4,8,8,256]{3,1,2,0:T(8,128)(2,1)} %bitcast.24) | data formatting | bytes 262144
  1.7 0.9 %copy.21 = bf16[4,8,8,256]{3,2,1,0:T(8,128)(2,1)S(1)} copy(bf16[4,8,8,256]{3,1,2,0:T(8,128)(2,1)} %bitcast.25) | data formatting | bytes 262144
  2.6 0.1 pad_maximum_fusion.1
  2.7 0.1 copy.16
  2.7 19.5 %all_to_all.13 = bf16[8,256,66]{1,2,0:T(8,128)(2,1)S(1)} all-to-all(bf16[8,256,66]{1,2,0:T(8,128)(2,1)S(1)} %copy.16), channel_id=1, replica_groups=mesh['space'=96,'group'=8] {'group'}, dimensions={0} | all-to-all | bytes 540672 | tf_op jit(solution)/shard_map/all_to_all | solution.py:191
  22.2 1.0 %copy.17 = bf16[8,256,66]{2,1,0:T(8,128)(2,1)} copy(bf16[8,256,66]{1,2,0:T(8,128)(2,1)S(1)} %all_to_all.13) | data formatting | bytes 540672 | tf_op jit(solution)/shard_map/all_to_all | solution.py:191
  23.2 5.2 %shard_map.46 = (f32[256,1024]{1,0:T(8,128)}, f32[32,1024]{1,0:T(8,128)}, f32[32,1024]{1,0:T(8,128)}, f32[256,512]{1,0:T(8,128)}) custom-call(bf16[2048,66]{1,0:T(8,128)(2,1)} %bitcast.18), custom_call_target="tpu_custom_call" | custom-call | flops 1887436800 | bytes 1843200 | tf_op jit(solution)/shard_map/pallas_call | solution.py:73
  28.5 1.9 %collective-permute-start = (f32[2,16,1024]{2,1,0:T(8,128)}, f32[2,16,1024]{2,1,0:T(8,128)S(1)}, u32[]{:S(2)}, u32[]{:S(2)}) collective-permute-start(f32[2,16,1024]{2,1,0:T(8,128)} %bitcast.27), channel_id=1, source_target_pairs={{0,8},{8,16},{16,24},{24,32},{32,40},{40,48},{48,56},{56,64},{64,7... | collective-permute-start | bytes 393224 | tf_op jit(solution)/shard_map/ppermute | solution.py:197
  30.4 12.4 %collective-permute-start.1 = (f32[2,16,1024]{2,1,0:T(8,128)}, f32[2,16,1024]{2,1,0:T(8,128)S(1)}, u32[]{:S(2)}, u32[]{:S(2)}) collective-permute-start(f32[2,16,1024]{2,1,0:T(8,128)} %bitcast.26), channel_id=1, source_target_pairs={{8,0},{16,8},{24,16},{32,24},{40,32},{48,40},{56,48},{64,56},{72,6... | collective-permute-start | bytes 393224 | tf_op jit(solution)/shard_map/ppermute | solution.py:198
  42.8 0.9 %collective-permute-done = f32[2,16,1024]{2,1,0:T(8,128)S(1)} collective-permute-done((f32[2,16,1024]{2,1,0:T(8,128)}, f32[2,16,1024]{2,1,0:T(8,128)S(1)}, u32[]{:S(2)}, u32[]{:S(2)}) %collective-permute-start) | collective-permute-done | bytes 131104 | tf_op jit(solution)/shard_map/ppermute | solution.py:197
  43.7 1.9 %collective-permute-done.1 = f32[2,16,1024]{2,1,0:T(8,128)S(1)} collective-permute-done((f32[2,16,1024]{2,1,0:T(8,128)}, f32[2,16,1024]{2,1,0:T(8,128)S(1)}, u32[]{:S(2)}, u32[]{:S(2)}) %collective-permute-start.1) | collective-permute-done | bytes 131104 | tf_op jit(solution)/shard_map/ppermute | solution.py:198
  45.6 1.3 %pad_maximum_fusion.4 = (f32[20,2,1024]{2,1,0:T(2,128)S(1)}, f32[20,2,1024]{2,1,0:T(2,128)S(1)}) fusion(f32[2,16,1024]{2,1,0:T(8,128)S(1)} %collective-permute-done.1, f32[16,16,1024]{2,1,0:T(8,128)} %bitcast.16, f32[2,16,1024]{2,1,0:T(8,128)S(1)} %collective-permute-done), kind=kLoop, calls=%fused_computation.5 | loop fusion | flops 163840 | bytes 1638400 | tf_op jit(solution)/shard_map/slice | solution.py:26
  46.9 1.6 %collective-permute-start.2 = (f32[20,2,1024]{2,1,0:T(2,128)S(1)}, f32[20,2,1024]{2,1,0:T(2,128)S(1)}, u32[]{:S(2)}, u32[]{:S(2)}) collective-permute-start(f32[20,2,1024]{2,1,0:T(2,128)S(1)} %get-tuple-element.13), channel_id=1, source_target_pairs={{0,1},{1,2},{2,3},{3,4},{4,5},{5,6},{6,7},{8,9},{9,10},{10,11},{11... | collective-permute-start | bytes 491528 | tf_op jit(solution)/shard_map/ppermute | solution.py:28
  48.5 1.3 %collective-permute-start.3 = (f32[20,2,1024]{2,1,0:T(2,128)S(1)}, f32[20,2,1024]{2,1,0:T(2,128)S(1)}, u32[]{:S(2)}, u32[]{:S(2)}) collective-permute-start(f32[20,2,1024]{2,1,0:T(2,128)S(1)} %get-tuple-element.14), channel_id=1, source_target_pairs={{1,0},{2,1},{3,2},{4,3},{5,4},{6,5},{7,6},{9,8},{10,9},{11,10},{12... | collective-permute-start | bytes 491528 | tf_op jit(solution)/shard_map/ppermute | solution.py:29
  49.8 0.0 copy-start.1
  49.8 6.6 %shard_map.47.w_ref = bf16[9,512,512]{2,1,0:T(8,128)(2,1)} custom-call(bf16[27,32,32]{2,1,0:T(8,128)(2,1)} %bitcast.23), custom_call_target="tpu_custom_call" | custom-call | flops 905969664 | bytes 4718592 | tf_op jit(solution)/shard_map/pallas_call | solution.py:173
  56.5 0.0 collective-permute-done.2
  56.5 0.0 collective-permute-done.3
  56.5 0.0 copy-done.1
  56.5 0.3 pad_maximum_fusion
  56.8 0.1 slice.20
  56.9 0.1 slice.18
  57.0 0.1 reshape.33.g_ref
  57.0 0.1 reshape.32.m_ref
  57.1 6.7 %shard_map.48.g_ref = f32[400,512]{1,0:T(8,128)S(1)} custom-call(bf16[400,512]{1,0:T(8,128)(2,1)S(1)} %reshape.32.m_ref, f32[400,512]{1,0:T(8,128)S(1)} %reshape.33.g_ref, bf16[9,512,512]{2,1,0:T(8,128)(2,1)} %shard_map.47.w_ref), custom_call_target="tpu_custom_call" | custom-call | flops 3774873600 | bytes 6766592 | tf_op jit(solution)/shard_map/pallas_call | solution.py:110
  63.8 0.0 copy-start
  63.8 0.9 %copy-done = f32[400,512]{1,0:T(8,128)} copy-done((f32[400,512]{1,0:T(8,128)}, f32[400,512]{1,0:T(8,128)S(1)}, u32[]{:S(2)}) %copy-start) | copy-done | bytes 819224
  64.7 3.7 %shard_map.49 = bf16[8,32,256]{2,1,0:T(8,128)(2,1)} custom-call(f32[400,512]{1,0:T(8,128)} %copy-done, f32[256,512]{1,0:T(8,128)} %get-tuple-element.12.d_ref, bf16[2048,66]{1,0:T(8,128)(2,1)} %bitcast.19), custom_call_target="tpu_custom_call" | custom-call | flops 603979776 | bytes 1744896 | tf_op jit(solution)/shard_map/pallas_call | solution.py:146
  68.4 16.3 %all_to_all.14 = bf16[8,32,256]{2,1,0:T(8,128)(2,1)S(1)} all-to-all(bf16[8,32,256]{2,1,0:T(8,128)(2,1)} %shard_map.49), channel_id=1, replica_groups=mesh['space'=96,'group'=8] {'group'}, dimensions={0} | all-to-all | bytes 262144 | tf_op jit(solution)/shard_map/all_to_all | solution.py:205
  84.8 0.7 copy.19
  (2 shorter events, 0.0 us)
Async XLA Ops:
  28.5 15.2 %collective-permute-start = (f32[2,16,1024]{2,1,0:T(8,128)}, f32[2,16,1024]{2,1,0:T(8,128)S(1)}, u32[]{:S(2)}, u32[]{:S(2)}) collective-permute-start(f32[2,16,1024]{2,1,0:T(8,128)} %bitcast.27), channel_id=1, source_target_pairs={{0,8},{8,16},{16,24},{24,32},{32,40},{40,48},{48,56},{56,64},{64,7... | collective-permute-start | bytes 393224 | tf_op jit(solution)/shard_map/ppermute | solution.py:197
  30.4 15.2 %collective-permute-start.1 = (f32[2,16,1024]{2,1,0:T(8,128)}, f32[2,16,1024]{2,1,0:T(8,128)S(1)}, u32[]{:S(2)}, u32[]{:S(2)}) collective-permute-start(f32[2,16,1024]{2,1,0:T(8,128)} %bitcast.26), channel_id=1, source_target_pairs={{8,0},{16,8},{24,16},{32,24},{40,32},{48,40},{56,48},{64,56},{72,6... | collective-permute-start | bytes 393224 | tf_op jit(solution)/shard_map/ppermute | solution.py:198
  46.9 9.6 %collective-permute-start.2 = (f32[20,2,1024]{2,1,0:T(2,128)S(1)}, f32[20,2,1024]{2,1,0:T(2,128)S(1)}, u32[]{:S(2)}, u32[]{:S(2)}) collective-permute-start(f32[20,2,1024]{2,1,0:T(2,128)S(1)} %get-tuple-element.13), channel_id=1, source_target_pairs={{0,1},{1,2},{2,3},{3,4},{4,5},{5,6},{6,7},{8,9},{9,10},{10,11},{11... | collective-permute-start | bytes 491528 | tf_op jit(solution)/shard_map/ppermute | solution.py:28
  48.5 8.0 %collective-permute-start.3 = (f32[20,2,1024]{2,1,0:T(2,128)S(1)}, f32[20,2,1024]{2,1,0:T(2,128)S(1)}, u32[]{:S(2)}, u32[]{:S(2)}) collective-permute-start(f32[20,2,1024]{2,1,0:T(2,128)S(1)} %get-tuple-element.14), channel_id=1, source_target_pairs={{1,0},{2,1},{3,2},{4,3},{5,4},{6,5},{7,6},{9,8},{10,9},{11,10},{12... | collective-permute-start | bytes 491528 | tf_op jit(solution)/shard_map/ppermute | solution.py:29
  49.8 6.7 %copy-start.1 = (f32[256,1024]{1,0:T(8,128)S(1)}, f32[256,1024]{1,0:T(8,128)}, u32[]{:S(2)}) copy-start(f32[256,1024]{1,0:T(8,128)} %get-tuple-element.10) | copy-start | bytes 3145732
  63.8 0.9 %copy-start = (f32[400,512]{1,0:T(8,128)}, f32[400,512]{1,0:T(8,128)S(1)}, u32[]{:S(2)}) copy-start(f32[400,512]{1,0:T(8,128)S(1)} %shard_map.48.g_ref) | copy-start | bytes 2457604

commit v11 on v10

--- a/solution.py
+++ b/solution.py
@@ -16,6 +16,7 @@
 EX = XD + 4
 EY = YD + 4
 ER = EX * EY
+W0, W1 = 16, 384
 
 
 def extended(shard, sides, width):
@@ -94,16 +95,16 @@
             part = jnp.dot(mean, w_ref[a * 3 + b], preferred_element_type=jnp.float32)
             acc = acc + pltpu.roll(part, (-off) % ER, 0)
     sig = 1.0 / (1.0 + jnp.exp(-acc))
-    gout = (g_ref[...] * sig * (1.0 + acc * (1.0 - sig))).astype(jnp.bfloat16)
-    acc = jnp.zeros((ER, ZC), jnp.float32)
+    gout = (g_ref[...] * sig * (1.0 + acc * (1.0 - sig))).astype(jnp.bfloat16)[W0:W1]
+    acc = jnp.zeros((W1 - W0, ZC), jnp.float32)
     for a in range(3):
         for b in range(3):
             off = (a - 1) * EY + (b - 1)
             part = lax.dot_general(
                 gout, w_ref[8 - (a * 3 + b)], (((1,), (1,)), ((), ())), preferred_element_type=jnp.float32
             )
-            acc = acc + pltpu.roll(part, (-off) % ER, 0)
-    o_ref[...] = acc
+            acc = acc + pltpu.roll(part, (-off) % (W1 - W0), 0)
+    o_ref[pl.ds(W0, W1 - W0), :] = acc
 
 
 def conv_pair(mean_ext, gy_ext, banded):

time: 86.4 us -> 86.2 us (level)
  no operation moved by 1% of the time
where the time goes in v11:
time: 86.2 us; the launch traced here: 85.3 us
  blocking collectives  35.8 us (42%)
  Pallas kernels  22.1 us (26%)
  starting transfers between devices  17.2 us (20%)
  local copies, waits for them, and re-layouts  4.81 us (6%)
  waiting for transfers between devices  2.82 us (3%)
  other arithmetic  2.38 us (3%)
    all_to_all x1, blocking collectives, per_device(): lax.all_to_all(payload, 'group', split_axis=0, concat_axis=0, tiled=True)  19.5 us
    all_to_all x1, blocking collectives, per_device(): lax.all_to_all(grads, 'group', split_axis=0, concat_axis=0, tiled=True)  16.3 us
    ppermute x1, starting transfers between devices, per_device(): after = lax.ppermute(lo.reshape(2, YD, 2 * ZC), 'space', down)  12.4 us
    pallas_call x1, Pallas kernels, banded_weights(): pl.pallas_call(band_kernel, out_shape=jax.ShapeDtypeStruct((9, ZC, ZC), k...  6.64 us
    pallas_call x1, Pallas kernels, conv_pair(): pl.pallas_call(conv_kernel, out_shape=jax.ShapeDtypeStruct((ER, ZC), jnp....  6.5 us
    pallas_call x1, Pallas kernels, scatter_sums(): pl.pallas_call(scatter_kernel, out_shape=(jax.ShapeDtypeStruct((XY, 2 * Z...  5.24 us
    pallas_call x1, Pallas kernels, gather_rows(): pl.pallas_call(gather_kernel, out_shape=jax.ShapeDtypeStruct((parts, C, n...  3.72 us
    unnamed x6, local copies, waits for them, and re-layouts  2.75 us
  transfers between devices with their start and end apart: 4, of which 2 were waited for; matrix products, arithmetic and copies ran while one was open for 0% of the time, Pallas kernels for 8%

profile of v11, /device:TPU:6, one launch (start us, length us, event | category | flops | bytes accessed | tf_op | source)
XLA Modules:
  0.0 85.3 jit_solution(14139165302741188560)
XLA Ops:
  0.0 0.7 select_convert_fusion
  0.7 0.9 %copy.20 = bf16[4,8,8,256]{3,2,1,0:T(8,128)(2,1)S(1)} copy(bf16[4,8,8,256]{3,1,2,0:T(8,128)(2,1)} %bitcast.24) | data formatting | bytes 262144
  1.7 0.9 %copy.21 = bf16[4,8,8,256]{3,2,1,0:T(8,128)(2,1)S(1)} copy(bf16[4,8,8,256]{3,1,2,0:T(8,128)(2,1)} %bitcast.25) | data formatting | bytes 262144
  2.6 0.1 pad_maximum_fusion.1
  2.7 0.1 copy.16
  2.7 19.5 %all_to_all.13 = bf16[8,256,66]{1,2,0:T(8,128)(2,1)S(1)} all-to-all(bf16[8,256,66]{1,2,0:T(8,128)(2,1)S(1)} %copy.16), channel_id=1, replica_groups=mesh['space'=96,'group'=8] {'group'}, dimensions={0} | all-to-all | bytes 540672 | tf_op jit(solution)/shard_map/all_to_all | solution.py:192
  22.2 1.0 %copy.17 = bf16[8,256,66]{2,1,0:T(8,128)(2,1)} copy(bf16[8,256,66]{1,2,0:T(8,128)(2,1)S(1)} %all_to_all.13) | data formatting | bytes 540672 | tf_op jit(solution)/shard_map/all_to_all | solution.py:192
  23.2 5.2 %shard_map.46 = (f32[256,1024]{1,0:T(8,128)}, f32[32,1024]{1,0:T(8,128)}, f32[32,1024]{1,0:T(8,128)}, f32[256,512]{1,0:T(8,128)}) custom-call(bf16[2048,66]{1,0:T(8,128)(2,1)} %bitcast.18), custom_call_target="tpu_custom_call" | custom-call | flops 1887436800 | bytes 1843200 | tf_op jit(solution)/shard_map/pallas_call | solution.py:74
  28.5 1.9 %collective-permute-start = (f32[2,16,1024]{2,1,0:T(8,128)}, f32[2,16,1024]{2,1,0:T(8,128)S(1)}, u32[]{:S(2)}, u32[]{:S(2)}) collective-permute-start(f32[2,16,1024]{2,1,0:T(8,128)} %bitcast.27), channel_id=1, source_target_pairs={{0,8},{8,16},{16,24},{24,32},{32,40},{40,48},{48,56},{56,64},{64,7... | collective-permute-start | bytes 393224 | tf_op jit(solution)/shard_map/ppermute | solution.py:198
  30.4 12.4 %collective-permute-start.1 = (f32[2,16,1024]{2,1,0:T(8,128)}, f32[2,16,1024]{2,1,0:T(8,128)S(1)}, u32[]{:S(2)}, u32[]{:S(2)}) collective-permute-start(f32[2,16,1024]{2,1,0:T(8,128)} %bitcast.26), channel_id=1, source_target_pairs={{8,0},{16,8},{24,16},{32,24},{40,32},{48,40},{56,48},{64,56},{72,6... | collective-permute-start | bytes 393224 | tf_op jit(solution)/shard_map/ppermute | solution.py:199
  42.8 0.9 %collective-permute-done = f32[2,16,1024]{2,1,0:T(8,128)S(1)} collective-permute-done((f32[2,16,1024]{2,1,0:T(8,128)}, f32[2,16,1024]{2,1,0:T(8,128)S(1)}, u32[]{:S(2)}, u32[]{:S(2)}) %collective-permute-start) | collective-permute-done | bytes 131104 | tf_op jit(solution)/shard_map/ppermute | solution.py:198
  43.7 1.9 %collective-permute-done.1 = f32[2,16,1024]{2,1,0:T(8,128)S(1)} collective-permute-done((f32[2,16,1024]{2,1,0:T(8,128)}, f32[2,16,1024]{2,1,0:T(8,128)S(1)}, u32[]{:S(2)}, u32[]{:S(2)}) %collective-permute-start.1) | collective-permute-done | bytes 131104 | tf_op jit(solution)/shard_map/ppermute | solution.py:199
  45.6 1.3 %pad_maximum_fusion.4 = (f32[20,2,1024]{2,1,0:T(2,128)S(1)}, f32[20,2,1024]{2,1,0:T(2,128)S(1)}) fusion(f32[2,16,1024]{2,1,0:T(8,128)S(1)} %collective-permute-done.1, f32[16,16,1024]{2,1,0:T(8,128)} %bitcast.16, f32[2,16,1024]{2,1,0:T(8,128)S(1)} %collective-permute-done), kind=kLoop, calls=%fused_computation.5 | loop fusion | flops 163840 | bytes 1638400 | tf_op jit(solution)/shard_map/slice | solution.py:27
  46.9 1.6 %collective-permute-start.2 = (f32[20,2,1024]{2,1,0:T(2,128)S(1)}, f32[20,2,1024]{2,1,0:T(2,128)S(1)}, u32[]{:S(2)}, u32[]{:S(2)}) collective-permute-start(f32[20,2,1024]{2,1,0:T(2,128)S(1)} %get-tuple-element.13), channel_id=1, source_target_pairs={{0,1},{1,2},{2,3},{3,4},{4,5},{5,6},{6,7},{8,9},{9,10},{10,11},{11... | collective-permute-start | bytes 491528 | tf_op jit(solution)/shard_map/ppermute | solution.py:29
  48.5 1.3 %collective-permute-start.3 = (f32[20,2,1024]{2,1,0:T(2,128)S(1)}, f32[20,2,1024]{2,1,0:T(2,128)S(1)}, u32[]{:S(2)}, u32[]{:S(2)}) collective-permute-start(f32[20,2,1024]{2,1,0:T(2,128)S(1)} %get-tuple-element.14), channel_id=1, source_target_pairs={{1,0},{2,1},{3,2},{4,3},{5,4},{6,5},{7,6},{9,8},{10,9},{11,10},{12... | collective-permute-start | bytes 491528 | tf_op jit(solution)/shard_map/ppermute | solution.py:30
  49.8 0.0 copy-start.1
  49.8 6.6 %shard_map.47.w_ref = bf16[9,512,512]{2,1,0:T(8,128)(2,1)} custom-call(bf16[27,32,32]{2,1,0:T(8,128)(2,1)} %bitcast.23), custom_call_target="tpu_custom_call" | custom-call | flops 905969664 | bytes 4718592 | tf_op jit(solution)/shard_map/pallas_call | solution.py:174
  56.5 0.0 collective-permute-done.2
  56.5 0.0 collective-permute-done.3
  56.5 0.0 copy-done.1
  56.5 0.3 pad_maximum_fusion
  56.8 0.1 slice.20
  56.9 0.1 slice.18
  57.0 0.1 reshape.33.g_ref
  57.0 0.1 reshape.32.m_ref
  57.1 6.5 %shard_map.48.g_ref = f32[400,512]{1,0:T(8,128)S(1)} custom-call(bf16[400,512]{1,0:T(8,128)(2,1)S(1)} %reshape.32.m_ref, f32[400,512]{1,0:T(8,128)S(1)} %reshape.33.g_ref, bf16[9,512,512]{2,1,0:T(8,128)(2,1)} %shard_map.47.w_ref), custom_call_target="tpu_custom_call" | custom-call | flops 3774873600 | bytes 6766592 | tf_op jit(solution)/shard_map/pallas_call | solution.py:111
  63.6 0.0 copy-start
  63.7 0.9 %copy-done = f32[400,512]{1,0:T(8,128)} copy-done((f32[400,512]{1,0:T(8,128)}, f32[400,512]{1,0:T(8,128)S(1)}, u32[]{:S(2)}) %copy-start) | copy-done | bytes 819224
  64.5 3.7 %shard_map.49 = bf16[8,32,256]{2,1,0:T(8,128)(2,1)} custom-call(f32[400,512]{1,0:T(8,128)} %copy-done, f32[256,512]{1,0:T(8,128)} %get-tuple-element.12.d_ref, bf16[2048,66]{1,0:T(8,128)(2,1)} %bitcast.19), custom_call_target="tpu_custom_call" | custom-call | flops 603979776 | bytes 1744896 | tf_op jit(solution)/shard_map/pallas_call | solution.py:147
  68.3 16.3 %all_to_all.14 = bf16[8,32,256]{2,1,0:T(8,128)(2,1)S(1)} all-to-all(bf16[8,32,256]{2,1,0:T(8,128)(2,1)} %shard_map.49), channel_id=1, replica_groups=mesh['space'=96,'group'=8] {'group'}, dimensions={0} | all-to-all | bytes 262144 | tf_op jit(solution)/shard_map/all_to_all | solution.py:206
  84.6 0.7 copy.19
  (2 shorter events, 0.0 us)
Async XLA Ops:
  28.5 15.2 %collective-permute-start = (f32[2,16,1024]{2,1,0:T(8,128)}, f32[2,16,1024]{2,1,0:T(8,128)S(1)}, u32[]{:S(2)}, u32[]{:S(2)}) collective-permute-start(f32[2,16,1024]{2,1,0:T(8,128)} %bitcast.27), channel_id=1, source_target_pairs={{0,8},{8,16},{16,24},{24,32},{32,40},{40,48},{48,56},{56,64},{64,7... | collective-permute-start | bytes 393224 | tf_op jit(solution)/shard_map/ppermute | solution.py:198
  30.4 15.2 %collective-permute-start.1 = (f32[2,16,1024]{2,1,0:T(8,128)}, f32[2,16,1024]{2,1,0:T(8,128)S(1)}, u32[]{:S(2)}, u32[]{:S(2)}) collective-permute-start(f32[2,16,1024]{2,1,0:T(8,128)} %bitcast.26), channel_id=1, source_target_pairs={{8,0},{16,8},{24,16},{32,24},{40,32},{48,40},{56,48},{64,56},{72,6... | collective-permute-start | bytes 393224 | tf_op jit(solution)/shard_map/ppermute | solution.py:199
  46.9 9.6 %collective-permute-start.2 = (f32[20,2,1024]{2,1,0:T(2,128)S(1)}, f32[20,2,1024]{2,1,0:T(2,128)S(1)}, u32[]{:S(2)}, u32[]{:S(2)}) collective-permute-start(f32[20,2,1024]{2,1,0:T(2,128)S(1)} %get-tuple-element.13), channel_id=1, source_target_pairs={{0,1},{1,2},{2,3},{3,4},{4,5},{5,6},{6,7},{8,9},{9,10},{10,11},{11... | collective-permute-start | bytes 491528 | tf_op jit(solution)/shard_map/ppermute | solution.py:29
  48.5 8.0 %collective-permute-start.3 = (f32[20,2,1024]{2,1,0:T(2,128)S(1)}, f32[20,2,1024]{2,1,0:T(2,128)S(1)}, u32[]{:S(2)}, u32[]{:S(2)}) collective-permute-start(f32[20,2,1024]{2,1,0:T(2,128)S(1)} %get-tuple-element.14), channel_id=1, source_target_pairs={{1,0},{2,1},{3,2},{4,3},{5,4},{6,5},{7,6},{9,8},{10,9},{11,10},{12... | collective-permute-start | bytes 491528 | tf_op jit(solution)/shard_map/ppermute | solution.py:30
  49.8 6.7 %copy-start.1 = (f32[256,1024]{1,0:T(8,128)S(1)}, f32[256,1024]{1,0:T(8,128)}, u32[]{:S(2)}) copy-start(f32[256,1024]{1,0:T(8,128)} %get-tuple-element.10) | copy-start | bytes 3145732
  63.6 0.9 %copy-start = (f32[400,512]{1,0:T(8,128)}, f32[400,512]{1,0:T(8,128)S(1)}, u32[]{:S(2)}) copy-start(f32[400,512]{1,0:T(8,128)S(1)} %shard_map.48.g_ref) | copy-start | bytes 2457604
